TPU v7x, 32 devices: a whole 2x2x4 slice. The times are simulated.
32 devices in a mesh: mem: 2 (over y), row: 16 (over z, x, core).
Axes of the slice: x: 2, y: 2, z: 4, core: 2. Of those that a mesh axis runs over, the one named last changes fastest.
Arguments:
- members: bfloat16 [32, 8, 2, 128, 512], P('mem', None, None, 'row'), may hold values from -6 to 6
- static_scale: float32 [8, 2, 128, 512], P('mem', None, 'row'), may hold values from 0.3 to 1.5
- observed: float32 [8, 2, 128, 512], P('mem', None, 'row'), may hold values from -5 to 5, as said below
- huber_class: int32 [8, 2, 128, 512], P('mem', None, 'row'), may hold values from 0 to 3
- scale_index: int32 [2, 128, 512], P(None, 'row'), may hold values from 0 to 3
Outputs:
- control: float32 [32, 2, 128, 512], P('mem', None, 'row')
- static_control: float32 [8, 2, 128, 512], P('mem', None, 'row')
- increment: float32 [8, 2, 128, 512], P('mem', None, 'row')
Inputs may be any that keep to these rules, and one draw needn't show every extreme that they name: observed departures of order one.
All inputs are finite; a program needn't handle non-finite values.
Results may differ from a plain program's by a relative error of at most 0.0035.
Values may be sent and summed in bfloat16 or wider, within the bound.
No kernel may reach another device: no remote copies, remote signals or barrier semaphores. Data moves between devices by JAX's collectives and lax.ppermute only.
A program may use at most 64 MiB of HBM per device.

v0:
```python
import math

import jax
import jax.numpy as jnp
from jax import lax
from jax.sharding import PartitionSpec as P

SWEEPS = 4
ITERS = 2


kappa_table = (0.06, 0.11, 0.17, 0.23)
huber_levels = (1.0, 0.5, 1.0, 2.0)


def with_halo(block, sides, width):
    for axis, dim in sides:
        count = lax.axis_size(axis)
        forward = [(i, i + 1) for i in range(count - 1)]
        backward = [(target, source) for source, target in forward]
        low = lax.ppermute(
            lax.slice_in_dim(block, block.shape[dim] - width, None, axis=dim), axis, forward
        )
        high = lax.ppermute(lax.slice_in_dim(block, 0, width, axis=dim), axis, backward)
        block = jnp.concatenate([low, block, high], axis=dim)
    return block


def kappa_field(scale_index):
    result = jnp.zeros(scale_index.shape, jnp.float32)
    for level_id in range(4):
        result = result + jnp.where(scale_index == level_id, kappa_table[level_id], 0.0).astype(
            jnp.float32
        )
    return result


def threshold_field(huber_class):
    result = jnp.zeros(huber_class.shape, jnp.float32)
    for level_id in range(4):
        result = result + jnp.where(huber_class == level_id, huber_levels[level_id], 0.0).astype(
            jnp.float32
        )
    return result


def laplace(padded):
    full = jnp.pad(padded, [(0, 0)] * (padded.ndim - 1) + [(1, 1)])
    centre = full[..., 1:-1, 1:-1]
    vertical = full[..., 2:, 1:-1] + full[..., :-2, 1:-1]
    sideways = full[..., 1:-1, 2:] + full[..., 1:-1, :-2]
    return vertical + sideways - 4.0 * centre


def pad_rows(field):
    return jnp.pad(field, [(0, 0)] * (field.ndim - 2) + [(1, 1), (0, 0)])


def deep_halo(field):
    return with_halo(field, (("row", 2),), SWEEPS)


def local(members, static_scale, observed, huber_class, scale_index):
    local_members = members.shape[0]
    rows = members.shape[3]
    ensemble_total = local_members * lax.axis_size("mem")
    ens_coef = math.sqrt(0.7 / (ensemble_total - 1))
    stat_coef = math.sqrt(0.3)
    kappa = kappa_field(scale_index)
    threshold = threshold_field(huber_class)
    observed_mask = (huber_class > 0).astype(jnp.float32)
    wide_kappa = with_halo(kappa, (("row", 1),), SWEEPS)
    global_row = lax.axis_index("row") * rows - SWEEPS + jnp.arange(rows + 2 * SWEEPS)
    inside = ((global_row >= 0) & (global_row < rows * lax.axis_size("row"))).astype(jnp.float32)[
        :, None
    ]

    def forward(field):
        extended = deep_halo(field)
        for sweep in range(SWEEPS):
            extended = (extended + wide_kappa * laplace(pad_rows(extended))) * inside
        return extended[:, :, SWEEPS : SWEEPS + rows]

    control = jnp.zeros((local_members,) + scale_index.shape, jnp.float32)
    static_control = jnp.zeros(static_scale.shape, jnp.float32)
    increment = jnp.zeros(static_scale.shape, jnp.float32)
    for turn in range(ITERS):
        misfit = increment - observed
        clipped = observed_mask * jnp.clip(misfit, -threshold, threshold)
        weight = observed_mask * threshold / jnp.maximum(jnp.abs(misfit), threshold)
        sent = clipped.astype(jnp.bfloat16)
        back = jnp.sum(
            members.astype(jnp.float32)
            * lax.all_gather(sent, "mem", axis=0, tiled=True).astype(jnp.float32)[None],
            axis=1,
        )
        static_back = stat_coef * static_scale * sent.astype(jnp.float32)
        adjoint_extended = deep_halo(jnp.concatenate([ens_coef * back, static_back], axis=0))
        for adjoint_sweep in range(SWEEPS):
            adjoint_extended = (
                adjoint_extended + laplace(pad_rows(wide_kappa * adjoint_extended))
            ) * inside
        swept = adjoint_extended[:, :, SWEEPS : SWEEPS + rows]
        grad_ens = control + swept[:local_members]
        grad_stat = static_control + swept[local_members:]
        local_norm = jnp.sum(grad_ens * grad_ens) + jnp.sum(grad_stat * grad_stat)
        norm = lax.psum(local_norm, ("mem", "row"))
        smoothed = forward(jnp.concatenate([grad_ens, grad_stat], axis=0))
        spread = smoothed[:local_members].astype(jnp.bfloat16)
        static_part = stat_coef * static_scale * smoothed[local_members:]
        image = (
            lax.psum_scatter(
                ens_coef
                * jnp.sum(
                    members.astype(jnp.float32) * spread.astype(jnp.float32)[:, None], axis=0
                ),
                "mem",
                scatter_dimension=0,
                tiled=True,
            )
            + static_part
        )
        local_curvature = jnp.sum(weight * image * image)
        curvature = lax.psum(local_curvature, ("mem", "row"))
        step = norm / (norm + curvature)
        control = control - step * grad_ens
        static_control = static_control - step * grad_stat
        increment = increment - step * image
    return (control, static_control, increment)


def solution(mesh):
    placed = (
        P("mem", None, None, "row", None),
        P("mem", None, "row", None),
        P("mem", None, "row", None),
        P("mem", None, "row", None),
        P(None, "row", None),
    )
    return jax.shard_map(
        local,
        mesh=mesh,
        in_specs=placed,
        out_specs=(
            P("mem", None, "row", None),
            P("mem", None, "row", None),
            P("mem", None, "row", None),
        ),
        check_vma=False,
    )
```

profile of v0, /device:TPU:0, one launch (start us, length us, event | category | flops | bytes accessed | tf_op | source)
XLA Modules:
  0.0 232.2 jit_solution(6273273860542850659)
XLA Ops:
  7.2 1.1 convert_multiply_fusion.5
  8.3 5.9 %all_gather.6 = bf16[8,2,8,512]{3,2,1,0:T(8,128)(2,1)S(1)} all-gather(bf16[4,2,8,512]{3,2,1,0:T(8,128)(2,1)S(1)} %get-tuple-element.28), channel_id=1, replica_groups=mesh['mem'=2,'row'=16] {'mem'}, dimensions={0}, use_global_device_ids=true | all-gather | bytes 196608 | tf_op jit(solution)/shard_map/all_gather | solution.py:94
  14.3 2.1 fusion
  16.8 1.3 collective-permute-start.1
  18.3 3.1 %collective-permute-start = (f32[20,2,4,512]{3,0,2,1:T(8,128)S(1)}, f32[20,2,4,512]{3,0,2,1:T(8,128)S(1)}, u32[]{:S(2)}, u32[]{:S(2)}) collective-permute-start(f32[20,2,4,512]{3,0,2,1:T(8,128)S(1)} %copy.8), channel_id=1, source_target_pairs={{0,1},{1,2},{2,3},{3,4},{4,5},{5,6},{6,7},{7,8},{8,9},{9,10},{10,1... | collective-permute-start | bytes 983048 | tf_op jit(solution)/shard_map/ppermute | solution.py:21
  21.4 3.5 %collective-permute-start.2 = (f32[2,4,512]{2,1,0:T(4,128)S(1)}, f32[2,4,512]{2,1,0:T(4,128)S(1)}, u32[]{:S(2)}, u32[]{:S(2)}) collective-permute-start(f32[2,4,512]{2,1,0:T(4,128)S(1)} %get-tuple-element.38), channel_id=1, source_target_pairs={{0,1},{1,2},{2,3},{3,4},{4,5},{5,6},{6,7},{7,8},{8,9},{9,10},{10,1... | collective-permute-start | bytes 49160 | tf_op jit(solution)/shard_map/ppermute | solution.py:21
  24.9 1.3 collective-permute-start.3
  26.3 1.8 collective-permute-done.3
  29.0 1.3 broadcast_multiply_fusion.5
  30.6 1.2 broadcast_multiply_fusion.4
  32.2 1.2 broadcast_multiply_fusion.3
  33.6 1.1 fusion.23
  35.1 1.3 collective-permute-start.5
  36.6 5.2 %collective-permute-start.4 = (f32[20,2,4,512]{3,0,2,1:T(8,128)S(1)}, f32[20,2,4,512]{3,0,2,1:T(8,128)S(1)}, u32[]{:S(2)}, u32[]{:S(2)}) collective-permute-start(f32[20,2,4,512]{3,0,2,1:T(8,128)S(1)} %copy.12), channel_id=1, source_target_pairs={{0,1},{1,2},{2,3},{3,4},{4,5},{5,6},{6,7},{7,8},{8,9},{9,10},{10,1... | collective-permute-start | bytes 983048 | tf_op jit(solution)/shard_map/ppermute | solution.py:21
  42.2 0.8 collective-permute-done.4
  43.7 1.2 fusion.29
  45.3 1.1 fusion.35
  46.7 1.1 fusion.41
  48.2 1.1 fusion.47
  50.4 0.7 broadcast_multiply_fusion.9
  51.8 0.7 multiply_reduce_fusion.1
  53.9 19.5 %reduce-scatter.3.cloned.1.call-done = f32[4,2,8,512]{3,2,1,0:T(8,128)} async-done(((f32[8,2,8,512]{3,2,1,0:T(8,128)}), f32[4,2,8,512]{3,2,1,0:T(8,128)}) %reduce-scatter.3.cloned.1.call-update) | async-done | bytes 131088 | tf_op jit(solution)/shard_map/reduce_scatter | solution.py:112
  73.3 2.5 %fusion.99 = (f32[]{:T(128)}, f32[4,2,8,512]{3,2,1,0:T(8,128)}) fusion(f32[4,2,8,512]{3,2,1,0:T(8,128)} %param.7, pred[4,2,8,512]{3,2,1,0:T(8,128)(4,1)S(1)} %get-tuple-element.29, s32[4,2,8,512]{3,2,1,0:T(8,128)} %param.8, f32[4,2,8,512]{3,2,1,0:T(8,128)} %reduce-scatter.3.cloned.1.call-done, f32[20,2,16,512]{3,2,1,0:T(8,128)} %copy-done.7, ...), kind=kLoop, calls=%fused_computation.165 | loop fusion | flops 720895 | bytes 819204 | tf_op jit(solution)/shard_map/reduce_sum | solution.py:123
  75.9 39.5 %all-reduce.33 = (f32[]{:T(128)}, f32[]{:T(128)}) all-reduce(f32[]{:T(128)S(6)} %add.345, f32[]{:T(128)} %get-tuple-element.19), channel_id=1, replica_groups=mesh['mem'=2,'row'=16] {'mem','row'}, use_global_device_ids=true, to_apply=%region_3.4 | all-reduce | flops 2 | bytes 16 | tf_op jit(solution)/shard_map/psum | solution.py:107
  117.3 1.2 convert_multiply_fusion.4
  118.5 5.4 %all_gather.7 = bf16[8,2,8,512]{3,2,1,0:T(8,128)(2,1)S(1)} all-gather(bf16[4,2,8,512]{3,2,1,0:T(8,128)(2,1)S(1)} %get-tuple-element.18), channel_id=1, replica_groups=mesh['mem'=2,'row'=16] {'mem'}, dimensions={0}, use_global_device_ids=true | all-gather | bytes 196608 | tf_op jit(solution)/shard_map/all_gather | solution.py:94
  124.8 1.3 collective-permute-start.7
  126.3 3.3 %collective-permute-start.6 = (f32[20,2,4,512]{3,0,2,1:T(8,128)S(1)}, f32[20,2,4,512]{3,0,2,1:T(8,128)S(1)}, u32[]{:S(2)}, u32[]{:S(2)}) collective-permute-start(f32[20,2,4,512]{3,0,2,1:T(8,128)S(1)} %copy.16), channel_id=1, source_target_pairs={{0,1},{1,2},{2,3},{3,4},{4,5},{5,6},{6,7},{7,8},{8,9},{9,10},{10,1... | collective-permute-start | bytes 983048 | tf_op jit(solution)/shard_map/ppermute | solution.py:21
  129.8 0.9 collective-permute-done.6
  131.5 1.3 broadcast_multiply_fusion.2
  133.0 1.2 broadcast_multiply_fusion.1
  134.5 1.2 broadcast_multiply_fusion
  135.9 1.1 fusion.67
  137.0 0.7 multiply_reduce_fusion.2
  137.7 0.9 multiply_reduce_fusion
  139.0 1.3 collective-permute-start.9
  140.5 9.4 %collective-permute-start.8 = (f32[20,2,4,512]{3,0,2,1:T(8,128)S(1)}, f32[20,2,4,512]{3,0,2,1:T(8,128)S(1)}, u32[]{:S(2)}, u32[]{:S(2)}) collective-permute-start(f32[20,2,4,512]{3,0,2,1:T(8,128)S(1)} %copy.20), channel_id=1, source_target_pairs={{0,1},{1,2},{2,3},{3,4},{4,5},{5,6},{6,7},{7,8},{8,9},{9,10},{10,1... | collective-permute-start | bytes 983048 | tf_op jit(solution)/shard_map/ppermute | solution.py:21
  150.1 0.8 collective-permute-done.8
  151.7 1.2 fusion.73
  153.3 1.1 fusion.79
  154.7 1.1 fusion.85
  156.2 1.1 fusion.91
  158.4 0.7 broadcast_multiply_fusion.8
  160.5 18.9 %reduce-scatter.5.cloned.1.call-done = f32[4,2,8,512]{3,2,1,0:T(8,128)} async-done(((f32[8,2,8,512]{3,2,1,0:T(8,128)}), f32[4,2,8,512]{3,2,1,0:T(8,128)}) %reduce-scatter.5.cloned.1.call-update) | async-done | bytes 131088 | tf_op jit(solution)/shard_map/reduce_scatter | solution.py:112
  179.4 2.0 fusion.100
  181.4 39.4 %all-reduce.32 = (f32[]{:T(128)}, f32[]{:T(128)}) all-reduce(f32[]{:T(128)S(6)} %add.382, f32[]{:T(128)} %fusion.100), channel_id=1, replica_groups=mesh['mem'=2,'row'=16] {'mem','row'}, use_global_device_ids=true, to_apply=%region_11.12 | all-reduce | flops 2 | bytes 16 | tf_op jit(solution)/shard_map/psum | solution.py:107
  222.6 1.0 multiply_subtract_fusion
  223.6 1.8 multiply_subtract_fusion.2
  (87 shorter events, 13.5 us)
Async XLA Ops:
  7.2 66.2 %reduce-scatter.3.cloned.1.call-start = ((), (), s32[]{:S(2)}) async-start(), calls=%async_computation.2 | async-start | bytes 393216 | tf_op jit(solution)/shard_map/reduce_scatter | solution.py:112
  16.4 4.9 %copy-start.10 = (s32[2,8,512]{2,1,0:T(8,128)S(1)}, s32[2,8,512]{2,1,0:T(8,128)}, u32[]{:S(2)}) copy-start(s32[2,8,512]{2,1,0:T(8,128)} %param.9) | copy-start | bytes 98308
  16.8 11.2 %collective-permute-start.1 = (f32[20,2,4,512]{3,0,2,1:T(8,128)S(1)}, f32[20,2,4,512]{3,0,2,1:T(8,128)S(1)}, u32[]{:S(2)}, u32[]{:S(2)}) collective-permute-start(f32[20,2,4,512]{3,0,2,1:T(8,128)S(1)} %copy.9), channel_id=1, source_target_pairs={{1,0},{2,1},{3,2},{4,3},{5,4},{6,5},{7,6},{8,7},{9,8},{10,9},{11,1... | collective-permute-start | bytes 983048 | tf_op jit(solution)/shard_map/ppermute | solution.py:24
  18.3 10.0 %collective-permute-start = (f32[20,2,4,512]{3,0,2,1:T(8,128)S(1)}, f32[20,2,4,512]{3,0,2,1:T(8,128)S(1)}, u32[]{:S(2)}, u32[]{:S(2)}) collective-permute-start(f32[20,2,4,512]{3,0,2,1:T(8,128)S(1)} %copy.8), channel_id=1, source_target_pairs={{0,1},{1,2},{2,3},{3,4},{4,5},{5,6},{6,7},{7,8},{8,9},{9,10},{10,1... | collective-permute-start | bytes 983048 | tf_op jit(solution)/shard_map/ppermute | solution.py:21
  21.4 4.8 %collective-permute-start.2 = (f32[2,4,512]{2,1,0:T(4,128)S(1)}, f32[2,4,512]{2,1,0:T(4,128)S(1)}, u32[]{:S(2)}, u32[]{:S(2)}) collective-permute-start(f32[2,4,512]{2,1,0:T(4,128)S(1)} %get-tuple-element.38), channel_id=1, source_target_pairs={{0,1},{1,2},{2,3},{3,4},{4,5},{5,6},{6,7},{7,8},{8,9},{9,10},{10,1... | collective-permute-start | bytes 49160 | tf_op jit(solution)/shard_map/ppermute | solution.py:21
  24.9 3.1 %collective-permute-start.3 = (f32[2,4,512]{2,1,0:T(4,128)S(1)}, f32[2,4,512]{2,1,0:T(4,128)S(1)}, u32[]{:S(2)}, u32[]{:S(2)}) collective-permute-start(f32[2,4,512]{2,1,0:T(4,128)S(1)} %get-tuple-element.39), channel_id=1, source_target_pairs={{1,0},{2,1},{3,2},{4,3},{5,4},{6,5},{7,6},{8,7},{9,8},{10,9},{11,1... | collective-permute-start | bytes 49160 | tf_op jit(solution)/shard_map/ppermute | solution.py:24
  35.1 6.9 %collective-permute-start.5 = (f32[20,2,4,512]{3,0,2,1:T(8,128)S(1)}, f32[20,2,4,512]{3,0,2,1:T(8,128)S(1)}, u32[]{:S(2)}, u32[]{:S(2)}) collective-permute-start(f32[20,2,4,512]{3,0,2,1:T(8,128)S(1)} %copy.13), channel_id=1, source_target_pairs={{1,0},{2,1},{3,2},{4,3},{5,4},{6,5},{7,6},{8,7},{9,8},{10,9},{11,1... | collective-permute-start | bytes 983048 | tf_op jit(solution)/shard_map/ppermute | solution.py:24
  36.6 6.3 %collective-permute-start.4 = (f32[20,2,4,512]{3,0,2,1:T(8,128)S(1)}, f32[20,2,4,512]{3,0,2,1:T(8,128)S(1)}, u32[]{:S(2)}, u32[]{:S(2)}) collective-permute-start(f32[20,2,4,512]{3,0,2,1:T(8,128)S(1)} %copy.12), channel_id=1, source_target_pairs={{0,1},{1,2},{2,3},{3,4},{4,5},{5,6},{6,7},{7,8},{8,9},{9,10},{10,1... | collective-permute-start | bytes 983048 | tf_op jit(solution)/shard_map/ppermute | solution.py:21
  48.2 1.6 copy-start
  49.3 1.1 copy-start.7
  51.2 128.3 %reduce-scatter.5.cloned.1.call-start = ((), (), s32[]{:S(2)}) async-start(), calls=%async_computation.3 | async-start | bytes 393216 | tf_op jit(solution)/shard_map/reduce_scatter | solution.py:112
  124.8 4.8 %collective-permute-start.7 = (f32[20,2,4,512]{3,0,2,1:T(8,128)S(1)}, f32[20,2,4,512]{3,0,2,1:T(8,128)S(1)}, u32[]{:S(2)}, u32[]{:S(2)}) collective-permute-start(f32[20,2,4,512]{3,0,2,1:T(8,128)S(1)} %copy.17), channel_id=1, source_target_pairs={{1,0},{2,1},{3,2},{4,3},{5,4},{6,5},{7,6},{8,7},{9,8},{10,9},{11,1... | collective-permute-start | bytes 983048 | tf_op jit(solution)/shard_map/ppermute | solution.py:24
  126.3 4.4 %collective-permute-start.6 = (f32[20,2,4,512]{3,0,2,1:T(8,128)S(1)}, f32[20,2,4,512]{3,0,2,1:T(8,128)S(1)}, u32[]{:S(2)}, u32[]{:S(2)}) collective-permute-start(f32[20,2,4,512]{3,0,2,1:T(8,128)S(1)} %copy.16), channel_id=1, source_target_pairs={{0,1},{1,2},{2,3},{3,4},{4,5},{5,6},{6,7},{7,8},{8,9},{9,10},{10,1... | collective-permute-start | bytes 983048 | tf_op jit(solution)/shard_map/ppermute | solution.py:21
  137.7 14.0 %copy-start.3 = (f32[4,2,8,512]{3,2,1,0:T(8,128)}, f32[4,2,8,512]{3,2,1,0:T(8,128)S(1)}, u32[]{:S(2)}) copy-start(f32[4,2,8,512]{3,2,1,0:T(8,128)S(1)} %get-tuple-element.8) | copy-start | bytes 393220
  138.6 13.1 %copy-start.1 = (f32[16,2,8,512]{3,2,1,0:T(8,128)}, f32[16,2,8,512]{3,2,1,0:T(8,128)S(1)}, u32[]{:S(2)}) copy-start(f32[16,2,8,512]{3,2,1,0:T(8,128)S(1)} %get-tuple-element.10) | copy-start | bytes 1572868
  139.0 10.9 %collective-permute-start.9 = (f32[20,2,4,512]{3,0,2,1:T(8,128)S(1)}, f32[20,2,4,512]{3,0,2,1:T(8,128)S(1)}, u32[]{:S(2)}, u32[]{:S(2)}) collective-permute-start(f32[20,2,4,512]{3,0,2,1:T(8,128)S(1)} %copy.21), channel_id=1, source_target_pairs={{1,0},{2,1},{3,2},{4,3},{5,4},{6,5},{7,6},{8,7},{9,8},{10,9},{11,1... | collective-permute-start | bytes 983048 | tf_op jit(solution)/shard_map/ppermute | solution.py:24
  140.5 10.4 %collective-permute-start.8 = (f32[20,2,4,512]{3,0,2,1:T(8,128)S(1)}, f32[20,2,4,512]{3,0,2,1:T(8,128)S(1)}, u32[]{:S(2)}, u32[]{:S(2)}) collective-permute-start(f32[20,2,4,512]{3,0,2,1:T(8,128)S(1)} %copy.20), channel_id=1, source_target_pairs={{0,1},{1,2},{2,3},{3,4},{4,5},{5,6},{6,7},{7,8},{8,9},{9,10},{10,1... | collective-permute-start | bytes 983048 | tf_op jit(solution)/shard_map/ppermute | solution.py:21
  157.3 1.1 copy-start.6
  158.4 64.2 %copy-start.2 = (f32[16,2,8,512]{3,2,1,0:T(8,128)S(1)}, f32[16,2,8,512]{3,2,1,0:T(8,128)}, u32[]{:S(2)}) copy-start(f32[16,2,8,512]{3,2,1,0:T(8,128)} %copy-done.1) | copy-start | bytes 1572868
  159.1 64.5 %copy-start.4 = (f32[4,2,8,512]{3,2,1,0:T(8,128)S(1)}, f32[4,2,8,512]{3,2,1,0:T(8,128)}, u32[]{:S(2)}) copy-start(f32[4,2,8,512]{3,2,1,0:T(8,128)} %copy-done.3) | copy-start | bytes 393220
  159.1 64.5 %copy-start.5 = (f32[4,2,8,512]{3,2,1,0:T(8,128)S(1)}, f32[4,2,8,512]{3,2,1,0:T(8,128)}, u32[]{:S(2)}) copy-start(f32[4,2,8,512]{3,2,1,0:T(8,128)} %param.6) | copy-start | bytes 393220
  159.1 64.5 %copy-start.8 = (f32[4,2,8,512]{3,2,1,0:T(8,128)S(1)}, f32[4,2,8,512]{3,2,1,0:T(8,128)}, u32[]{:S(2)}) copy-start(f32[4,2,8,512]{3,2,1,0:T(8,128)} %get-tuple-element.20) | copy-start | bytes 393220
  179.4 44.2 %copy-start.9 = (f32[4,2,8,512]{3,2,1,0:T(8,128)S(1)}, f32[4,2,8,512]{3,2,1,0:T(8,128)}, u32[]{:S(2)}) copy-start(f32[4,2,8,512]{3,2,1,0:T(8,128)} %reduce-scatter.5.cloned.1.call-done) | copy-start | bytes 393220
Sparse Core Ops, SparseCore 0:
  51.3 22.0 reduce-scatter.2
  159.3 20.1 reduce-scatter.4
where the time goes:
time: 233 us; the launch traced here: 232 us
  blocking collectives  90.1 us (39%)
  waiting for transfers between devices  42.6 us (18%)
  other arithmetic  37.7 us (16%)
  starting transfers between devices  31 us (13%)
  between operations  21.1 us (9%)
  local copies, waits for them, and re-layouts  9.57 us (4%)
    psum x2, blocking collectives, local(): norm = lax.psum(local_norm, ('mem', 'row'))  78.9 us
    reduce_scatter x2, waiting for transfers between devices, local(): lax.psum_scatter(ens_coef * jnp.sum(members.astype(jnp.float32) * spread....  38.4 us
    ppermute x5, starting transfers between devices, with_halo(): lax.ppermute(lax.slice_in_dim(block, block.shape[dim] - width, None, axis...  24.4 us
    all_gather x2, blocking collectives, local(): lax.all_gather(sent, 'mem', axis=0, tiled=True).astype(jnp.float32)[None]  11.3 us
    mul x8, other arithmetic, forward(): extended = (extended + wide_kappa * laplace(pad_rows(extended))) * inside  9.04 us
    mul x8, other arithmetic, local(): wide_kappa * adjoint_extended  7.76 us
    ppermute x5, starting transfers between devices, with_halo(): lax.ppermute(lax.slice_in_dim(block, 0, width, axis=dim), axis, backward)  6.46 us
    pad x16, local copies, waits for them, and re-layouts, pad_rows(): return jnp.pad(field, [(0, 0)] * (field.ndim - 2) + [(1, 1), (0, 0)])  4.95 us
  transfers between devices with their start and end apart: 12, of which 6 were waited for; matrix products, arithmetic and copies ran while one was open for 1% of the time, Pallas kernels for 0%

commit v1 on v0

v1 whole, which is shorter than its diff:
```python
import functools
import math

import jax
import jax.numpy as jnp
from jax import lax
from jax.experimental import pallas as pl
from jax.experimental.pallas import tpu as pltpu
from jax.sharding import PartitionSpec as P

SWEEPS = 4
ITERS = 2
SUB = 8
LANES = 128
kappa_table = (0.06, 0.11, 0.17, 0.23)
huber_levels = (1.0, 0.5, 1.0, 2.0)
f32 = jnp.float32
bf16 = jnp.bfloat16


def table(index, values):
    result = jnp.full(index.shape, values[3], f32)
    for entry in range(3):
        result = jnp.where(index == entry, f32(values[entry]), result)
    return result


class Plan:
    def __init__(self, members, static_scale, mem, row):
        self.K, self.V, self.L, self.R, self.X = members.shape
        self.S = static_scale.shape[0]
        self.mem, self.row = mem, row
        self.devices = mem * row
        self.KT = -(-self.K // SUB)
        self.ST = -(-(self.S * self.L) // SUB)
        self.PM = self.L * self.KT
        self.PN = self.PM + self.ST
        self.F = self.K + self.S
        self.C = self.X // LANES
        self.RE = self.R + 4 * SWEEPS
        self.RG = self.R + 2 * SWEEPS
        self.pads = self.K % SUB != 0 or (self.S * self.L) % SUB != 0
        self.ens = math.sqrt(0.7 / (self.K * mem - 1))
        self.stat = math.sqrt(0.3)

    def slot(self, field, level):
        if field < self.K:
            return level * self.KT + field // SUB, field % SUB
        at = (field - self.K) * self.L + level
        return self.PM + at // SUB, at % SUB


def strided(start, count):
    return pl.ds(start, count, stride=SUB)


def scatter(ref, tile, where, value):
    for c in range(value.shape[1] // LANES):
        ref[tile, c, where, :] = value[:, c * LANES : (c + 1) * LANES]


def gather(ref, tile, where):
    return jnp.concatenate([ref[tile, c, where, :] for c in range(ref.shape[1])], axis=1)


def back_kernel(p, first, *refs):
    if first:
        members, static_scale, scale_index, obs, cls, obs_in, cls_in, back, msg, sent = refs
    else:
        members, static_scale, obs, cls, obs_in, cls_in, image, got, back, msg, step_out, sent = refs
    me = lax.axis_index("mem")
    if p.pads:
        back[...] = jnp.zeros(back.shape, f32)
    if not first:
        total = jnp.sum(got[...], axis=0, keepdims=True)
        norm = jnp.sum(total[:, :LANES], axis=1, keepdims=True)
        curvature = jnp.sum(total[:, LANES:], axis=1, keepdims=True)
        step = norm / (norm + curvature)
        step_out[...] = jnp.broadcast_to(step, step_out.shape)
    for shift in range(p.mem):
        base = lax.rem(me + (p.mem - shift), p.mem) * p.S
        for s in range(p.S):
            for l in range(p.L):
                if shift == 0:
                    seen, index = obs[s, l], cls[s, l]
                else:
                    seen, index = obs_in[shift - 1, s, l], cls_in[shift - 1, s, l]
                threshold = table(index, huber_levels)
                if first:
                    misfit = -seen
                else:
                    misfit = -(step * image[base + s, l]) - seen
                clipped = jnp.where(index > 0, jnp.clip(misfit, -threshold, threshold), 0.0)
                rounded = clipped.astype(bf16).astype(f32)
                sent[base + s, l] = rounded
                if shift == 0:
                    tile, lane = p.slot(p.K + s, l)
                    value = p.stat * static_scale[s, l] * rounded
                    scatter(back, tile, strided(lane, p.R), value)
                    msg[p.K + s, l] = value.astype(bf16)
    if first:
        for l in range(p.L):
            msg[p.F, l] = scale_index[l].astype(f32).astype(bf16)
    for l in range(p.L):
        for k in range(p.K):
            value = members[k, 0, l].astype(f32) * sent[0, l]
            for v in range(1, p.V):
                value = value + members[k, v, l].astype(f32) * sent[v, l]
            value = p.ens * value
            tile, lane = p.slot(k, l)
            scatter(back, tile, strided(lane, p.R), value)
            msg[k, l] = value.astype(bf16)


def sideways(u, first_lane, last_lane):
    right = [pltpu.roll(part, 1, 1) for part in u]
    left = [pltpu.roll(part, LANES - 1, 1) for part in u]
    zero = jnp.zeros_like(u[0])
    before, after = [zero] + right[:-1], left[1:] + [zero]
    return [
        jnp.where(first_lane, before[i], right[i]) + jnp.where(last_lane, after[i], left[i])
        for i in range(len(u))
    ]


def stencil(above, here, below, side):
    across = side(here)
    return [(above[c] + below[c]) + across[c] - 4.0 * here[c] for c in range(len(here))]


def sweep_kernel(p, first, *refs):
    if first:
        members, static_scale, scale_index, back, low, high, grad, kap, norm, part, lo, hi, a, b, out = refs
    else:
        members, static_scale, kap, before, step, back, low, high, grad, norm, part, lo, hi, a, b, out = refs
    me, at = lax.axis_index("mem"), lax.axis_index("row")
    low_ok = jnp.where(at > 0, 1.0, 0.0).astype(f32)
    high_ok = jnp.where(at < p.row - 1, 1.0, 0.0).astype(f32)
    R, RE, RG, W = p.R, p.RE, p.RG, SWEEPS
    H = 2 * W
    for ref, dst in ((low, lo), (high, hi)):
        if p.pads:
            dst[...] = jnp.zeros(dst.shape, f32)
        skip = R - H if ref is low else 0
        for field in range(p.F):
            for l in range(p.L):
                tile, lane = p.slot(field, l)
                scatter(dst, tile, strided(lane, H), ref[field, l].astype(f32)[skip : skip + H])
    if first:
        for l in range(p.L):
            pieces = (
                (table(low[p.F, l].astype(f32)[R - H :], kappa_table) * low_ok, 0),
                (table(scale_index[l].astype(f32), kappa_table), H),
                (table(high[p.F, l].astype(f32)[:H], kappa_table) * high_ok, H + R),
            )
            for value, offset in pieces:
                for r in range(value.shape[0]):
                    scatter(kap, l, pl.ds((offset + r) * SUB, SUB), jnp.broadcast_to(value[r : r + 1], (SUB, p.X)))
                for j in range(p.ST * SUB):
                    if (j % p.L) == l:
                        scatter(kap, p.L + j // SUB, strided(offset * SUB + j % SUB, value.shape[0]), value)
    lane = lax.broadcasted_iota(jnp.int32, (SUB, LANES), 1)
    first_lane, last_lane = lane == 0, lane == LANES - 1
    side = functools.partial(sideways, first_lane=first_lane, last_lane=last_lane)
    cols = range(p.C)

    def tiles(ref, r, *lead):
        return [ref[(*lead, c, pl.ds(r * SUB, SUB), slice(None))] for c in cols]

    def keep(value, ref, r, *lead):
        for c in cols:
            ref[(*lead, c, pl.ds(r * SUB, SUB), slice(None))] = value[c]

    if not first:
        step_tile = jnp.broadcast_to(step[0:1, 0:1], (SUB, LANES))

    def problem(t, total):
        which = jnp.where(t < p.PM, t // p.KT, t - p.PM + p.L)
        source = None
        for sweep in range(W):
            target = (a, b)[sweep % 2]
            held = []
            for r in range(sweep, RE - sweep):
                if sweep:
                    u = tiles(source, r)
                elif r < H:
                    u = tiles(lo, r, t)
                elif r < H + R:
                    u = tiles(back, r - H, t)
                else:
                    u = tiles(hi, r - H - R, t)
                factor = tiles(kap, r, which)
                w = [factor[c] * u[c] for c in cols]
                held = (held + [(u, w)])[-3:]
                if len(held) < 3:
                    continue
                (_, w0), (u1, w1), (_, w2) = held
                change = stencil(w0, w1, w2, side)
                value = [u1[c] + change[c] for c in cols]
                if sweep < W - 1:
                    keep(value, target, r - 1)
                    continue
                if not first:
                    earlier = tiles(before, r - 1 - W, t)
                    value = [value[c] - step_tile * earlier[c] for c in cols]
                if r - 1 < H:
                    value = [one * low_ok for one in value]
                elif r - 1 >= H + R:
                    value = [one * high_ok for one in value]
                else:
                    for one in value:
                        total = total + one * one
                keep(value, grad, r - 1 - W, t)
            source = target
        for sweep in range(W):
            target = (a, b)[sweep % 2]
            held = []
            for r in range(W + sweep, RE - W - sweep):
                u = tiles(source, r) if sweep else tiles(grad, r - W, t)
                held = (held + [u])[-3:]
                if len(held) < 3:
                    continue
                change = stencil(*held, side)
                factor = tiles(kap, r - 1, which)
                value = [held[1][c] + factor[c] * change[c] for c in cols]
                if sweep < W - 1:
                    keep(value, target, r - 1)
                else:
                    keep(value, out, r - 1 - H, t)
            source = target
        return total

    total = lax.fori_loop(0, p.PN, problem, jnp.zeros((SUB, LANES), f32))
    norm[...] = jnp.sum(total, axis=0, keepdims=True)
    for l in range(p.L):
        sums = [None] * p.V
        for k in range(p.K):
            tile, j = p.slot(k, l)
            spread = gather(out, tile, strided(j, R)).astype(bf16).astype(f32)
            for v in range(p.V):
                term = members[k, v, l].astype(f32) * spread
                sums[v] = term if k == 0 else sums[v] + term
        for v in range(p.V):
            part[v, l] = p.ens * sums[v]
    for s in range(p.S):
        for l in range(p.L):
            tile, j = p.slot(p.K + s, l)
            own = me * p.S + s
            part[own, l] = part[own, l] + p.stat * static_scale[s, l] * gather(out, tile, strided(j, R))


def curvature_kernel(p, first, *refs):
    if first:
        part, got, norm, obs, cls, image, send = refs
    else:
        part, got, norm, obs, cls, image_before, step, image, send = refs
    me = lax.axis_index("mem")
    if first:
        for v in range(p.V):
            for l in range(p.L):
                value = part[v, l]
                for other in range(p.mem - 1):
                    value = value + got[other, v, l].astype(f32)
                image[v, l] = value
    total = jnp.zeros((p.R, p.X), f32)
    for s in range(p.S):
        for l in range(p.L):
            own = me * p.S + s
            if first:
                value = image[own, l]
                misfit = -obs[s, l]
            else:
                value = part[own, l]
                for other in range(p.mem - 1):
                    value = value + got[other, s, l].astype(f32)
                image[s, l] = value
                misfit = -(step[0:1, 0:1] * image_before[own, l]) - obs[s, l]
            index = cls[s, l]
            threshold = table(index, huber_levels)
            weight = jnp.where(index > 0, threshold / jnp.maximum(jnp.abs(misfit), threshold), 0.0)
            total = total + weight * value * value
    total = jnp.sum(total, axis=0, keepdims=True)
    total = sum(total[:, i * LANES : (i + 1) * LANES] for i in range(p.X // LANES))
    both = jnp.concatenate([norm[...], total], axis=1)
    send[...] = jnp.broadcast_to(both, send.shape)


def final_kernel(p, got, step, grad0, grad1, image0, image1, control, static_control, increment):
    me = lax.axis_index("mem")
    total = jnp.sum(got[...], axis=0, keepdims=True)
    norm = jnp.sum(total[:, :LANES], axis=1, keepdims=True)
    curvature = jnp.sum(total[:, LANES:], axis=1, keepdims=True)
    second = norm / (norm + curvature)
    first = step[0:1, 0:1]
    for field in range(p.F):
        for l in range(p.L):
            tile, lane = p.slot(field, l)
            where = strided(SWEEPS * SUB + lane, p.R)
            value = -(first * gather(grad0, tile, where)) - second * gather(grad1, tile, where)
            if field < p.K:
                control[field, l] = value
            else:
                static_control[field - p.K, l] = value
    for s in range(p.S):
        for l in range(p.L):
            increment[s, l] = -(first * image0[me * p.S + s, l]) - second * image1[s, l]


def call(kernel, p, outs, scratch, name):
    vmem = pl.BlockSpec(memory_space=pltpu.VMEM)

    def run(*args):
        return pl.pallas_call(
            kernel,
            out_shape=tuple(jax.ShapeDtypeStruct(shape, dtype) for shape, dtype in outs),
            in_specs=[vmem] * len(args),
            out_specs=tuple(vmem for _ in outs),
            scratch_shapes=[pltpu.VMEM(shape, dtype) for shape, dtype in scratch],
            name=name,
        )(*args)

    return run


def local(members, static_scale, observed, huber_class, scale_index):
    p = Plan(members, static_scale, lax.axis_size("mem"), lax.axis_size("row"))
    K, V, L, R, X, S = p.K, p.V, p.L, p.R, p.X, p.S
    assert R >= 2 * SWEEPS

    def round_mem(block, shift):
        return lax.ppermute(block, "mem", [(i, (i + shift) % p.mem) for i in range(p.mem)])

    def round_row(block, shift):
        return lax.ppermute(block, "row", [(i, (i + shift) % p.row) for i in range(p.row)])

    me = lax.axis_index("mem")
    shifts = range(1, p.mem)
    obs_in = jnp.stack([round_mem(observed, shift) for shift in shifts])
    cls_in = jnp.stack([round_mem(huber_class, shift) for shift in shifts])
    C = p.C
    back_shape = ((p.PN, C, R * SUB, LANES), f32)
    sent_shape = ((V, L, R, X), f32)
    halo = (p.PN, C, 2 * SWEEPS * SUB, LANES)
    work = [(halo, f32), (halo, f32), ((C, p.RE * SUB, LANES), f32), ((C, p.RE * SUB, LANES), f32), back_shape]
    grad_shape = ((p.PN, C, p.RG * SUB, LANES), f32)
    norm_shape = ((1, LANES), f32)
    step_shape = ((1, LANES), f32)
    send_shape = ((p.devices, 2 * LANES), f32)

    back, msg = call(
        functools.partial(back_kernel, p, True), p,
        [back_shape, ((p.F + 1, L, R, X), bf16)], [sent_shape], "back0",
    )(members, static_scale, scale_index, observed, huber_class, obs_in, cls_in)
    low, high = round_row(msg, 1), round_row(msg, p.row - 1)
    grad0, kap, norm, part = call(
        functools.partial(sweep_kernel, p, True), p,
        [grad_shape, ((L + p.ST, C, p.RE * SUB, LANES), f32), norm_shape, sent_shape], work, "sweep0",
    )(members, static_scale, scale_index, back, low, high)
    rounded = part.astype(bf16)
    got = jnp.stack([round_mem(rounded, shift) for shift in shifts])
    image0, send = call(
        functools.partial(curvature_kernel, p, True), p, [sent_shape, send_shape], [], "curv0",
    )(part, got, norm, observed, huber_class)
    sums = lax.all_to_all(send, ("mem", "row"), 0, 0, tiled=True)

    back, msg, step = call(
        functools.partial(back_kernel, p, False), p,
        [back_shape, ((p.F, L, R, X), bf16), step_shape], [sent_shape], "back1",
    )(members, static_scale, observed, huber_class, obs_in, cls_in, image0, sums)
    low, high = round_row(msg, 1), round_row(msg, p.row - 1)
    grad1, norm, part = call(
        functools.partial(sweep_kernel, p, False), p, [grad_shape, norm_shape, sent_shape], work, "sweep1",
    )(members, static_scale, kap, grad0, step, back, low, high)
    rounded = part.astype(bf16)
    got = jnp.stack([
        round_mem(lax.dynamic_slice_in_dim(rounded, lax.rem(me + shift, p.mem) * S, S, axis=0), shift)
        for shift in shifts
    ])
    image1, send = call(
        functools.partial(curvature_kernel, p, False), p, [((S, L, R, X), f32), send_shape], [], "curv1",
    )(part, got, norm, observed, huber_class, image0, step)
    sums = lax.all_to_all(send, ("mem", "row"), 0, 0, tiled=True)
    return call(
        functools.partial(final_kernel, p), p,
        [((K, L, R, X), f32), ((S, L, R, X), f32), ((S, L, R, X), f32)], [], "final",
    )(sums, step, grad0, grad1, image0, image1)


def solution(mesh):
    placed = (
        P("mem", None, None, "row", None),
        P("mem", None, "row", None),
        P("mem", None, "row", None),
        P("mem", None, "row", None),
        P(None, "row", None),
    )
    return jax.shard_map(
        local,
        mesh=mesh,
        in_specs=placed,
        out_specs=(
            P("mem", None, "row", None),
            P("mem", None, "row", None),
            P("mem", None, "row", None),
        ),
        check_vma=False,
    )
```

time: 233 us -> 105 us (0.45)
  blocking collectives: 90.1 us -> 24.1 us
  other arithmetic: 37.7 us -> 0.97 us
  Pallas kernels: 0 us -> 32.4 us
  between operations: 21.1 us -> 0.66 us
  waiting for transfers between devices: 42.6 us -> 24.1 us
  starting transfers between devices: 31 us -> 14.5 us
    psum x2 -> x0, blocking collectives: 78.9 us -> none  [local(): norm = lax.psum(local_norm, ('mem', 'row'))]
    reduce_scatter x2 -> x0, waiting for transfers between devices: 38.4 us -> none  [local(): lax.psum_scatter(ens_coef * jnp.sum(members.astype(jnp.float32) * spread....]
    pallas_call x0 -> x7, Pallas kernels: none -> 32.4 us  [run(): pl.pallas_call(kernel, out_shape=tuple((jax.ShapeDtypeStruct(shape, dtype...]
    all_to_all x0 -> x2, blocking collectives: none -> 24.1 us  [local(): sums = lax.all_to_all(send, ('mem', 'row'), 0, 0, tiled=True)]
    mul x24 -> x0, other arithmetic: 22.9 us -> none  [the longest x8 9.04 us: forward(): extended = (extended + wide_kappa * laplace(pad_rows(extended))) * inside]
    ppermute x10 -> x8, waiting for transfers between devices: 4.2 us -> 24.1 us  [the longest x4 13.7 us: round_mem(): lax.ppermute(block, 'mem', [(i, (i + shift) % p.mem) for i in range(p.mem)])]
    ppermute x10 -> x8, starting transfers between devices: 30.9 us -> 14.5 us  [the longest x4 8.89 us: round_row(): lax.ppermute(block, 'row', [(i, (i + shift) % p.row) for i in range(p.row)])]
    all_gather x2 -> x0, blocking collectives: 11.3 us -> none  [local(): lax.all_gather(sent, 'mem', axis=0, tiled=True).astype(jnp.float32)[None]]
  transfers between devices with their start and end apart: 12 -> 8, of which waited for: 6 -> 6; matrix products, arithmetic and copies ran while one was open for 1% -> 0% of each run, Pallas kernels for 0% -> 0%
where the time goes in v1:
time: 105 us; the launch traced here: 104 us
  Pallas kernels  32.4 us (31%)
  waiting for transfers between devices  24.1 us (23%)
  blocking collectives  24.1 us (23%)
  starting transfers between devices  14.5 us (14%)
  local copies, waits for them, and re-layouts  7.31 us (7%)
    pallas_call x7, Pallas kernels, run(): pl.pallas_call(kernel, out_shape=tuple((jax.ShapeDtypeStruct(shape, dtype...  32.4 us
    all_to_all x2, blocking collectives, local(): sums = lax.all_to_all(send, ('mem', 'row'), 0, 0, tiled=True)  24.1 us
    ppermute x4, waiting for transfers between devices, round_mem(): lax.ppermute(block, 'mem', [(i, (i + shift) % p.mem) for i in range(p.mem)])  13.7 us
    ppermute x4, waiting for transfers between devices, round_row(): lax.ppermute(block, 'row', [(i, (i + shift) % p.row) for i in range(p.row)])  10.3 us
    ppermute x4, starting transfers between devices, round_row(): lax.ppermute(block, 'row', [(i, (i + shift) % p.row) for i in range(p.row)])  8.89 us
    ppermute x4, starting transfers between devices, round_mem(): lax.ppermute(block, 'mem', [(i, (i + shift) % p.mem) for i in range(p.mem)])  5.63 us
    unnamed x18, local copies, waits for them, and re-layouts  4.82 us
  transfers between devices with their start and end apart: 8, of which 6 were waited for; matrix products, arithmetic and copies ran while one was open for 0% of the time, Pallas kernels for 0%

profile of v1, /device:TPU:0, one launch (start us, length us, event | category | flops | bytes accessed | tf_op | source)
XLA Modules:
  0.0 104.1 jit_solution(6495997866282892448)
XLA Ops:
  0.6 3.1 %collective-permute-start = (f32[4,2,8,512]{3,2,1,0:T(8,128)}, f32[4,2,8,512]{3,2,1,0:T(8,128)S(1)}, u32[]{:S(2)}, u32[]{:S(2)}) collective-permute-start(f32[4,2,8,512]{3,2,1,0:T(8,128)} %refs_3_.7), channel_id=1, source_target_pairs={{0,16},{16,0},{1,17},{17,1},{2,18},{18,2},{3,19},{19,3},{4,20},{20... | collective-permute-start | bytes 393224 | tf_op jit(solution)/shard_map/ppermute | solution.py:331
  3.7 0.1 collective-permute-start.1
  3.8 4.5 %collective-permute-done = f32[4,2,8,512]{3,2,1,0:T(8,128)S(1)} collective-permute-done((f32[4,2,8,512]{3,2,1,0:T(8,128)}, f32[4,2,8,512]{3,2,1,0:T(8,128)S(1)}, u32[]{:S(2)}, u32[]{:S(2)}) %collective-permute-start) | collective-permute-done | bytes 131104 | tf_op jit(solution)/shard_map/ppermute | solution.py:331
  8.2 0.0 copy-start
  8.3 2.0 %collective-permute-done.1 = s32[4,2,8,512]{3,2,1,0:T(8,128)S(1)} collective-permute-done((s32[4,2,8,512]{3,2,1,0:T(8,128)}, s32[4,2,8,512]{3,2,1,0:T(8,128)S(1)}, u32[]{:S(2)}, u32[]{:S(2)}) %collective-permute-start.1) | collective-permute-done | bytes 131104 | tf_op jit(solution)/shard_map/ppermute | solution.py:331
  10.2 0.0 copy-start.1
  10.2 0.0 copy-done
  10.2 0.7 copy-done.1
  10.9 3.3 %back0.1 = (f32[5,4,64,128]{3,2,1,0:T(8,128)}, bf16[21,2,8,512]{3,2,1,0:T(8,128)(2,1)}) custom-call(bf16[16,8,2,8,512]{4,3,2,1,0:T(8,128)(2,1)} %refs_0_.7, f32[4,2,8,512]{3,2,1,0:T(8,128)} %refs_1_.7, s32[2,8,512]{2,1,0:T(8,128)} %refs_2_.4, f32[4,2,8,512]{3,2,1,0:T(8,128)} %refs_3_.7, s32[4,2,8,512]{3,2,1,0:T(8,128)} %refs_4_.5, ...), custom_call_target="tpu_custom_call" | custom-call | tf_op jit(solution)/shard_map/back0/pallas_call | solution.py:313
  14.2 0.0 collective-permute-start.2
  14.2 4.4 %collective-permute-start.3 = (bf16[21,2,8,512]{3,2,1,0:T(8,128)(2,1)}, bf16[21,2,8,512]{3,2,1,0:T(8,128)(2,1)S(1)}, u32[]{:S(2)}, u32[]{:S(2)}) collective-permute-start(bf16[21,2,8,512]{3,2,1,0:T(8,128)(2,1)} %get-tuple-element.20), channel_id=1, source_target_pairs={{0,15},{1,0},{2,1},{3,2},{4,3},{5,4},{6,5},{7,6},{8,7},{9,8},{10,9... | collective-permute-start | bytes 1032200 | tf_op jit(solution)/shard_map/ppermute | solution.py:334
  18.7 5.2 %collective-permute-done.2.refs_4_ = bf16[21,2,8,512]{3,2,1,0:T(8,128)(2,1)S(1)} collective-permute-done((bf16[21,2,8,512]{3,2,1,0:T(8,128)(2,1)}, bf16[21,2,8,512]{3,2,1,0:T(8,128)(2,1)S(1)}, u32[]{:S(2)}, u32[]{:S(2)}) %collective-permute-start.2) | collective-permute-done | bytes 344096 | tf_op jit(solution)/shard_map/ppermute | solution.py:334
  23.9 0.0 copy-start.2
  23.9 0.0 collective-permute-done.3.refs_5_
  23.9 0.0 copy-start.3
  23.9 0.7 copy-done.2
  24.6 0.1 copy-done.3
  24.7 9.1 %sweep0.1 = (f32[5,4,128,128]{3,2,1,0:T(8,128)}, f32[3,4,192,128]{3,2,1,0:T(8,128)}, f32[1,128]{1,0:T(1,128)}, f32[8,2,8,512]{3,2,1,0:T(8,128)}) custom-call(bf16[16,8,2,8,512]{4,3,2,1,0:T(8,128)(2,1)} %refs_0_.7, f32[4,2,8,512]{3,2,1,0:T(8,128)} %refs_1_.7, s32[2,8,512]{2,1,0:T(8,128)} %refs_2_.4, f32[5,4,64,128]{3,2,1,0:T(8,128)} %get-tuple-element.19.refs_3_, ...), custom_call_target="tpu_custom_call" | custom-call | tf_op jit(solution)/shard_map/sweep0/pallas_call | solution.py:313
  33.8 1.0 convert_element_type.6
  34.8 1.8 %collective-permute-start.4 = (bf16[8,2,8,512]{3,2,1,0:T(8,128)(2,1)S(1)}, bf16[8,2,8,512]{3,2,1,0:T(8,128)(2,1)S(1)}, u32[]{:S(2)}, u32[]{:S(2)}) collective-permute-start(bf16[8,2,8,512]{3,2,1,0:T(8,128)(2,1)S(1)} %convert_element_type.6), channel_id=1, source_target_pairs={{0,16},{16,0},{1,17},{17,1},{2,18},{18,2},{3,19},{19,3},{4,20},{20... | collective-permute-start | bytes 393224 | tf_op jit(solution)/shard_map/ppermute | solution.py:331
  36.6 3.2 %collective-permute-done.4 = bf16[8,2,8,512]{3,2,1,0:T(8,128)(2,1)S(1)} collective-permute-done((bf16[8,2,8,512]{3,2,1,0:T(8,128)(2,1)S(1)}, bf16[8,2,8,512]{3,2,1,0:T(8,128)(2,1)S(1)}, u32[]{:S(2)}, u32[]{:S(2)}) %collective-permute-start.4) | collective-permute-done | bytes 131104 | tf_op jit(solution)/shard_map/ppermute | solution.py:331
  39.8 0.0 copy-start.6
  39.8 0.7 copy-done.6
  40.5 1.9 %curv0.1 = (f32[8,2,8,512]{3,2,1,0:T(8,128)}, f32[32,256]{1,0:T(8,128)}) custom-call(f32[8,2,8,512]{3,2,1,0:T(8,128)} %get-tuple-element.23.refs_0_, bf16[1,8,2,8,512]{4,3,2,1,0:T(8,128)(2,1)} %bitcast.18, f32[1,128]{1,0:T(1,128)} %get-tuple-element.24.refs_2_, f32[4,2,8,512]{3,2,1,0:T(8,128)} %refs_3_.7, s32[4,2,8,512]{3,2,1,0:T(8,128)} %refs_4_.5), custom_call_target="tpu_custom_call" | custom-call | tf_op jit(solution)/shard_map/curv0/pallas_call | solution.py:313
  42.4 0.8 copy.8
  43.2 14.0 %all_to_all.22 = f32[32,1,256]{2,1,0:T(1,128)S(1)} all-to-all(f32[32,1,256]{2,1,0:T(1,128)S(1)} %copy.8), channel_id=1, replica_groups=mesh['mem'=2,'row'=16] {'mem','row'}, dimensions={0} | all-to-all | bytes 65536 | tf_op jit(solution)/shard_map/all_to_all | solution.py:364
  57.2 0.6 copy.15
  57.8 3.4 %back1.1 = (f32[5,4,64,128]{3,2,1,0:T(8,128)}, bf16[20,2,8,512]{3,2,1,0:T(8,128)(2,1)}, f32[1,128]{1,0:T(1,128)}) custom-call(bf16[16,8,2,8,512]{4,3,2,1,0:T(8,128)(2,1)} %refs_0_.7, f32[4,2,8,512]{3,2,1,0:T(8,128)} %refs_1_.7, f32[4,2,8,512]{3,2,1,0:T(8,128)} %refs_3_.7, s32[4,2,8,512]{3,2,1,0:T(8,128)} %refs_4_.5, f32[1,4,2,8,512]{4,3,2,1,0:T(8,128)} %bitcast.13, ...), custom_call_target="tpu_custom_call" | custom-call | tf_op jit(solution)/shard_map/back1/pallas_call | solution.py:313
  61.2 0.1 collective-permute-start.5
  61.3 4.3 %collective-permute-start.6 = (bf16[20,2,8,512]{3,2,1,0:T(8,128)(2,1)}, bf16[20,2,8,512]{3,2,1,0:T(8,128)(2,1)S(1)}, u32[]{:S(2)}, u32[]{:S(2)}) collective-permute-start(bf16[20,2,8,512]{3,2,1,0:T(8,128)(2,1)} %get-tuple-element.29), channel_id=1, source_target_pairs={{0,15},{1,0},{2,1},{3,2},{4,3},{5,4},{6,5},{7,6},{8,7},{9,8},{10,9... | collective-permute-start | bytes 983048 | tf_op jit(solution)/shard_map/ppermute | solution.py:334
  65.7 5.1 %collective-permute-done.5.refs_6_ = bf16[20,2,8,512]{3,2,1,0:T(8,128)(2,1)S(1)} collective-permute-done((bf16[20,2,8,512]{3,2,1,0:T(8,128)(2,1)}, bf16[20,2,8,512]{3,2,1,0:T(8,128)(2,1)S(1)}, u32[]{:S(2)}, u32[]{:S(2)}) %collective-permute-start.5) | collective-permute-done | bytes 327712 | tf_op jit(solution)/shard_map/ppermute | solution.py:334
  70.7 0.0 copy-start.4
  70.7 0.0 collective-permute-done.6.refs_7_
  70.7 0.0 copy-start.5
  70.7 0.7 copy-done.4
  71.5 0.1 copy-done.5
  71.6 9.8 %sweep1.1 = (f32[5,4,128,128]{3,2,1,0:T(8,128)}, f32[1,128]{1,0:T(1,128)}, f32[8,2,8,512]{3,2,1,0:T(8,128)}) custom-call(bf16[16,8,2,8,512]{4,3,2,1,0:T(8,128)(2,1)} %refs_0_.7, f32[4,2,8,512]{3,2,1,0:T(8,128)} %refs_1_.7, f32[3,4,192,128]{3,2,1,0:T(8,128)} %get-tuple-element.21.refs_2_, f32[5,4,128,128]{3,2,1,0:T(8,128)} %get-tuple-element.22.refs_3_.grad0, ...), custom_call_target="tpu_custom_call" | custom-call | tf_op jit(solution)/shard_map/sweep1/pallas_call | solution.py:313
  81.3 0.9 dynamic-slice_convert_fusion
  82.3 0.7 collective-permute-start.7
  82.9 4.1 %collective-permute-done.7 = bf16[4,2,8,512]{3,2,1,0:T(8,128)(2,1)S(1)} collective-permute-done((bf16[4,2,8,512]{3,2,1,0:T(8,128)(2,1)S(1)}, bf16[4,2,8,512]{3,2,1,0:T(8,128)(2,1)S(1)}, u32[]{:S(2)}, u32[]{:S(2)}) %collective-permute-start.7) | collective-permute-done | bytes 65568 | tf_op jit(solution)/shard_map/ppermute | solution.py:331
  87.0 0.0 copy-start.7
  87.0 0.6 copy-done.7
  87.7 1.9 %curv1.1 = (f32[4,2,8,512]{3,2,1,0:T(8,128)}, f32[32,256]{1,0:T(8,128)}) custom-call(f32[8,2,8,512]{3,2,1,0:T(8,128)} %get-tuple-element.30.refs_0_, bf16[1,4,2,8,512]{4,3,2,1,0:T(8,128)(2,1)} %bitcast.19, f32[1,128]{1,0:T(1,128)} %get-tuple-element.31.refs_2_, f32[4,2,8,512]{3,2,1,0:T(8,128)} %refs_3_.7, s32[4,2,8,512]{3,2,1,0:T(8,128)} %refs_4_.5, ...), custom_call_target="tpu_custom_call" | custom-call | tf_op jit(solution)/shard_map/curv1/pallas_call | solution.py:313
  89.6 0.8 copy.9
  90.4 10.1 %all_to_all.23 = f32[32,1,256]{2,1,0:T(1,128)S(1)} all-to-all(f32[32,1,256]{2,1,0:T(1,128)S(1)} %copy.9), channel_id=1, replica_groups=mesh['mem'=2,'row'=16] {'mem','row'}, dimensions={0} | all-to-all | bytes 65536 | tf_op jit(solution)/shard_map/all_to_all | solution.py:382
  100.5 0.6 copy.14
  101.1 2.9 %final.1 = (f32[16,2,8,512]{3,2,1,0:T(8,128)}, f32[4,2,8,512]{3,2,1,0:T(8,128)}, f32[4,2,8,512]{3,2,1,0:T(8,128)}) custom-call(f32[32,256]{1,0:T(8,128)} %bitcast.16, f32[1,128]{1,0:T(1,128)} %get-tuple-element.27.refs_4_.refs_6_.step, f32[5,4,128,128]{3,2,1,0:T(8,128)} %get-tuple-element.22.refs_3_.grad0, f32[5,4,128,128]{3,2,1,0:T(8,128)} %get-tuple-element.33.grad1, ...), custom_call_target="tpu_custom_call" | custom-call | tf_op jit(solution)/shard_map/final/pallas_call | solution.py:313
Async XLA Ops:
  0.6 7.6 %collective-permute-start = (f32[4,2,8,512]{3,2,1,0:T(8,128)}, f32[4,2,8,512]{3,2,1,0:T(8,128)S(1)}, u32[]{:S(2)}, u32[]{:S(2)}) collective-permute-start(f32[4,2,8,512]{3,2,1,0:T(8,128)} %refs_3_.7), channel_id=1, source_target_pairs={{0,16},{16,0},{1,17},{17,1},{2,18},{18,2},{3,19},{19,3},{4,20},{20... | collective-permute-start | bytes 393224 | tf_op jit(solution)/shard_map/ppermute | solution.py:331
  3.7 6.5 %collective-permute-start.1 = (s32[4,2,8,512]{3,2,1,0:T(8,128)}, s32[4,2,8,512]{3,2,1,0:T(8,128)S(1)}, u32[]{:S(2)}, u32[]{:S(2)}) collective-permute-start(s32[4,2,8,512]{3,2,1,0:T(8,128)} %refs_4_.5), channel_id=1, source_target_pairs={{0,16},{16,0},{1,17},{17,1},{2,18},{18,2},{3,19},{19,3},{4,20},{20... | collective-permute-start | bytes 393224 | tf_op jit(solution)/shard_map/ppermute | solution.py:331
  8.2 2.0 %copy-start = (f32[4,2,8,512]{3,2,1,0:T(8,128)}, f32[4,2,8,512]{3,2,1,0:T(8,128)S(1)}, u32[]{:S(2)}) copy-start(f32[4,2,8,512]{3,2,1,0:T(8,128)S(1)} %collective-permute-done) | copy-start | bytes 393220
  10.2 0.7 copy-start.1
  14.2 9.7 %collective-permute-start.2 = (bf16[21,2,8,512]{3,2,1,0:T(8,128)(2,1)}, bf16[21,2,8,512]{3,2,1,0:T(8,128)(2,1)S(1)}, u32[]{:S(2)}, u32[]{:S(2)}) collective-permute-start(bf16[21,2,8,512]{3,2,1,0:T(8,128)(2,1)} %get-tuple-element.20), channel_id=1, source_target_pairs={{0,1},{1,2},{2,3},{3,4},{4,5},{5,6},{6,7},{7,8},{8,9},{9,10},{10,1... | collective-permute-start | bytes 1032200 | tf_op jit(solution)/shard_map/ppermute | solution.py:334
  14.2 9.7 %collective-permute-start.3 = (bf16[21,2,8,512]{3,2,1,0:T(8,128)(2,1)}, bf16[21,2,8,512]{3,2,1,0:T(8,128)(2,1)S(1)}, u32[]{:S(2)}, u32[]{:S(2)}) collective-permute-start(bf16[21,2,8,512]{3,2,1,0:T(8,128)(2,1)} %get-tuple-element.20), channel_id=1, source_target_pairs={{0,15},{1,0},{2,1},{3,2},{4,3},{5,4},{6,5},{7,6},{8,7},{9,8},{10,9... | collective-permute-start | bytes 1032200 | tf_op jit(solution)/shard_map/ppermute | solution.py:334
  23.9 0.7 copy-start.2
  23.9 0.8 copy-start.3
  34.8 5.0 %collective-permute-start.4 = (bf16[8,2,8,512]{3,2,1,0:T(8,128)(2,1)S(1)}, bf16[8,2,8,512]{3,2,1,0:T(8,128)(2,1)S(1)}, u32[]{:S(2)}, u32[]{:S(2)}) collective-permute-start(bf16[8,2,8,512]{3,2,1,0:T(8,128)(2,1)S(1)} %convert_element_type.6), channel_id=1, source_target_pairs={{0,16},{16,0},{1,17},{17,1},{2,18},{18,2},{3,19},{19,3},{4,20},{20... | collective-permute-start | bytes 393224 | tf_op jit(solution)/shard_map/ppermute | solution.py:331
  39.8 0.7 copy-start.6
  61.2 9.5 %collective-permute-start.5 = (bf16[20,2,8,512]{3,2,1,0:T(8,128)(2,1)}, bf16[20,2,8,512]{3,2,1,0:T(8,128)(2,1)S(1)}, u32[]{:S(2)}, u32[]{:S(2)}) collective-permute-start(bf16[20,2,8,512]{3,2,1,0:T(8,128)(2,1)} %get-tuple-element.29), channel_id=1, source_target_pairs={{0,1},{1,2},{2,3},{3,4},{4,5},{5,6},{6,7},{7,8},{8,9},{9,10},{10,1... | collective-permute-start | bytes 983048 | tf_op jit(solution)/shard_map/ppermute | solution.py:334
  61.3 9.4 %collective-permute-start.6 = (bf16[20,2,8,512]{3,2,1,0:T(8,128)(2,1)}, bf16[20,2,8,512]{3,2,1,0:T(8,128)(2,1)S(1)}, u32[]{:S(2)}, u32[]{:S(2)}) collective-permute-start(bf16[20,2,8,512]{3,2,1,0:T(8,128)(2,1)} %get-tuple-element.29), channel_id=1, source_target_pairs={{0,15},{1,0},{2,1},{3,2},{4,3},{5,4},{6,5},{7,6},{8,7},{9,8},{10,9... | collective-permute-start | bytes 983048 | tf_op jit(solution)/shard_map/ppermute | solution.py:334
  70.7 0.7 copy-start.4
  70.7 0.8 copy-start.5
  82.3 4.8 %collective-permute-start.7 = (bf16[4,2,8,512]{3,2,1,0:T(8,128)(2,1)S(1)}, bf16[4,2,8,512]{3,2,1,0:T(8,128)(2,1)S(1)}, u32[]{:S(2)}, u32[]{:S(2)}) collective-permute-start(bf16[4,2,8,512]{3,2,1,0:T(8,128)(2,1)S(1)} %dynamic-slice_convert_fusion), channel_id=1, source_target_pairs={{0,16},{16,0},{1,17},{17,1},{2,18},{18,2},{3,19},{19,3},{4,20},{20... | collective-permute-start | bytes 196616 | tf_op jit(solution)/shard_map/ppermute | solution.py:331
  87.0 0.6 copy-start.7

commit v2 on v1

--- a/solution.py
+++ b/solution.py
@@ -72,7 +72,7 @@
     if p.pads:
         back[...] = jnp.zeros(back.shape, f32)
     if not first:
-        total = jnp.sum(got[...], axis=0, keepdims=True)
+        total = jnp.sum(got[...], axis=0)
         norm = jnp.sum(total[:, :LANES], axis=1, keepdims=True)
         curvature = jnp.sum(total[:, LANES:], axis=1, keepdims=True)
         step = norm / (norm + curvature)
@@ -130,9 +130,9 @@
 
 def sweep_kernel(p, first, *refs):
     if first:
-        members, static_scale, scale_index, back, low, high, grad, kap, norm, part, lo, hi, a, b, out = refs
+        members, static_scale, scale_index, back, low, high, grad, kap, norm, part, ship, lo, hi, a, b, out = refs
     else:
-        members, static_scale, kap, before, step, back, low, high, grad, norm, part, lo, hi, a, b, out = refs
+        members, static_scale, kap, before, step, back, low, high, grad, norm, part, ship, lo, hi, a, b, out = refs
     me, at = lax.axis_index("mem"), lax.axis_index("row")
     low_ok = jnp.where(at > 0, 1.0, 0.0).astype(f32)
     high_ok = jnp.where(at < p.row - 1, 1.0, 0.0).astype(f32)
@@ -247,6 +247,15 @@
             tile, j = p.slot(p.K + s, l)
             own = me * p.S + s
             part[own, l] = part[own, l] + p.stat * static_scale[s, l] * gather(out, tile, strided(j, R))
+    for l in range(p.L):
+        if first:
+            for v in range(p.V):
+                ship[v, l] = part[v, l].astype(bf16)
+            continue
+        for shift in range(1, p.mem):
+            base = lax.rem(me + shift, p.mem) * p.S
+            for s in range(p.S):
+                ship[shift - 1, s, l] = part[base + s, l].astype(bf16)
 
 
 def curvature_kernel(p, first, *refs):
@@ -282,12 +291,12 @@
     total = jnp.sum(total, axis=0, keepdims=True)
     total = sum(total[:, i * LANES : (i + 1) * LANES] for i in range(p.X // LANES))
     both = jnp.concatenate([norm[...], total], axis=1)
-    send[...] = jnp.broadcast_to(both, send.shape)
+    send[...] = jnp.broadcast_to(both[None], send.shape)
 
 
 def final_kernel(p, got, step, grad0, grad1, image0, image1, control, static_control, increment):
     me = lax.axis_index("mem")
-    total = jnp.sum(got[...], axis=0, keepdims=True)
+    total = jnp.sum(got[...], axis=0)
     norm = jnp.sum(total[:, :LANES], axis=1, keepdims=True)
     curvature = jnp.sum(total[:, LANES:], axis=1, keepdims=True)
     second = norm / (norm + curvature)
@@ -316,6 +325,7 @@
             in_specs=[vmem] * len(args),
             out_specs=tuple(vmem for _ in outs),
             scratch_shapes=[pltpu.VMEM(shape, dtype) for shape, dtype in scratch],
+            compiler_params=pltpu.CompilerParams(vmem_limit_bytes=16 << 20),
             name=name,
         )(*args)
 
@@ -333,7 +343,6 @@
     def round_row(block, shift):
         return lax.ppermute(block, "row", [(i, (i + shift) % p.row) for i in range(p.row)])
 
-    me = lax.axis_index("mem")
     shifts = range(1, p.mem)
     obs_in = jnp.stack([round_mem(observed, shift) for shift in shifts])
     cls_in = jnp.stack([round_mem(huber_class, shift) for shift in shifts])
@@ -345,41 +354,38 @@
     grad_shape = ((p.PN, C, p.RG * SUB, LANES), f32)
     norm_shape = ((1, LANES), f32)
     step_shape = ((1, LANES), f32)
-    send_shape = ((p.devices, 2 * LANES), f32)
+    send_shape = ((p.devices, 1, 2 * LANES), f32)
 
     back, msg = call(
         functools.partial(back_kernel, p, True), p,
         [back_shape, ((p.F + 1, L, R, X), bf16)], [sent_shape], "back0",
     )(members, static_scale, scale_index, observed, huber_class, obs_in, cls_in)
     low, high = round_row(msg, 1), round_row(msg, p.row - 1)
-    grad0, kap, norm, part = call(
+    grad0, kap, norm, part, ship = call(
         functools.partial(sweep_kernel, p, True), p,
-        [grad_shape, ((L + p.ST, C, p.RE * SUB, LANES), f32), norm_shape, sent_shape], work, "sweep0",
+        [grad_shape, ((L + p.ST, C, p.RE * SUB, LANES), f32), norm_shape, sent_shape, ((V, L, R, X), bf16)],
+        work, "sweep0",
     )(members, static_scale, scale_index, back, low, high)
-    rounded = part.astype(bf16)
-    got = jnp.stack([round_mem(rounded, shift) for shift in shifts])
+    got = jnp.stack([round_mem(ship, shift) for shift in shifts])
     image0, send = call(
         functools.partial(curvature_kernel, p, True), p, [sent_shape, send_shape], [], "curv0",
     )(part, got, norm, observed, huber_class)
-    sums = lax.all_to_all(send, ("mem", "row"), 0, 0, tiled=True)
+    sums = lax.all_to_all(send, ("mem", "row"), 0, 0)
 
     back, msg, step = call(
         functools.partial(back_kernel, p, False), p,
         [back_shape, ((p.F, L, R, X), bf16), step_shape], [sent_shape], "back1",
     )(members, static_scale, observed, huber_class, obs_in, cls_in, image0, sums)
     low, high = round_row(msg, 1), round_row(msg, p.row - 1)
-    grad1, norm, part = call(
-        functools.partial(sweep_kernel, p, False), p, [grad_shape, norm_shape, sent_shape], work, "sweep1",
+    grad1, norm, part, ship = call(
+        functools.partial(sweep_kernel, p, False), p,
+        [grad_shape, norm_shape, sent_shape, ((p.mem - 1, S, L, R, X), bf16)], work, "sweep1",
     )(members, static_scale, kap, grad0, step, back, low, high)
-    rounded = part.astype(bf16)
-    got = jnp.stack([
-        round_mem(lax.dynamic_slice_in_dim(rounded, lax.rem(me + shift, p.mem) * S, S, axis=0), shift)
-        for shift in shifts
-    ])
+    got = jnp.stack([round_mem(ship[shift - 1], shift) for shift in shifts])
     image1, send = call(
         functools.partial(curvature_kernel, p, False), p, [((S, L, R, X), f32), send_shape], [], "curv1",
     )(part, got, norm, observed, huber_class, image0, step)
-    sums = lax.all_to_all(send, ("mem", "row"), 0, 0, tiled=True)
+    sums = lax.all_to_all(send, ("mem", "row"), 0, 0)
     return call(
         functools.partial(final_kernel, p), p,
         [((K, L, R, X), f32), ((S, L, R, X), f32), ((S, L, R, X), f32)], [], "final",

time: 105 us -> 83.7 us (0.80)
  Pallas kernels: 32.4 us -> 15.9 us
  waiting for transfers between devices: 24.1 us -> 32.3 us
  starting transfers between devices: 14.5 us -> 9.29 us
  blocking collectives: 24.1 us -> 20.2 us
  local copies, waits for them, and re-layouts: 7.31 us -> 5.07 us
    pallas_call x7, Pallas kernels: 32.4 us -> 15.9 us  [run(): pl.pallas_call(kernel, out_shape=tuple((jax.ShapeDtypeStruct(shape, dtype...]
    ppermute x4, waiting for transfers between devices: 10.3 us -> 18.4 us  [round_row(): lax.ppermute(block, 'row', [(i, (i + shift) % p.row) for i in range(p.row)])]
    ppermute x4, starting transfers between devices: 8.89 us -> 3.95 us  [round_row(): lax.ppermute(block, 'row', [(i, (i + shift) % p.row) for i in range(p.row)])]
    all_to_all x2, blocking collectives: 24.1 us -> 20.2 us  [local(): sums = lax.all_to_all(send, ('mem', 'row'), 0, 0)]
    all_to_all x2 -> x0, local copies, waits for them, and re-layouts: 1.58 us -> none  [local(): sums = lax.all_to_all(send, ('mem', 'row'), 0, 0, tiled=True)]
    unnamed x18 -> x16, local copies, waits for them, and re-layouts: 4.82 us -> 5.07 us
  transfers between devices with their start and end apart: 8 -> 8, of which waited for: 6 -> 8; matrix products, arithmetic and copies ran while one was open for 0% -> 0% of each run, Pallas kernels for 0% -> 0%
where the time goes in v2:
time: 83.7 us; the launch traced here: 83.4 us
  waiting for transfers between devices  32.3 us (39%)
  blocking collectives  20.2 us (24%)
  Pallas kernels  15.9 us (19%)
  starting transfers between devices  9.29 us (11%)
  local copies, waits for them, and re-layouts  5.07 us (6%)
    all_to_all x2, blocking collectives, local(): sums = lax.all_to_all(send, ('mem', 'row'), 0, 0)  20.2 us
    ppermute x4, waiting for transfers between devices, round_row(): lax.ppermute(block, 'row', [(i, (i + shift) % p.row) for i in range(p.row)])  18.4 us
    pallas_call x7, Pallas kernels, run(): pl.pallas_call(kernel, out_shape=tuple((jax.ShapeDtypeStruct(shape, dtype...  15.9 us
    ppermute x4, waiting for transfers between devices, round_mem(): lax.ppermute(block, 'mem', [(i, (i + shift) % p.mem) for i in range(p.mem)])  13.9 us
    ppermute x4, starting transfers between devices, round_mem(): lax.ppermute(block, 'mem', [(i, (i + shift) % p.mem) for i in range(p.mem)])  5.34 us
    unnamed x16, local copies, waits for them, and re-layouts  5.07 us
    ppermute x4, starting transfers between devices, round_row(): lax.ppermute(block, 'row', [(i, (i + shift) % p.row) for i in range(p.row)])  3.95 us
  transfers between devices with their start and end apart: 8, of which 8 were waited for; matrix products, arithmetic and copies ran while one was open for 0% of the time, Pallas kernels for 0%

profile of v2, /device:TPU:0, one launch (start us, length us, event | category | flops | bytes accessed | tf_op | source)
XLA Modules:
  0.0 83.4 jit_solution(11557587213072115596)
XLA Ops:
  0.6 3.1 %collective-permute-start = (f32[4,2,8,512]{3,2,1,0:T(8,128)}, f32[4,2,8,512]{3,2,1,0:T(8,128)S(1)}, u32[]{:S(2)}, u32[]{:S(2)}) collective-permute-start(f32[4,2,8,512]{3,2,1,0:T(8,128)} %refs_3_.7), channel_id=1, source_target_pairs={{0,16},{16,0},{1,17},{17,1},{2,18},{18,2},{3,19},{19,3},{4,20},{20... | collective-permute-start | bytes 393224 | tf_op jit(solution)/shard_map/ppermute | solution.py:341
  3.7 0.1 collective-permute-start.1
  3.8 4.5 %collective-permute-done = f32[4,2,8,512]{3,2,1,0:T(8,128)S(1)} collective-permute-done((f32[4,2,8,512]{3,2,1,0:T(8,128)}, f32[4,2,8,512]{3,2,1,0:T(8,128)S(1)}, u32[]{:S(2)}, u32[]{:S(2)}) %collective-permute-start) | collective-permute-done | bytes 131104 | tf_op jit(solution)/shard_map/ppermute | solution.py:341
  8.3 2.0 %collective-permute-done.1 = s32[4,2,8,512]{3,2,1,0:T(8,128)S(1)} collective-permute-done((s32[4,2,8,512]{3,2,1,0:T(8,128)}, s32[4,2,8,512]{3,2,1,0:T(8,128)S(1)}, u32[]{:S(2)}, u32[]{:S(2)}) %collective-permute-start.1) | collective-permute-done | bytes 131104 | tf_op jit(solution)/shard_map/ppermute | solution.py:341
  10.2 0.0 copy-start
  10.2 1.6 %copy-done = bf16[16,8,2,8,512]{4,3,2,1,0:T(8,128)(2,1)S(1)} copy-done((bf16[16,8,2,8,512]{4,3,2,1,0:T(8,128)(2,1)S(1)}, bf16[16,8,2,8,512]{4,3,2,1,0:T(8,128)(2,1)}, u32[]{:S(2)}) %copy-start) | copy-done | bytes 2097176
  11.8 0.0 copy-start.2
  11.8 0.9 %copy-done.2 = f32[4,2,8,512]{3,2,1,0:T(8,128)S(1)} copy-done((f32[4,2,8,512]{3,2,1,0:T(8,128)S(1)}, f32[4,2,8,512]{3,2,1,0:T(8,128)}, u32[]{:S(2)}) %copy-start.2) | copy-done | bytes 131096
  12.7 0.0 copy-start.3
  12.7 0.9 %copy-done.3 = f32[4,2,8,512]{3,2,1,0:T(8,128)S(1)} copy-done((f32[4,2,8,512]{3,2,1,0:T(8,128)S(1)}, f32[4,2,8,512]{3,2,1,0:T(8,128)}, u32[]{:S(2)}) %copy-start.3) | copy-done | bytes 131096
  13.6 0.0 copy-start.5
  13.6 0.9 %copy-done.5 = s32[4,2,8,512]{3,2,1,0:T(8,128)S(1)} copy-done((s32[4,2,8,512]{3,2,1,0:T(8,128)S(1)}, s32[4,2,8,512]{3,2,1,0:T(8,128)}, u32[]{:S(2)}) %copy-start.5) | copy-done | bytes 131096
  14.5 0.0 copy-start.7
  14.5 0.8 copy-done.7
  15.3 0.6 back0.1
  15.9 3.4 %collective-permute-start.3 = (bf16[21,2,8,512]{3,2,1,0:T(8,128)(2,1)S(1)}, bf16[21,2,8,512]{3,2,1,0:T(8,128)(2,1)S(1)}, u32[]{:S(2)}, u32[]{:S(2)}) collective-permute-start(bf16[21,2,8,512]{3,2,1,0:T(8,128)(2,1)S(1)} %get-tuple-element.22), channel_id=1, source_target_pairs={{0,15},{1,0},{2,1},{3,2},{4,3},{5,4},{6,5},{7,6},{8,7},{9,8},{10,9... | collective-permute-start | bytes 1032200 | tf_op jit(solution)/shard_map/ppermute | solution.py:344
  19.2 0.0 collective-permute-start.2
  19.3 4.8 %collective-permute-done.3.refs_5_ = bf16[21,2,8,512]{3,2,1,0:T(8,128)(2,1)S(1)} collective-permute-done((bf16[21,2,8,512]{3,2,1,0:T(8,128)(2,1)S(1)}, bf16[21,2,8,512]{3,2,1,0:T(8,128)(2,1)S(1)}, u32[]{:S(2)}, u32[]{:S(2)}) %collective-permute-start.3) | collective-permute-done | bytes 344096 | tf_op jit(solution)/shard_map/ppermute | solution.py:344
  24.0 4.6 %collective-permute-done.2.refs_4_ = bf16[21,2,8,512]{3,2,1,0:T(8,128)(2,1)S(1)} collective-permute-done((bf16[21,2,8,512]{3,2,1,0:T(8,128)(2,1)S(1)}, bf16[21,2,8,512]{3,2,1,0:T(8,128)(2,1)S(1)}, u32[]{:S(2)}, u32[]{:S(2)}) %collective-permute-start.2) | collective-permute-done | bytes 344096 | tf_op jit(solution)/shard_map/ppermute | solution.py:344
  28.6 0.0 copy-start.4
  28.6 0.0 copy-start.6
  28.6 0.0 copy-start.1
  28.6 6.6 %sweep0.1 = (f32[5,4,128,128]{3,2,1,0:T(8,128)S(1)}, f32[3,4,192,128]{3,2,1,0:T(8,128)S(1)}, f32[1,128]{1,0:T(1,128)S(1)}, f32[8,2,8,512]{3,2,1,0:T(8,128)S(1)}, bf16[8,2,8,512]{3,2,1,0:T(8,128)(2,1)S(1)}) custom-call(bf16[16,8,2,8,512]{4,3,2,1,0:T(8,128)(2,1)S(1)} %copy-done, f32[4,2,8,512]{3,2,1,0:T(8,128)S(1)} %copy-done.2, s32[2,8,512]{2,1,0:T(8,128)S(1)} %copy-done.7, ...), custom_call_target="tpu_custom_call" | custom-call | tf_op jit(solution)/shard_map/sweep0/pallas_call | solution.py:322
  35.2 1.6 %collective-permute-start.4 = (bf16[8,2,8,512]{3,2,1,0:T(8,128)(2,1)S(1)}, bf16[8,2,8,512]{3,2,1,0:T(8,128)(2,1)S(1)}, u32[]{:S(2)}, u32[]{:S(2)}) collective-permute-start(bf16[8,2,8,512]{3,2,1,0:T(8,128)(2,1)S(1)} %get-tuple-element.26), channel_id=1, source_target_pairs={{0,16},{16,0},{1,17},{17,1},{2,18},{18,2},{3,19},{19,3},{4,20},{20... | collective-permute-start | bytes 393224 | tf_op jit(solution)/shard_map/ppermute | solution.py:341
  36.8 3.4 %collective-permute-done.4 = bf16[8,2,8,512]{3,2,1,0:T(8,128)(2,1)S(1)} collective-permute-done((bf16[8,2,8,512]{3,2,1,0:T(8,128)(2,1)S(1)}, bf16[8,2,8,512]{3,2,1,0:T(8,128)(2,1)S(1)}, u32[]{:S(2)}, u32[]{:S(2)}) %collective-permute-start.4) | collective-permute-done | bytes 131104 | tf_op jit(solution)/shard_map/ppermute | solution.py:341
  40.2 0.0 copy-done.4
  40.2 0.0 copy-done.6
  40.2 0.1 curv0.1
  40.4 10.9 %all_to_all.10.refs_7_ = f32[32,1,256]{2,1,0:T(1,128)S(1)} all-to-all(f32[32,1,256]{2,1,0:T(1,128)S(1)} %get-tuple-element.29), channel_id=1, replica_groups=mesh['mem'=2,'row'=16] {'mem','row'}, dimensions={0} | all-to-all | bytes 65536 | tf_op jit(solution)/shard_map/all_to_all | solution.py:373
  51.2 0.0 copy-done.1
  51.2 0.7 back1.1
  51.9 0.3 collective-permute-start.6
  52.3 0.2 collective-permute-start.5
  52.5 4.4 %collective-permute-done.6.refs_7_ = bf16[20,2,8,512]{3,2,1,0:T(8,128)(2,1)S(1)} collective-permute-done((bf16[20,2,8,512]{3,2,1,0:T(8,128)(2,1)S(1)}, bf16[20,2,8,512]{3,2,1,0:T(8,128)(2,1)S(1)}, u32[]{:S(2)}, u32[]{:S(2)}) %collective-permute-start.6) | collective-permute-done | bytes 327712 | tf_op jit(solution)/shard_map/ppermute | solution.py:344
  56.9 4.7 %collective-permute-done.5.refs_6_ = bf16[20,2,8,512]{3,2,1,0:T(8,128)(2,1)S(1)} collective-permute-done((bf16[20,2,8,512]{3,2,1,0:T(8,128)(2,1)S(1)}, bf16[20,2,8,512]{3,2,1,0:T(8,128)(2,1)S(1)}, u32[]{:S(2)}, u32[]{:S(2)}) %collective-permute-start.5) | collective-permute-done | bytes 327712 | tf_op jit(solution)/shard_map/ppermute | solution.py:344
  61.6 6.6 %sweep1.1 = (f32[5,4,128,128]{3,2,1,0:T(8,128)S(1)}, f32[1,128]{1,0:T(1,128)S(1)}, f32[8,2,8,512]{3,2,1,0:T(8,128)S(1)}, bf16[1,4,2,8,512]{4,3,2,1,0:T(8,128)(2,1)S(1)}) custom-call(bf16[16,8,2,8,512]{4,3,2,1,0:T(8,128)(2,1)S(1)} %copy-done.1, f32[4,2,8,512]{3,2,1,0:T(8,128)S(1)} %copy-done.2, f32[3,4,192,128]{3,2,1,0:T(8,128)S(1)} %get-tuple-element.23.refs_2_, ...), custom_call_target="tpu_custom_call" | custom-call | tf_op jit(solution)/shard_map/sweep1/pallas_call | solution.py:322
  68.2 0.6 collective-permute-start.7
  68.8 4.0 %collective-permute-done.7 = bf16[4,2,8,512]{3,2,1,0:T(8,128)(2,1)S(1)} collective-permute-done((bf16[4,2,8,512]{3,2,1,0:T(8,128)(2,1)S(1)}, bf16[4,2,8,512]{3,2,1,0:T(8,128)(2,1)S(1)}, u32[]{:S(2)}, u32[]{:S(2)}) %collective-permute-start.7) | collective-permute-done | bytes 65568 | tf_op jit(solution)/shard_map/ppermute | solution.py:341
  72.8 0.1 curv1.1
  72.9 9.3 %all_to_all.11.got = f32[32,1,256]{2,1,0:T(1,128)S(1)} all-to-all(f32[32,1,256]{2,1,0:T(1,128)S(1)} %get-tuple-element.36), channel_id=1, replica_groups=mesh['mem'=2,'row'=16] {'mem','row'}, dimensions={0} | all-to-all | bytes 65536 | tf_op jit(solution)/shard_map/all_to_all | solution.py:388
  82.2 1.2 %final.1 = (f32[16,2,8,512]{3,2,1,0:T(8,128)}, f32[4,2,8,512]{3,2,1,0:T(8,128)}, f32[4,2,8,512]{3,2,1,0:T(8,128)}) custom-call(f32[32,1,256]{2,1,0:T(1,128)S(1)} %all_to_all.11.got, f32[1,128]{1,0:T(1,128)S(1)} %get-tuple-element.30.refs_4_.refs_6_.step, f32[5,4,128,128]{3,2,1,0:T(8,128)S(1)} %get-tuple-element.24.refs_3_.grad0, ...), custom_call_target="tpu_custom_call" | custom-call | tf_op jit(solution)/shard_map/final/pallas_call | solution.py:322
Async XLA Ops:
  0.6 7.6 %collective-permute-start = (f32[4,2,8,512]{3,2,1,0:T(8,128)}, f32[4,2,8,512]{3,2,1,0:T(8,128)S(1)}, u32[]{:S(2)}, u32[]{:S(2)}) collective-permute-start(f32[4,2,8,512]{3,2,1,0:T(8,128)} %refs_3_.7), channel_id=1, source_target_pairs={{0,16},{16,0},{1,17},{17,1},{2,18},{18,2},{3,19},{19,3},{4,20},{20... | collective-permute-start | bytes 393224 | tf_op jit(solution)/shard_map/ppermute | solution.py:341
  3.7 6.5 %collective-permute-start.1 = (s32[4,2,8,512]{3,2,1,0:T(8,128)}, s32[4,2,8,512]{3,2,1,0:T(8,128)S(1)}, u32[]{:S(2)}, u32[]{:S(2)}) collective-permute-start(s32[4,2,8,512]{3,2,1,0:T(8,128)} %refs_4_.5), channel_id=1, source_target_pairs={{0,16},{16,0},{1,17},{17,1},{2,18},{18,2},{3,19},{19,3},{4,20},{20... | collective-permute-start | bytes 393224 | tf_op jit(solution)/shard_map/ppermute | solution.py:341
  10.2 1.6 %copy-start = (bf16[16,8,2,8,512]{4,3,2,1,0:T(8,128)(2,1)S(1)}, bf16[16,8,2,8,512]{4,3,2,1,0:T(8,128)(2,1)}, u32[]{:S(2)}) copy-start(bf16[16,8,2,8,512]{4,3,2,1,0:T(8,128)(2,1)} %refs_0_.7) | copy-start | bytes 6291460
  11.8 0.9 %copy-start.2 = (f32[4,2,8,512]{3,2,1,0:T(8,128)S(1)}, f32[4,2,8,512]{3,2,1,0:T(8,128)}, u32[]{:S(2)}) copy-start(f32[4,2,8,512]{3,2,1,0:T(8,128)} %refs_1_.7) | copy-start | bytes 393220
  12.7 0.9 %copy-start.3 = (f32[4,2,8,512]{3,2,1,0:T(8,128)S(1)}, f32[4,2,8,512]{3,2,1,0:T(8,128)}, u32[]{:S(2)}) copy-start(f32[4,2,8,512]{3,2,1,0:T(8,128)} %refs_3_.7) | copy-start | bytes 393220
  13.6 0.9 %copy-start.5 = (s32[4,2,8,512]{3,2,1,0:T(8,128)S(1)}, s32[4,2,8,512]{3,2,1,0:T(8,128)}, u32[]{:S(2)}) copy-start(s32[4,2,8,512]{3,2,1,0:T(8,128)} %refs_4_.5) | copy-start | bytes 393220
  14.5 0.8 copy-start.7
  15.9 8.2 %collective-permute-start.3 = (bf16[21,2,8,512]{3,2,1,0:T(8,128)(2,1)S(1)}, bf16[21,2,8,512]{3,2,1,0:T(8,128)(2,1)S(1)}, u32[]{:S(2)}, u32[]{:S(2)}) collective-permute-start(bf16[21,2,8,512]{3,2,1,0:T(8,128)(2,1)S(1)} %get-tuple-element.22), channel_id=1, source_target_pairs={{0,15},{1,0},{2,1},{3,2},{4,3},{5,4},{6,5},{7,6},{8,7},{9,8},{10,9... | collective-permute-start | bytes 1032200 | tf_op jit(solution)/shard_map/ppermute | solution.py:344
  19.2 9.4 %collective-permute-start.2 = (bf16[21,2,8,512]{3,2,1,0:T(8,128)(2,1)S(1)}, bf16[21,2,8,512]{3,2,1,0:T(8,128)(2,1)S(1)}, u32[]{:S(2)}, u32[]{:S(2)}) collective-permute-start(bf16[21,2,8,512]{3,2,1,0:T(8,128)(2,1)S(1)} %get-tuple-element.22), channel_id=1, source_target_pairs={{0,1},{1,2},{2,3},{3,4},{4,5},{5,6},{6,7},{7,8},{8,9},{9,10},{10,1... | collective-permute-start | bytes 1032200 | tf_op jit(solution)/shard_map/ppermute | solution.py:344
  28.6 11.6 %copy-start.4 = (f32[4,2,8,512]{3,2,1,0:T(8,128)S(1)}, f32[4,2,8,512]{3,2,1,0:T(8,128)}, u32[]{:S(2)}) copy-start(f32[4,2,8,512]{3,2,1,0:T(8,128)} %refs_3_.7) | copy-start | bytes 393220
  28.6 11.6 %copy-start.6 = (s32[4,2,8,512]{3,2,1,0:T(8,128)S(1)}, s32[4,2,8,512]{3,2,1,0:T(8,128)}, u32[]{:S(2)}) copy-start(s32[4,2,8,512]{3,2,1,0:T(8,128)} %refs_4_.5) | copy-start | bytes 393220
  28.6 22.6 %copy-start.1 = (bf16[16,8,2,8,512]{4,3,2,1,0:T(8,128)(2,1)S(1)}, bf16[16,8,2,8,512]{4,3,2,1,0:T(8,128)(2,1)}, u32[]{:S(2)}) copy-start(bf16[16,8,2,8,512]{4,3,2,1,0:T(8,128)(2,1)} %refs_0_.7) | copy-start | bytes 6291460
  35.2 5.0 %collective-permute-start.4 = (bf16[8,2,8,512]{3,2,1,0:T(8,128)(2,1)S(1)}, bf16[8,2,8,512]{3,2,1,0:T(8,128)(2,1)S(1)}, u32[]{:S(2)}, u32[]{:S(2)}) collective-permute-start(bf16[8,2,8,512]{3,2,1,0:T(8,128)(2,1)S(1)} %get-tuple-element.26), channel_id=1, source_target_pairs={{0,16},{16,0},{1,17},{17,1},{2,18},{18,2},{3,19},{19,3},{4,20},{20... | collective-permute-start | bytes 393224 | tf_op jit(solution)/shard_map/ppermute | solution.py:341
  51.9 4.9 %collective-permute-start.6 = (bf16[20,2,8,512]{3,2,1,0:T(8,128)(2,1)S(1)}, bf16[20,2,8,512]{3,2,1,0:T(8,128)(2,1)S(1)}, u32[]{:S(2)}, u32[]{:S(2)}) collective-permute-start(bf16[20,2,8,512]{3,2,1,0:T(8,128)(2,1)S(1)} %get-tuple-element.32), channel_id=1, source_target_pairs={{0,15},{1,0},{2,1},{3,2},{4,3},{5,4},{6,5},{7,6},{8,7},{9,8},{10,9... | collective-permute-start | bytes 983048 | tf_op jit(solution)/shard_map/ppermute | solution.py:344
  52.3 9.3 %collective-permute-start.5 = (bf16[20,2,8,512]{3,2,1,0:T(8,128)(2,1)S(1)}, bf16[20,2,8,512]{3,2,1,0:T(8,128)(2,1)S(1)}, u32[]{:S(2)}, u32[]{:S(2)}) collective-permute-start(bf16[20,2,8,512]{3,2,1,0:T(8,128)(2,1)S(1)} %get-tuple-element.32), channel_id=1, source_target_pairs={{0,1},{1,2},{2,3},{3,4},{4,5},{5,6},{6,7},{7,8},{8,9},{9,10},{10,1... | collective-permute-start | bytes 983048 | tf_op jit(solution)/shard_map/ppermute | solution.py:344
  68.2 4.6 %collective-permute-start.7 = (bf16[4,2,8,512]{3,2,1,0:T(8,128)(2,1)S(1)}, bf16[4,2,8,512]{3,2,1,0:T(8,128)(2,1)S(1)}, u32[]{:S(2)}, u32[]{:S(2)}) collective-permute-start(bf16[4,2,8,512]{3,2,1,0:T(8,128)(2,1)S(1)} %bitcast.11), channel_id=1, source_target_pairs={{0,16},{16,0},{1,17},{17,1},{2,18},{18,2},{3,19},{19,3},{4,20},{20... | collective-permute-start | bytes 196616 | tf_op jit(solution)/shard_map/ppermute | solution.py:341

commit v3 on v2

v3 whole, which is shorter than its diff:
```python
import functools
import math

import jax
import jax.numpy as jnp
from jax import lax
from jax.experimental import pallas as pl
from jax.experimental.pallas import tpu as pltpu
from jax.sharding import PartitionSpec as P

SWEEPS = 4
ITERS = 2
SUB = 8
LANES = 128
kappa_table = (0.06, 0.11, 0.17, 0.23)
huber_levels = (1.0, 0.5, 1.0, 2.0)
f32 = jnp.float32
bf16 = jnp.bfloat16


def table(index, values):
    result = jnp.full(index.shape, values[3], f32)
    for entry in range(3):
        result = jnp.where(index == entry, f32(values[entry]), result)
    return result


class Plan:
    def __init__(self, members, static_scale, mem, row):
        self.K, self.V, self.L, self.R, self.X = members.shape
        self.S = static_scale.shape[0]
        self.mem, self.row = mem, row
        self.devices = mem * row
        self.KT = -(-self.K // SUB)
        self.ST = -(-(self.S * self.L) // SUB)
        self.PM = self.L * self.KT
        self.PN = self.PM + self.ST
        self.F = self.K + self.S
        self.C = self.X // LANES
        self.RE = self.R + 4 * SWEEPS
        self.RG = self.R + 2 * SWEEPS
        self.pads = self.K % SUB != 0 or (self.S * self.L) % SUB != 0
        self.ens = math.sqrt(0.7 / (self.K * mem - 1))
        self.stat = math.sqrt(0.3)

    def fields(self, level):
        own = [(k, level) for k in range(self.K)]
        return own + [(self.K + s, l) for s in range(self.S) for l in range(self.L)] if level == 0 else own

    def tiles(self, level):
        return self.KT + self.ST if level == 0 else self.KT

    def inner(self, field, level):
        if field < self.K:
            return field // SUB, field % SUB
        at = (field - self.K) * self.L + level
        return self.KT + at // SUB, at % SUB

    def slot(self, field, level):
        if field < self.K:
            return level * self.KT + field // SUB, field % SUB
        at = (field - self.K) * self.L + level
        return self.PM + at // SUB, at % SUB


def strided(start, count):
    return pl.ds(start, count, stride=SUB)


def scatter(ref, tile, where, value):
    for c in range(value.shape[1] // LANES):
        ref[tile, c, where, :] = value[:, c * LANES : (c + 1) * LANES]


def gather(ref, tile, where):
    return jnp.concatenate([ref[tile, c, where, :] for c in range(ref.shape[1])], axis=1)


def load_kernel(p, obs, cls, obs_out, cls_out, sent, code, sems):
    pairs = ((obs, obs_out), (cls, cls_out))
    copies = [pltpu.make_async_copy(src, dst, sems.at[i]) for i, (src, dst) in enumerate(pairs)]
    for copy in copies:
        copy.start()
    for copy in copies:
        copy.wait()
    for s in range(p.S):
        for l in range(p.L):
            index = cls_out[s, l]
            threshold = table(index, huber_levels)
            clipped = jnp.where(index > 0, jnp.clip(-obs_out[s, l], -threshold, threshold), 0.0)
            sent[s, l] = clipped.astype(bf16)
            code[s, l] = index.astype(f32).astype(bf16)


def fetch_kernel(p, members, static_scale, scale_index, after, members_out, static_out, scale_out, sems):
    pairs = ((members, members_out), (static_scale, static_out), (scale_index, scale_out))
    copies = [pltpu.make_async_copy(src, dst, sems.at[i]) for i, (src, dst) in enumerate(pairs)]
    for copy in copies:
        copy.start()
    for copy in copies:
        copy.wait()


def back_kernel(p, first, *refs):
    if first:
        members, static_scale, scale_index, own, others, back, *msgs, sent = refs
    else:
        members, static_scale, obs, cls, obs_in, code_in, image, got, back, step_out, *msgs, sent = refs
    me = lax.axis_index("mem")
    if p.pads:
        back[...] = jnp.zeros(back.shape, f32)
    if not first:
        total = jnp.sum(got[...], axis=0)
        norm = jnp.sum(total[:, :LANES], axis=1, keepdims=True)
        curvature = jnp.sum(total[:, LANES:], axis=1, keepdims=True)
        step = norm / (norm + curvature)
        step_out[...] = jnp.broadcast_to(step, step_out.shape)
    for shift in range(p.mem):
        base = lax.rem(me + (p.mem - shift), p.mem) * p.S
        for s in range(p.S):
            for l in range(p.L):
                if first:
                    rounded = (own[s, l] if shift == 0 else others[shift - 1, s, l]).astype(f32)
                else:
                    if shift == 0:
                        seen, index = obs[s, l], cls[s, l]
                    else:
                        seen, index = obs_in[shift - 1, s, l], code_in[shift - 1, s, l].astype(f32)
                    threshold = table(index, huber_levels)
                    misfit = -(step * image[base + s, l]) - seen
                    clipped = jnp.where(index > 0, jnp.clip(misfit, -threshold, threshold), 0.0)
                    rounded = clipped.astype(bf16).astype(f32)
                sent[base + s, l] = rounded
                if shift == 0:
                    tile, lane = p.slot(p.K + s, l)
                    value = p.stat * static_scale[s, l] * rounded
                    scatter(back, tile, strided(lane, p.R), value)
                    msgs[0][p.K + s * p.L + l] = value.astype(bf16)
    if first:
        for l in range(p.L):
            msgs[0][p.K + p.S * p.L + l] = scale_index[l].astype(f32).astype(bf16)
    for l in range(p.L):
        for k in range(p.K):
            value = members[k, 0, l].astype(f32) * sent[0, l]
            for v in range(1, p.V):
                value = value + members[k, v, l].astype(f32) * sent[v, l]
            value = p.ens * value
            tile, lane = p.slot(k, l)
            scatter(back, tile, strided(lane, p.R), value)
            msgs[l][k] = value.astype(bf16)


def sideways(u, first_lane, last_lane):
    right = [pltpu.roll(part, 1, 1) for part in u]
    left = [pltpu.roll(part, LANES - 1, 1) for part in u]
    zero = jnp.zeros_like(u[0])
    before, after = [zero] + right[:-1], left[1:] + [zero]
    return [
        jnp.where(first_lane, before[i], right[i]) + jnp.where(last_lane, after[i], left[i])
        for i in range(len(u))
    ]


def stencil(above, here, below, side):
    across = side(here)
    return [(above[c] + below[c]) + across[c] - 4.0 * here[c] for c in range(len(here))]


def sweep_kernel(p, first, level, *refs):
    refs = list(refs)
    members, static_scale, back, low, high = refs[:5]
    refs = refs[5:]
    if first and level == 0:
        scale_index, *refs = refs
    else:
        kap, *refs = refs
    if level:
        rest, *refs = refs
    if not first:
        before, step, *refs = refs
    grad, norm, part, ship, *refs = refs
    if level == 0 and p.L > 1:
        rest, *refs = refs
    if first and level == 0:
        kap, *refs = refs
    lo, hi, a, b, out = refs
    me, at = lax.axis_index("mem"), lax.axis_index("row")
    low_ok = jnp.where(at > 0, 1.0, 0.0).astype(f32)
    high_ok = jnp.where(at < p.row - 1, 1.0, 0.0).astype(f32)
    R, RE, RG, W = p.R, p.RE, p.RG, SWEEPS
    H = 2 * W
    fields = p.fields(level)
    count = p.tiles(level)
    for ref, dst in ((low, lo), (high, hi)):
        if p.pads:
            dst[...] = jnp.zeros(dst.shape, f32)
        skip = R - H if ref is low else 0
        for i, (field, l) in enumerate(fields):
            tile, lane = p.inner(field, l)
            scatter(dst, tile, strided(lane, H), ref[i].astype(f32)[skip : skip + H])
    if first and level == 0:
        for l in range(p.L):
            pieces = (
                (table(low[len(fields) + l].astype(f32)[R - H :], kappa_table) * low_ok, 0),
                (table(scale_index[l].astype(f32), kappa_table), H),
                (table(high[len(fields) + l].astype(f32)[:H], kappa_table) * high_ok, H + R),
            )
            for value, offset in pieces:
                for r in range(value.shape[0]):
                    scatter(kap, l, pl.ds((offset + r) * SUB, SUB), jnp.broadcast_to(value[r : r + 1], (SUB, p.X)))
                for j in range(p.ST * SUB):
                    if (j % p.L) == l:
                        scatter(kap, p.L + j // SUB, strided(offset * SUB + j % SUB, value.shape[0]), value)
    lane = lax.broadcasted_iota(jnp.int32, (SUB, LANES), 1)
    first_lane, last_lane = lane == 0, lane == LANES - 1
    side = functools.partial(sideways, first_lane=first_lane, last_lane=last_lane)
    cols = range(p.C)

    def tiles(ref, r, *lead):
        return [ref[(*lead, c, pl.ds(r * SUB, SUB), slice(None))] for c in cols]

    def keep(value, ref, r, *lead):
        for c in cols:
            ref[(*lead, c, pl.ds(r * SUB, SUB), slice(None))] = value[c]

    if not first:
        step_tile = jnp.broadcast_to(step[0:1, 0:1], (SUB, LANES))

    def problem(t, total):
        if level == 0:
            which = jnp.where(t < p.KT, 0, t - p.KT + p.L)
            whole = jnp.where(t < p.KT, t, t - p.KT + p.PM)
        else:
            which, whole = level, t + level * p.KT
        source = None
        for sweep in range(W):
            target = (a, b)[sweep % 2]
            held = []
            for r in range(sweep, RE - sweep):
                if sweep:
                    u = tiles(source, r)
                elif r < H:
                    u = tiles(lo, r, t)
                elif r < H + R:
                    u = tiles(back, r - H, whole)
                else:
                    u = tiles(hi, r - H - R, t)
                factor = tiles(kap, r, which)
                w = [factor[c] * u[c] for c in cols]
                held = (held + [(u, w)])[-3:]
                if len(held) < 3:
                    continue
                (_, w0), (u1, w1), (_, w2) = held
                change = stencil(w0, w1, w2, side)
                value = [u1[c] + change[c] for c in cols]
                if sweep < W - 1:
                    keep(value, target, r - 1)
                    continue
                if not first:
                    earlier = tiles(before, r - 1 - W, t)
                    value = [value[c] - step_tile * earlier[c] for c in cols]
                if r - 1 < H:
                    value = [one * low_ok for one in value]
                elif r - 1 >= H + R:
                    value = [one * high_ok for one in value]
                else:
                    for one in value:
                        total = total + one * one
                keep(value, grad, r - 1 - W, t)
            source = target
        for sweep in range(W):
            target = (a, b)[sweep % 2]
            held = []
            for r in range(W + sweep, RE - W - sweep):
                u = tiles(source, r) if sweep else tiles(grad, r - W, t)
                held = (held + [u])[-3:]
                if len(held) < 3:
                    continue
                change = stencil(*held, side)
                factor = tiles(kap, r - 1, which)
                value = [held[1][c] + factor[c] * change[c] for c in cols]
                if sweep < W - 1:
                    keep(value, target, r - 1)
                else:
                    keep(value, out, r - 1 - H, t)
            source = target
        return total

    total = lax.fori_loop(0, count, problem, jnp.zeros((SUB, LANES), f32))
    norm[...] = jnp.sum(total, axis=0, keepdims=True)
    sums = [None] * p.V
    for k in range(p.K):
        tile, j = p.inner(k, level)
        spread = gather(out, tile, strided(j, R)).astype(bf16).astype(f32)
        for v in range(p.V):
            term = members[k, v, level].astype(f32) * spread
            sums[v] = term if k == 0 else sums[v] + term
    for v in range(p.V):
        part[v] = p.ens * sums[v]
    for s in range(p.S):
        own = me * p.S + s
        if level:
            part[own] = part[own] + rest[level - 1, s]
            continue
        for l in range(p.L):
            tile, j = p.inner(p.K + s, l)
            value = p.stat * static_scale[s, l] * gather(out, tile, strided(j, R))
            if l:
                rest[l - 1, s] = value
            else:
                part[own] = part[own] + value
    if first:
        ship[...] = part[...].astype(bf16)
        return
    for shift in range(1, p.mem):
        base = lax.rem(me + shift, p.mem) * p.S
        for s in range(p.S):
            ship[shift - 1, s] = part[base + s].astype(bf16)


def curvature_kernel(p, first, *refs):
    parts, gots, norms, refs = refs[: p.L], refs[p.L : 2 * p.L], refs[2 * p.L : 3 * p.L], refs[3 * p.L :]
    if first:
        obs, cls, image, send = refs
    else:
        obs, cls, image_before, step, image, send = refs
    me = lax.axis_index("mem")
    total = jnp.zeros((p.R, p.X), f32)
    for l in range(p.L):
        if first:
            for v in range(p.V):
                value = parts[l][v]
                for other in range(p.mem - 1):
                    value = value + gots[l][other, v].astype(f32)
                image[v, l] = value
        for s in range(p.S):
            own = me * p.S + s
            if first:
                value = image[own, l]
                misfit = -obs[s, l]
            else:
                value = parts[l][own]
                for other in range(p.mem - 1):
                    value = value + gots[l][other, s].astype(f32)
                image[s, l] = value
                misfit = -(step[0:1, 0:1] * image_before[own, l]) - obs[s, l]
            index = cls[s, l]
            threshold = table(index, huber_levels)
            weight = jnp.where(index > 0, threshold / jnp.maximum(jnp.abs(misfit), threshold), 0.0)
            total = total + weight * value * value
    total = jnp.sum(total, axis=0, keepdims=True)
    total = sum(total[:, i * LANES : (i + 1) * LANES] for i in range(p.X // LANES))
    norm = sum(one[...] for one in norms)
    send[...] = jnp.broadcast_to(jnp.concatenate([norm, total], axis=1)[None], send.shape)


def final_kernel(p, got, step, image0, image1, *refs):
    before, after, outs = refs[: p.L], refs[p.L : 2 * p.L], refs[2 * p.L :]
    control, static_control, increment = outs
    me = lax.axis_index("mem")
    total = jnp.sum(got[...], axis=0)
    norm = jnp.sum(total[:, :LANES], axis=1, keepdims=True)
    curvature = jnp.sum(total[:, LANES:], axis=1, keepdims=True)
    second = norm / (norm + curvature)
    first = step[0:1, 0:1]
    for level in range(p.L):
        for field, l in p.fields(level):
            tile, lane = p.inner(field, l)
            where = strided(SWEEPS * SUB + lane, p.R)
            value = -(first * gather(before[level], tile, where)) - second * gather(after[level], tile, where)
            if field < p.K:
                control[field, l] = value
            else:
                static_control[field - p.K, l] = value
    for s in range(p.S):
        for l in range(p.L):
            increment[s, l] = -(first * image0[me * p.S + s, l]) - second * image1[s, l]


def call(kernel, p, outs, scratch, name, far=0, cost=0):
    vmem = pl.BlockSpec(memory_space=pltpu.VMEM)
    anywhere = pl.BlockSpec(memory_space=pl.ANY)

    def run(*args):
        return pl.pallas_call(
            kernel,
            out_shape=tuple(jax.ShapeDtypeStruct(shape, dtype) for shape, dtype in outs),
            in_specs=[anywhere] * far + [vmem] * (len(args) - far),
            out_specs=tuple(vmem for _ in outs),
            scratch_shapes=scratch,
            compiler_params=pltpu.CompilerParams(vmem_limit_bytes=16 << 20),
            cost_estimate=pl.CostEstimate(flops=cost, bytes_accessed=cost, transcendentals=0),
            name=name,
        )(*args)

    return run


def local(members, static_scale, observed, huber_class, scale_index):
    p = Plan(members, static_scale, lax.axis_size("mem"), lax.axis_size("row"))
    K, V, L, R, X, S, C = p.K, p.V, p.L, p.R, p.X, p.S, p.C
    assert R >= 2 * SWEEPS

    def round_mem(block, shift):
        return lax.ppermute(block, "mem", [(i, (i + shift) % p.mem) for i in range(p.mem)])

    def round_row(block, shift):
        return lax.ppermute(block, "row", [(i, (i + shift) % p.row) for i in range(p.row)])

    vmem = lambda shape: pltpu.VMEM(shape, f32)
    part = functools.partial
    shifts = range(1, p.mem)
    own_shape = (S, L, R, X)
    full_shape = (V, L, R, X)
    back_shape = (p.PN, C, R * SUB, LANES)
    send_shape = ((p.devices, 1, 2 * LANES), f32)
    line = ((1, LANES), f32)

    obs, cls, own, code = call(
        part(load_kernel, p), p,
        [(own_shape, f32), (own_shape, jnp.int32), (own_shape, bf16), (own_shape, bf16)],
        [pltpu.SemaphoreType.DMA((2,))], "load", far=2,
    )(observed, huber_class)
    others = jnp.stack([round_mem(own, shift) for shift in shifts])
    members, static_scale, scale_index = call(
        part(fetch_kernel, p), p,
        [(x.shape, x.dtype) for x in (members, static_scale, scale_index)],
        [pltpu.SemaphoreType.DMA((3,))], "fetch", far=3, cost=4 << 20,
    )(members, static_scale, scale_index, own)
    obs_in = jnp.stack([round_mem(obs, shift) for shift in shifts])
    code_in = jnp.stack([round_mem(code, shift) for shift in shifts])

    grads, image, step, kap, sums = [], None, None, None, None
    for turn in range(ITERS):
        first = turn == 0
        sizes = [len(p.fields(level)) for level in range(L)]
        if first:
            sizes[0] += L
        msg_shapes = [((size, R, X), bf16) for size in sizes]
        if first:
            back, *msgs = call(
                part(back_kernel, p, True), p, [(back_shape, f32)] + msg_shapes, [vmem(full_shape)], "back0",
            )(members, static_scale, scale_index, own, others)
        else:
            back, step, *msgs = call(
                part(back_kernel, p, False), p, [(back_shape, f32), line] + msg_shapes, [vmem(full_shape)], "back1",
            )(members, static_scale, obs, cls, obs_in, code_in, image, sums)
        halos = [(round_row(msg, 1), round_row(msg, p.row - 1)) for msg in msgs]
        grad, norms, partial_images, gots, rest = [], [], [], [], None
        for level in range(L):
            count = p.tiles(level)
            args = [members, static_scale, back, *halos[level]]
            args += [scale_index] if first and level == 0 else [kap]
            args += [rest] if level else []
            args += [] if first else [grads[0][level], step]
            ship_shape = (V, R, X) if first else (p.mem - 1, S, R, X)
            outs = [((count, C, p.RG * SUB, LANES), f32), line, ((V, R, X), f32), (ship_shape, bf16)]
            if level == 0 and L > 1:
                outs.append(((L - 1, S, R, X), f32))
            if first and level == 0:
                outs.append(((L + p.ST, C, p.RE * SUB, LANES), f32))
            halo = vmem((count, C, 2 * SWEEPS * SUB, LANES))
            work = [halo, halo, vmem((C, p.RE * SUB, LANES)), vmem((C, p.RE * SUB, LANES))]
            g, norm, partial_image, ship, *more = call(
                part(sweep_kernel, p, first, level), p, outs, work + [vmem((count, C, R * SUB, LANES))],
                f"sweep{turn}_{level}", cost=8 << 20,
            )(*args)
            if level == 0 and L > 1:
                rest, *more = more
            if first and level == 0:
                kap = more[0]
            grad.append(g)
            norms.append(norm)
            partial_images.append(partial_image)
            gots.append(jnp.stack([round_mem(ship if first else ship[shift - 1], shift) for shift in shifts]))
        grads.append(grad)
        if first:
            image, send = call(
                part(curvature_kernel, p, True), p, [(full_shape, f32), send_shape], [], "curv0",
            )(*partial_images, *gots, *norms, obs, cls)
        else:
            last, send = call(
                part(curvature_kernel, p, False), p, [(own_shape, f32), send_shape], [], "curv1",
            )(*partial_images, *gots, *norms, obs, cls, image, step)
        sums = lax.all_to_all(send, ("mem", "row"), 0, 0)
    return call(
        part(final_kernel, p), p,
        [((K, L, R, X), f32), (own_shape, f32), (own_shape, f32)], [], "final",
    )(sums, step, image, last, *grads[0], *grads[1])


def solution(mesh):
    placed = (
        P("mem", None, None, "row", None),
        P("mem", None, "row", None),
        P("mem", None, "row", None),
        P("mem", None, "row", None),
        P(None, "row", None),
    )
    return jax.shard_map(
        local,
        mesh=mesh,
        in_specs=placed,
        out_specs=(
            P("mem", None, "row", None),
            P("mem", None, "row", None),
            P("mem", None, "row", None),
        ),
        check_vma=False,
    )
```

time: 83.7 us -> 80.4 us (0.961)
  starting transfers between devices: 9.29 us -> 24.6 us
  waiting for transfers between devices: 32.3 us -> 18.4 us
  blocking collectives: 20.2 us -> 10.4 us
  local copies, waits for them, and re-layouts: 5.07 us -> 8.3 us
  Pallas kernels: 15.9 us -> 17.4 us
    ppermute x4 -> x8, waiting for transfers between devices: 18.4 us -> 6.47 us  [round_row(): lax.ppermute(block, 'row', [(i, (i + shift) % p.row) for i in range(p.row)])]
    all_to_all x2 -> x1, blocking collectives: 20.2 us -> 10.4 us  [local(): sums = lax.all_to_all(send, ('mem', 'row'), 0, 0)]
    ppermute x4 -> x8, starting transfers between devices: 3.95 us -> 13.1 us  [round_row(): lax.ppermute(block, 'row', [(i, (i + shift) % p.row) for i in range(p.row)])]
    ppermute x4 -> x7, waiting for transfers between devices: 13.9 us -> 4.92 us  [round_mem(): lax.ppermute(block, 'mem', [(i, (i + shift) % p.mem) for i in range(p.mem)])]
    all_to_all x0 -> x1, waiting for transfers between devices: none -> 7.06 us  [local(): sums = lax.all_to_all(send, ('mem', 'row'), 0, 0)]
    all_to_all x0 -> x1, starting transfers between devices: none -> 3.27 us  [local(): sums = lax.all_to_all(send, ('mem', 'row'), 0, 0)]
    unnamed x16 -> x30, local copies, waits for them, and re-layouts: 5.07 us -> 8.3 us
    ppermute x4 -> x7, starting transfers between devices: 5.34 us -> 8.26 us  [round_mem(): lax.ppermute(block, 'mem', [(i, (i + shift) % p.mem) for i in range(p.mem)])]
  transfers between devices with their start and end apart: 8 -> 16, of which waited for: 8 -> 7; matrix products, arithmetic and copies ran while one was open for 0% -> 0% of each run, Pallas kernels for 0% -> 13%
where the time goes in v3:
time: 80.4 us; the launch traced here: 80 us
  starting transfers between devices  24.6 us (31%)
  waiting for transfers between devices  18.4 us (23%)
  Pallas kernels  17.4 us (22%)
  blocking collectives  10.4 us (13%)
  local copies, waits for them, and re-layouts  8.3 us (10%)
  between operations  0.85 us (1%)
    pallas_call x11, Pallas kernels, run(): pl.pallas_call(kernel, out_shape=tuple((jax.ShapeDtypeStruct(shape, dtype...  17.4 us
    ppermute x8, starting transfers between devices, round_row(): lax.ppermute(block, 'row', [(i, (i + shift) % p.row) for i in range(p.row)])  13.1 us
    all_to_all x1, blocking collectives, local(): sums = lax.all_to_all(send, ('mem', 'row'), 0, 0)  10.4 us
    unnamed x30, local copies, waits for them, and re-layouts  8.3 us
    ppermute x7, starting transfers between devices, round_mem(): lax.ppermute(block, 'mem', [(i, (i + shift) % p.mem) for i in range(p.mem)])  8.26 us
    all_to_all x1, waiting for transfers between devices, local(): sums = lax.all_to_all(send, ('mem', 'row'), 0, 0)  7.06 us
    ppermute x8, waiting for transfers between devices, round_row(): lax.ppermute(block, 'row', [(i, (i + shift) % p.row) for i in range(p.row)])  6.47 us
    ppermute x7, waiting for transfers between devices, round_mem(): lax.ppermute(block, 'mem', [(i, (i + shift) % p.mem) for i in range(p.mem)])  4.92 us
  transfers between devices with their start and end apart: 16, of which 7 were waited for; matrix products, arithmetic and copies ran while one was open for 0% of the time, Pallas kernels for 13%

profile of v3, /device:TPU:0, one launch (start us, length us, event | category | flops | bytes accessed | tf_op | source)
XLA Modules:
  0.0 80.0 jit_solution(9456831688206170336)
XLA Ops:
  0.6 0.9 %copy-done.11 = f32[4,2,8,512]{3,2,1,0:T(8,128)S(1)} copy-done((f32[4,2,8,512]{3,2,1,0:T(8,128)S(1)}, f32[4,2,8,512]{3,2,1,0:T(8,128)}, u32[]{:S(2)}) %copy-start.11) | copy-done | bytes 131096
  1.5 0.9 %copy-done.12 = s32[4,2,8,512]{3,2,1,0:T(8,128)S(1)} copy-done((s32[4,2,8,512]{3,2,1,0:T(8,128)S(1)}, s32[4,2,8,512]{3,2,1,0:T(8,128)}, u32[]{:S(2)}) %copy-start.12) | copy-done | bytes 131096
  2.4 1.0 %load.1 = (f32[4,2,8,512]{3,2,1,0:T(8,128)S(1)}, s32[4,2,8,512]{3,2,1,0:T(8,128)S(1)}, bf16[4,2,8,512]{3,2,1,0:T(8,128)(2,1)S(1)}, bf16[4,2,8,512]{3,2,1,0:T(8,128)(2,1)}) custom-call(f32[4,2,8,512]{3,2,1,0:T(8,128)S(1)} %copy-done.11, s32[4,2,8,512]{3,2,1,0:T(8,128)S(1)} %copy-done.12), custom_call_target="tpu_custom_call" | custom-call | tf_op jit(solution)/shard_map/load/pallas_call | solution.py:385
  3.4 0.0 copy-start.8
  3.4 3.1 %collective-permute-start.2 = (bf16[4,2,8,512]{3,2,1,0:T(8,128)(2,1)S(1)}, bf16[4,2,8,512]{3,2,1,0:T(8,128)(2,1)S(1)}, u32[]{:S(2)}, u32[]{:S(2)}) collective-permute-start(bf16[4,2,8,512]{3,2,1,0:T(8,128)(2,1)S(1)} %get-tuple-element.40.after.refs_3_), channel_id=1, source_target_pairs={{0,16},{16,0},{1,17},{17,1},{2,18},{18,2},{3,19},{19,3},{4,20},{20... | collective-permute-start | bytes 196616 | tf_op jit(solution)/shard_map/ppermute | solution.py:405
  6.5 1.6 %copy-done.7 = bf16[16,8,2,8,512]{4,3,2,1,0:T(8,128)(2,1)S(1)} copy-done((bf16[16,8,2,8,512]{4,3,2,1,0:T(8,128)(2,1)S(1)}, bf16[16,8,2,8,512]{4,3,2,1,0:T(8,128)(2,1)}, u32[]{:S(2)}) %copy-start.7) | copy-done | bytes 2097176
  8.1 0.9 %copy-done.10 = f32[4,2,8,512]{3,2,1,0:T(8,128)S(1)} copy-done((f32[4,2,8,512]{3,2,1,0:T(8,128)S(1)}, f32[4,2,8,512]{3,2,1,0:T(8,128)}, u32[]{:S(2)}) %copy-start.10) | copy-done | bytes 131096
  9.0 0.8 copy-done.13
  9.7 0.4 fetch.1
  10.1 0.0 collective-permute-done.2
  10.1 0.5 back0.1
  10.6 3.7 %collective-permute-start.4 = (bf16[26,8,512]{2,1,0:T(8,128)(2,1)S(1)}, bf16[26,8,512]{2,1,0:T(8,128)(2,1)S(1)}, u32[]{:S(2)}, u32[]{:S(2)}) collective-permute-start(bf16[26,8,512]{2,1,0:T(8,128)(2,1)S(1)} %get-tuple-element.48), channel_id=1, source_target_pairs={{0,15},{1,0},{2,1},{3,2},{4,3},{5,4},{6,5},{7,6},{8,7},{9,8},{10,9... | collective-permute-start | bytes 638984 | tf_op jit(solution)/shard_map/ppermute | solution.py:408
  14.4 4.4 %collective-permute-start.6 = (bf16[16,8,512]{2,1,0:T(8,128)(2,1)S(1)}, bf16[16,8,512]{2,1,0:T(8,128)(2,1)S(1)}, u32[]{:S(2)}, u32[]{:S(2)}) collective-permute-start(bf16[16,8,512]{2,1,0:T(8,128)(2,1)S(1)} %get-tuple-element.50), channel_id=1, source_target_pairs={{0,15},{1,0},{2,1},{3,2},{4,3},{5,4},{6,5},{7,6},{8,7},{9,8},{10,9... | collective-permute-start | bytes 393224 | tf_op jit(solution)/shard_map/ppermute | solution.py:408
  18.8 0.5 collective-permute-start
  19.3 0.0 collective-permute-done.4.refs_4_
  19.3 3.0 %collective-permute-done.3.refs_3_ = bf16[26,8,512]{2,1,0:T(8,128)(2,1)S(1)} collective-permute-done((bf16[26,8,512]{2,1,0:T(8,128)(2,1)S(1)}, bf16[26,8,512]{2,1,0:T(8,128)(2,1)S(1)}, u32[]{:S(2)}, u32[]{:S(2)}) %collective-permute-start.3) | collective-permute-done | bytes 213024 | tf_op jit(solution)/shard_map/ppermute | solution.py:408
  22.3 3.8 %sweep0_0.1 = (f32[3,4,128,128]{3,2,1,0:T(8,128)S(1)}, f32[1,128]{1,0:T(1,128)S(1)}, f32[8,8,512]{2,1,0:T(8,128)S(1)}, bf16[8,8,512]{2,1,0:T(8,128)(2,1)S(1)}, f...) custom-call(bf16[16,8,2,8,512]{4,3,2,1,0:T(8,128)(2,1)S(1)} %get-tuple-element.41.refs_0_, ...), custom_call_target="tpu_custom_call" | custom-call | flops 8388608 | bytes 8388608 | tf_op jit(solution)/shard_map/sweep0_0/pallas_call | solution.py:385
  26.2 0.0 collective-permute-done.5.refs_3_
  26.2 2.5 %sweep0_1.1 = (f32[2,4,128,128]{3,2,1,0:T(8,128)S(1)}, f32[1,128]{1,0:T(1,128)S(1)}, f32[8,8,512]{2,1,0:T(8,128)S(1)}, bf16[8,8,512]{2,1,0:T(8,128)(2,1)S(1)}) custom-call(bf16[16,8,2,8,512]{4,3,2,1,0:T(8,128)(2,1)S(1)} %get-tuple-element.41.refs_0_, f32[4,2,8,512]{3,2,1,0:T(8,128)S(1)} %get-tuple-element.42.refs_1_, ...), custom_call_target="tpu_custom_call" | custom-call | flops 8388608 | bytes 8388608 | tf_op jit(solution)/shard_map/sweep0_1/pallas_call | solution.py:385
  28.7 0.0 copy-start.5
  28.8 0.6 collective-permute-start.8
  29.3 1.5 %collective-permute-start.7 = (bf16[8,8,512]{2,1,0:T(8,128)(2,1)S(1)}, bf16[8,8,512]{2,1,0:T(8,128)(2,1)S(1)}, u32[]{:S(2)}, u32[]{:S(2)}) collective-permute-start(bf16[8,8,512]{2,1,0:T(8,128)(2,1)S(1)} %get-tuple-element.54), channel_id=1, source_target_pairs={{0,16},{16,0},{1,17},{17,1},{2,18},{18,2},{3,19},{19,3},{4,20},{20... | collective-permute-start | bytes 196616 | tf_op jit(solution)/shard_map/ppermute | solution.py:405
  30.8 0.5 collective-permute-start.1
  31.4 1.7 %collective-permute-done.8 = bf16[8,8,512]{2,1,0:T(8,128)(2,1)S(1)} collective-permute-done((bf16[8,8,512]{2,1,0:T(8,128)(2,1)S(1)}, bf16[8,8,512]{2,1,0:T(8,128)(2,1)S(1)}, u32[]{:S(2)}, u32[]{:S(2)}) %collective-permute-start.8) | collective-permute-done | bytes 65568 | tf_op jit(solution)/shard_map/ppermute | solution.py:405
  33.1 0.7 collective-permute-done.7
  33.8 0.1 curv0.1
  33.9 0.7 copy-done.2
  34.6 0.6 copy-done.14
  35.2 3.3 %all-to-all-start = ((f32[32,1,256]{2,1,0:T(1,128)}), f32[32,1,256]{2,1,0:T(1,128)}, u32[]{:S(2)}, u32[]{:S(2)}) async-start(f32[32,1,256]{2,1,0:T(1,128)} %copy-done.14), calls=%async_computation | async-start | bytes 65536 | tf_op jit(solution)/shard_map/all_to_all | solution.py:485
  38.5 0.0 collective-permute-done.1
  38.5 0.0 collective-permute-done
  38.5 7.1 %all-to-all-done.refs_7_ = f32[32,1,256]{2,1,0:T(1,128)} async-done(((f32[32,1,256]{2,1,0:T(1,128)}), f32[32,1,256]{2,1,0:T(1,128)}, u32[]{:S(2)}, u32[]{:S(2)}) %all-to-all-start) | async-done | bytes 32800 | tf_op jit(solution)/shard_map/all_to_all | solution.py:485
  45.6 1.0 %copy-done.3 = f32[8,2,8,512]{3,2,1,0:T(8,128)S(1)} copy-done((f32[8,2,8,512]{3,2,1,0:T(8,128)S(1)}, f32[8,2,8,512]{3,2,1,0:T(8,128)}, u32[]{:S(2)}) %copy-start.3) | copy-done | bytes 262168
  46.6 0.9 %copy-done.9 = s32[4,2,8,512]{3,2,1,0:T(8,128)S(1)} copy-done((s32[4,2,8,512]{3,2,1,0:T(8,128)S(1)}, s32[4,2,8,512]{3,2,1,0:T(8,128)}, u32[]{:S(2)}) %copy-start.9) | copy-done | bytes 131096
  47.5 1.6 %back1.1 = (f32[5,4,64,128]{3,2,1,0:T(8,128)S(1)}, f32[1,128]{1,0:T(1,128)S(1)}, bf16[24,8,512]{2,1,0:T(8,128)(2,1)S(1)}, bf16[16,8,512]{2,1,0:T(8,128)(2,1)S(1)}) custom-call(bf16[16,8,2,8,512]{4,3,2,1,0:T(8,128)(2,1)S(1)} %get-tuple-element.41.refs_0_, f32[4,2,8,512]{3,2,1,0:T(8,128)S(1)} %get-tuple-element.42.refs_1_, ...), custom_call_target="tpu_custom_call" | custom-call | tf_op jit(solution)/shard_map/back1/pallas_call | solution.py:385
  49.1 0.4 collective-permute-start.10
  49.6 0.1 collective-permute-start.9
  49.7 4.3 %collective-permute-start.12 = (bf16[16,8,512]{2,1,0:T(8,128)(2,1)S(1)}, bf16[16,8,512]{2,1,0:T(8,128)(2,1)S(1)}, u32[]{:S(2)}, u32[]{:S(2)}) collective-permute-start(bf16[16,8,512]{2,1,0:T(8,128)(2,1)S(1)} %get-tuple-element.65), channel_id=1, source_target_pairs={{0,15},{1,0},{2,1},{3,2},{4,3},{5,4},{6,5},{7,6},{8,7},{9,8},{10,9... | collective-permute-start | bytes 393224 | tf_op jit(solution)/shard_map/ppermute | solution.py:408
  54.0 3.4 %collective-permute-done.9.refs_3_ = bf16[24,8,512]{2,1,0:T(8,128)(2,1)S(1)} collective-permute-done((bf16[24,8,512]{2,1,0:T(8,128)(2,1)S(1)}, bf16[24,8,512]{2,1,0:T(8,128)(2,1)S(1)}, u32[]{:S(2)}, u32[]{:S(2)}) %collective-permute-start.9) | collective-permute-done | bytes 196640 | tf_op jit(solution)/shard_map/ppermute | solution.py:408
  57.5 3.7 %sweep1_0.1 = (f32[3,4,128,128]{3,2,1,0:T(8,128)S(1)}, f32[1,128]{1,0:T(1,128)S(1)}, f32[8,8,512]{2,1,0:T(8,128)S(1)}, bf16[1,4,8,512]{3,2,1,0:T(8,128)(2,1)S(1)}, f32[1,4,8,512]{3,2,1,0:T(8,128)S(1)}) custom-call(bf16[16,8,2,8,512]{4,3,2,1,0:T(8,128)(2,1)S(1)} %get-tuple-element.41.refs_0_, f32[4,2,8,512]{3,2,1,0:T(8,128)S(1)} %get-tuple-element.42.refs_1_, ...), custom_call_target="tpu_custom_call" | custom-call | flops 8388608 | bytes 8388608 | tf_op jit(solution)/shard_map/sweep1_0/pallas_call | solution.py:385
  61.2 2.5 %sweep1_1.1 = (f32[2,4,128,128]{3,2,1,0:T(8,128)S(1)}, f32[1,128]{1,0:T(1,128)S(1)}, f32[8,8,512]{2,1,0:T(8,128)S(1)}, bf16[1,4,8,512]{3,2,1,0:T(8,128)(2,1)S(1)}) custom-call(bf16[16,8,2,8,512]{4,3,2,1,0:T(8,128)(2,1)S(1)} %get-tuple-element.41.refs_0_, f32[4,2,8,512]{3,2,1,0:T(8,128)S(1)} %get-tuple-element.42.refs_1_, ...), custom_call_target="tpu_custom_call" | custom-call | flops 8388608 | bytes 8388608 | tf_op jit(solution)/shard_map/sweep1_1/pallas_call | solution.py:385
  63.8 0.7 collective-permute-start.14
  64.4 1.4 %collective-permute-start.13 = (bf16[4,8,512]{2,1,0:T(8,128)(2,1)S(1)}, bf16[4,8,512]{2,1,0:T(8,128)(2,1)S(1)}, u32[]{:S(2)}, u32[]{:S(2)}) collective-permute-start(bf16[4,8,512]{2,1,0:T(8,128)(2,1)S(1)} %bitcast.14), channel_id=1, source_target_pairs={{0,16},{16,0},{1,17},{17,1},{2,18},{18,2},{3,19},{19,3},{4,20},{20... | collective-permute-start | bytes 98312 | tf_op jit(solution)/shard_map/ppermute | solution.py:405
  65.8 1.9 %collective-permute-done.14 = bf16[4,8,512]{2,1,0:T(8,128)(2,1)S(1)} collective-permute-done((bf16[4,8,512]{2,1,0:T(8,128)(2,1)S(1)}, bf16[4,8,512]{2,1,0:T(8,128)(2,1)S(1)}, u32[]{:S(2)}, u32[]{:S(2)}) %collective-permute-start.14) | collective-permute-done | bytes 32800 | tf_op jit(solution)/shard_map/ppermute | solution.py:405
  67.7 0.6 collective-permute-done.13
  68.3 0.1 curv1.1
  68.5 10.4 %all_to_all.10.got = f32[32,1,256]{2,1,0:T(1,128)S(1)} all-to-all(f32[32,1,256]{2,1,0:T(1,128)S(1)} %get-tuple-element.73), channel_id=1, replica_groups=mesh['mem'=2,'row'=16] {'mem','row'}, dimensions={0} | all-to-all | bytes 65536 | tf_op jit(solution)/shard_map/all_to_all | solution.py:485
  78.9 1.2 %final.1 = (f32[16,2,8,512]{3,2,1,0:T(8,128)}, f32[4,2,8,512]{3,2,1,0:T(8,128)}, f32[4,2,8,512]{3,2,1,0:T(8,128)}) custom-call(f32[32,1,256]{2,1,0:T(1,128)S(1)} %all_to_all.10.got, f32[1,128]{1,0:T(1,128)S(1)} %get-tuple-element.63.refs_7_.refs_8_.refs_9_.step, f32[8,2,8,512]{3,2,1,0:T(8,128)S(1)} %copy-done.4, ...), custom_call_target="tpu_custom_call" | custom-call | tf_op jit(solution)/shard_map/final/pallas_call | solution.py:385
  (26 shorter events, 0.1 us)
Async XLA Ops:
  0.6 0.9 %copy-start.11 = (f32[4,2,8,512]{3,2,1,0:T(8,128)S(1)}, f32[4,2,8,512]{3,2,1,0:T(8,128)}, u32[]{:S(2)}) copy-start(f32[4,2,8,512]{3,2,1,0:T(8,128)} %obs.1) | copy-start | bytes 393220
  1.5 0.9 %copy-start.12 = (s32[4,2,8,512]{3,2,1,0:T(8,128)S(1)}, s32[4,2,8,512]{3,2,1,0:T(8,128)}, u32[]{:S(2)}) copy-start(s32[4,2,8,512]{3,2,1,0:T(8,128)} %cls.1) | copy-start | bytes 393220
  3.4 30.4 %copy-start.8 = (s32[4,2,8,512]{3,2,1,0:T(8,128)}, s32[4,2,8,512]{3,2,1,0:T(8,128)S(1)}, u32[]{:S(2)}) copy-start(s32[4,2,8,512]{3,2,1,0:T(8,128)S(1)} %get-tuple-element.44.refs_7_.refs_3_) | copy-start | bytes 393220
  3.4 6.7 %collective-permute-start.2 = (bf16[4,2,8,512]{3,2,1,0:T(8,128)(2,1)S(1)}, bf16[4,2,8,512]{3,2,1,0:T(8,128)(2,1)S(1)}, u32[]{:S(2)}, u32[]{:S(2)}) collective-permute-start(bf16[4,2,8,512]{3,2,1,0:T(8,128)(2,1)S(1)} %get-tuple-element.40.after.refs_3_), channel_id=1, source_target_pairs={{0,16},{16,0},{1,17},{17,1},{2,18},{18,2},{3,19},{19,3},{4,20},{20... | collective-permute-start | bytes 196616 | tf_op jit(solution)/shard_map/ppermute | solution.py:405
  6.5 1.6 %copy-start.7 = (bf16[16,8,2,8,512]{4,3,2,1,0:T(8,128)(2,1)S(1)}, bf16[16,8,2,8,512]{4,3,2,1,0:T(8,128)(2,1)}, u32[]{:S(2)}) copy-start(bf16[16,8,2,8,512]{4,3,2,1,0:T(8,128)(2,1)} %members.1) | copy-start | bytes 6291460
  8.1 0.9 %copy-start.10 = (f32[4,2,8,512]{3,2,1,0:T(8,128)S(1)}, f32[4,2,8,512]{3,2,1,0:T(8,128)}, u32[]{:S(2)}) copy-start(f32[4,2,8,512]{3,2,1,0:T(8,128)} %static_scale.1) | copy-start | bytes 393220
  9.0 0.8 copy-start.13
  10.6 8.7 %collective-permute-start.4 = (bf16[26,8,512]{2,1,0:T(8,128)(2,1)S(1)}, bf16[26,8,512]{2,1,0:T(8,128)(2,1)S(1)}, u32[]{:S(2)}, u32[]{:S(2)}) collective-permute-start(bf16[26,8,512]{2,1,0:T(8,128)(2,1)S(1)} %get-tuple-element.48), channel_id=1, source_target_pairs={{0,15},{1,0},{2,1},{3,2},{4,3},{5,4},{6,5},{7,6},{8,7},{9,8},{10,9... | collective-permute-start | bytes 638984 | tf_op jit(solution)/shard_map/ppermute | solution.py:408
  14.4 8.0 %collective-permute-start.3 = (bf16[26,8,512]{2,1,0:T(8,128)(2,1)S(1)}, bf16[26,8,512]{2,1,0:T(8,128)(2,1)S(1)}, u32[]{:S(2)}, u32[]{:S(2)}) collective-permute-start(bf16[26,8,512]{2,1,0:T(8,128)(2,1)S(1)} %get-tuple-element.48), channel_id=1, source_target_pairs={{0,1},{1,2},{2,3},{3,4},{4,5},{5,6},{6,7},{7,8},{8,9},{9,10},{10,1... | collective-permute-start | bytes 638984 | tf_op jit(solution)/shard_map/ppermute | solution.py:408
  14.4 11.8 %collective-permute-start.6 = (bf16[16,8,512]{2,1,0:T(8,128)(2,1)S(1)}, bf16[16,8,512]{2,1,0:T(8,128)(2,1)S(1)}, u32[]{:S(2)}, u32[]{:S(2)}) collective-permute-start(bf16[16,8,512]{2,1,0:T(8,128)(2,1)S(1)} %get-tuple-element.50), channel_id=1, source_target_pairs={{0,15},{1,0},{2,1},{3,2},{4,3},{5,4},{6,5},{7,6},{8,7},{9,8},{10,9... | collective-permute-start | bytes 393224 | tf_op jit(solution)/shard_map/ppermute | solution.py:408
  18.8 7.4 %collective-permute-start.5 = (bf16[16,8,512]{2,1,0:T(8,128)(2,1)S(1)}, bf16[16,8,512]{2,1,0:T(8,128)(2,1)S(1)}, u32[]{:S(2)}, u32[]{:S(2)}) collective-permute-start(bf16[16,8,512]{2,1,0:T(8,128)(2,1)S(1)} %get-tuple-element.50), channel_id=1, source_target_pairs={{0,1},{1,2},{2,3},{3,4},{4,5},{5,6},{6,7},{7,8},{8,9},{9,10},{10,1... | collective-permute-start | bytes 393224 | tf_op jit(solution)/shard_map/ppermute | solution.py:408
  18.8 19.7 %collective-permute-start = (f32[4,2,8,512]{3,2,1,0:T(8,128)S(1)}, f32[4,2,8,512]{3,2,1,0:T(8,128)}, u32[]{:S(2)}, u32[]{:S(2)}) collective-permute-start(f32[4,2,8,512]{3,2,1,0:T(8,128)S(1)} %get-tuple-element.43.refs_6_.refs_2_), channel_id=1, source_target_pairs={{0,16},{16,0},{1,17},{17,1},{2,18},{18,2},{3,19},{19,3},{4,20},{20... | collective-permute-start | bytes 393224 | tf_op jit(solution)/shard_map/ppermute | solution.py:405
  26.2 2.6 %copy-start = (f32[3,4,128,128]{3,2,1,0:T(8,128)}, f32[3,4,128,128]{3,2,1,0:T(8,128)S(1)}, u32[]{:S(2)}) copy-start(f32[3,4,128,128]{3,2,1,0:T(8,128)S(1)} %get-tuple-element.62.refs_6_.refs_0_) | copy-start | bytes 2359300
  28.7 5.2 %copy-start.5 = (f32[2,4,128,128]{3,2,1,0:T(8,128)}, f32[2,4,128,128]{3,2,1,0:T(8,128)S(1)}, u32[]{:S(2)}) copy-start(f32[2,4,128,128]{3,2,1,0:T(8,128)S(1)} %get-tuple-element.67.refs_7_.refs_1_) | copy-start | bytes 1572868
  28.8 4.3 %collective-permute-start.8 = (bf16[8,8,512]{2,1,0:T(8,128)(2,1)S(1)}, bf16[8,8,512]{2,1,0:T(8,128)(2,1)S(1)}, u32[]{:S(2)}, u32[]{:S(2)}) collective-permute-start(bf16[8,8,512]{2,1,0:T(8,128)(2,1)S(1)} %get-tuple-element.55), channel_id=1, source_target_pairs={{0,16},{16,0},{1,17},{17,1},{2,18},{18,2},{3,19},{19,3},{4,20},{20... | collective-permute-start | bytes 196616 | tf_op jit(solution)/shard_map/ppermute | solution.py:405
  29.3 4.5 %collective-permute-start.7 = (bf16[8,8,512]{2,1,0:T(8,128)(2,1)S(1)}, bf16[8,8,512]{2,1,0:T(8,128)(2,1)S(1)}, u32[]{:S(2)}, u32[]{:S(2)}) collective-permute-start(bf16[8,8,512]{2,1,0:T(8,128)(2,1)S(1)} %get-tuple-element.54), channel_id=1, source_target_pairs={{0,16},{16,0},{1,17},{17,1},{2,18},{18,2},{3,19},{19,3},{4,20},{20... | collective-permute-start | bytes 196616 | tf_op jit(solution)/shard_map/ppermute | solution.py:405
  30.8 7.6 %collective-permute-start.1 = (bf16[4,2,8,512]{3,2,1,0:T(8,128)(2,1)}, bf16[4,2,8,512]{3,2,1,0:T(8,128)(2,1)}, u32[]{:S(2)}, u32[]{:S(2)}) collective-permute-start(bf16[4,2,8,512]{3,2,1,0:T(8,128)(2,1)} %get-tuple-element.45), channel_id=1, source_target_pairs={{0,16},{16,0},{1,17},{17,1},{2,18},{18,2},{3,19},{19,3},{4,20},{20... | collective-permute-start | bytes 196616 | tf_op jit(solution)/shard_map/ppermute | solution.py:405
  33.9 0.7 copy-start.2
  34.6 0.6 copy-start.14
  35.2 10.4 %all-to-all-start = ((f32[32,1,256]{2,1,0:T(1,128)}), f32[32,1,256]{2,1,0:T(1,128)}, u32[]{:S(2)}, u32[]{:S(2)}) async-start(f32[32,1,256]{2,1,0:T(1,128)} %copy-done.14), calls=%async_computation | async-start | bytes 65536 | tf_op jit(solution)/shard_map/all_to_all | solution.py:485
  45.6 11.9 %copy-start.1 = (f32[3,4,128,128]{3,2,1,0:T(8,128)S(1)}, f32[3,4,128,128]{3,2,1,0:T(8,128)}, u32[]{:S(2)}) copy-start(f32[3,4,128,128]{3,2,1,0:T(8,128)} %copy-done) | copy-start | bytes 2359300
  45.6 1.0 %copy-start.3 = (f32[8,2,8,512]{3,2,1,0:T(8,128)S(1)}, f32[8,2,8,512]{3,2,1,0:T(8,128)}, u32[]{:S(2)}) copy-start(f32[8,2,8,512]{3,2,1,0:T(8,128)} %copy-done.2) | copy-start | bytes 786436
  46.6 0.9 %copy-start.9 = (s32[4,2,8,512]{3,2,1,0:T(8,128)S(1)}, s32[4,2,8,512]{3,2,1,0:T(8,128)}, u32[]{:S(2)}) copy-start(s32[4,2,8,512]{3,2,1,0:T(8,128)} %copy-done.8) | copy-start | bytes 393220
  49.1 4.9 %collective-permute-start.10 = (bf16[24,8,512]{2,1,0:T(8,128)(2,1)S(1)}, bf16[24,8,512]{2,1,0:T(8,128)(2,1)S(1)}, u32[]{:S(2)}, u32[]{:S(2)}) collective-permute-start(bf16[24,8,512]{2,1,0:T(8,128)(2,1)S(1)} %get-tuple-element.61), channel_id=1, source_target_pairs={{0,15},{1,0},{2,1},{3,2},{4,3},{5,4},{6,5},{7,6},{8,7},{9,8},{10,9... | collective-permute-start | bytes 589832 | tf_op jit(solution)/shard_map/ppermute | solution.py:408
  49.6 7.9 %collective-permute-start.9 = (bf16[24,8,512]{2,1,0:T(8,128)(2,1)S(1)}, bf16[24,8,512]{2,1,0:T(8,128)(2,1)S(1)}, u32[]{:S(2)}, u32[]{:S(2)}) collective-permute-start(bf16[24,8,512]{2,1,0:T(8,128)(2,1)S(1)} %get-tuple-element.61), channel_id=1, source_target_pairs={{0,1},{1,2},{2,3},{3,4},{4,5},{5,6},{6,7},{7,8},{8,9},{9,10},{10,1... | collective-permute-start | bytes 589832 | tf_op jit(solution)/shard_map/ppermute | solution.py:408
  49.7 11.5 %collective-permute-start.12 = (bf16[16,8,512]{2,1,0:T(8,128)(2,1)S(1)}, bf16[16,8,512]{2,1,0:T(8,128)(2,1)S(1)}, u32[]{:S(2)}, u32[]{:S(2)}) collective-permute-start(bf16[16,8,512]{2,1,0:T(8,128)(2,1)S(1)} %get-tuple-element.65), channel_id=1, source_target_pairs={{0,15},{1,0},{2,1},{3,2},{4,3},{5,4},{6,5},{7,6},{8,7},{9,8},{10,9... | collective-permute-start | bytes 393224 | tf_op jit(solution)/shard_map/ppermute | solution.py:408
  54.0 7.2 %collective-permute-start.11 = (bf16[16,8,512]{2,1,0:T(8,128)(2,1)S(1)}, bf16[16,8,512]{2,1,0:T(8,128)(2,1)S(1)}, u32[]{:S(2)}, u32[]{:S(2)}) collective-permute-start(bf16[16,8,512]{2,1,0:T(8,128)(2,1)S(1)} %get-tuple-element.65), channel_id=1, source_target_pairs={{0,1},{1,2},{2,3},{3,4},{4,5},{5,6},{6,7},{7,8},{8,9},{9,10},{10,1... | collective-permute-start | bytes 393224 | tf_op jit(solution)/shard_map/ppermute | solution.py:408
  57.5 3.7 %copy-start.6 = (f32[2,4,128,128]{3,2,1,0:T(8,128)S(1)}, f32[2,4,128,128]{3,2,1,0:T(8,128)}, u32[]{:S(2)}) copy-start(f32[2,4,128,128]{3,2,1,0:T(8,128)} %copy-done.5) | copy-start | bytes 1572868
  61.2 17.7 %copy-start.4 = (f32[8,2,8,512]{3,2,1,0:T(8,128)S(1)}, f32[8,2,8,512]{3,2,1,0:T(8,128)}, u32[]{:S(2)}) copy-start(f32[8,2,8,512]{3,2,1,0:T(8,128)} %copy-done.2) | copy-start | bytes 786436
  63.8 4.0 %collective-permute-start.14 = (bf16[4,8,512]{2,1,0:T(8,128)(2,1)S(1)}, bf16[4,8,512]{2,1,0:T(8,128)(2,1)S(1)}, u32[]{:S(2)}, u32[]{:S(2)}) collective-permute-start(bf16[4,8,512]{2,1,0:T(8,128)(2,1)S(1)} %bitcast.15), channel_id=1, source_target_pairs={{0,16},{16,0},{1,17},{17,1},{2,18},{18,2},{3,19},{19,3},{4,20},{20... | collective-permute-start | bytes 98312 | tf_op jit(solution)/shard_map/ppermute | solution.py:405
  64.4 3.9 %collective-permute-start.13 = (bf16[4,8,512]{2,1,0:T(8,128)(2,1)S(1)}, bf16[4,8,512]{2,1,0:T(8,128)(2,1)S(1)}, u32[]{:S(2)}, u32[]{:S(2)}) collective-permute-start(bf16[4,8,512]{2,1,0:T(8,128)(2,1)S(1)} %bitcast.14), channel_id=1, source_target_pairs={{0,16},{16,0},{1,17},{17,1},{2,18},{18,2},{3,19},{19,3},{4,20},{20... | collective-permute-start | bytes 98312 | tf_op jit(solution)/shard_map/ppermute | solution.py:405

commit v4 on v3

--- a/solution.py
+++ b/solution.py
@@ -7,6 +7,7 @@
 from jax.experimental import pallas as pl
 from jax.experimental.pallas import tpu as pltpu
 from jax.sharding import PartitionSpec as P
+
 
 SWEEPS = 4
 ITERS = 2
@@ -35,7 +36,6 @@
         self.ST = -(-(self.S * self.L) // SUB)
         self.PM = self.L * self.KT
         self.PN = self.PM + self.ST
-        self.F = self.K + self.S
         self.C = self.X // LANES
         self.RE = self.R + 4 * SWEEPS
         self.RG = self.R + 2 * SWEEPS
@@ -92,7 +92,7 @@
             code[s, l] = index.astype(f32).astype(bf16)
 
 
-def fetch_kernel(p, members, static_scale, scale_index, after, members_out, static_out, scale_out, sems):
+def fetch_kernel(members, static_scale, scale_index, after, members_out, static_out, scale_out, sems):
     pairs = ((members, members_out), (static_scale, static_out), (scale_index, scale_out))
     copies = [pltpu.make_async_copy(src, dst, sems.at[i]) for i, (src, dst) in enumerate(pairs)]
     for copy in copies:
@@ -187,7 +187,7 @@
     me, at = lax.axis_index("mem"), lax.axis_index("row")
     low_ok = jnp.where(at > 0, 1.0, 0.0).astype(f32)
     high_ok = jnp.where(at < p.row - 1, 1.0, 0.0).astype(f32)
-    R, RE, RG, W = p.R, p.RE, p.RG, SWEEPS
+    R, RE, W = p.R, p.RE, SWEEPS
     H = 2 * W
     fields = p.fields(level)
     count = p.tiles(level)
@@ -321,7 +321,7 @@
 def curvature_kernel(p, first, *refs):
     parts, gots, norms, refs = refs[: p.L], refs[p.L : 2 * p.L], refs[2 * p.L : 3 * p.L], refs[3 * p.L :]
     if first:
-        obs, cls, image, send = refs
+        obs, cls, _, _, image, send = refs
     else:
         obs, cls, image_before, step, image, send = refs
     me = lax.axis_index("mem")
@@ -377,9 +377,9 @@
             increment[s, l] = -(first * image0[me * p.S + s, l]) - second * image1[s, l]
 
 
-def call(kernel, p, outs, scratch, name, far=0, cost=0):
+def call(kernel, outs, scratch, far=0, cost=0):
     vmem = pl.BlockSpec(memory_space=pltpu.VMEM)
-    anywhere = pl.BlockSpec(memory_space=pl.ANY)
+    anywhere = pl.BlockSpec(memory_space=pltpu.MemorySpace.HBM)
 
     def run(*args):
         return pl.pallas_call(
@@ -388,10 +388,9 @@
             in_specs=[anywhere] * far + [vmem] * (len(args) - far),
             out_specs=tuple(vmem for _ in outs),
             scratch_shapes=scratch,
-            compiler_params=pltpu.CompilerParams(vmem_limit_bytes=16 << 20),
+            compiler_params=pltpu.CompilerParams(vmem_limit_bytes=8 << 20),
             cost_estimate=pl.CostEstimate(flops=cost, bytes_accessed=cost, transcendentals=0),
-            name=name,
-        )(*args)
+        )(*[pltpu.with_memory_space_constraint(x, pltpu.MemorySpace.HBM) for x in args[:far]], *args[far:])
 
     return run
 
@@ -417,15 +416,15 @@
     line = ((1, LANES), f32)
 
     obs, cls, own, code = call(
-        part(load_kernel, p), p,
+        part(load_kernel, p),
         [(own_shape, f32), (own_shape, jnp.int32), (own_shape, bf16), (own_shape, bf16)],
-        [pltpu.SemaphoreType.DMA((2,))], "load", far=2,
+        [pltpu.SemaphoreType.DMA((2,))], far=2,
     )(observed, huber_class)
     others = jnp.stack([round_mem(own, shift) for shift in shifts])
     members, static_scale, scale_index = call(
-        part(fetch_kernel, p), p,
+        fetch_kernel,
         [(x.shape, x.dtype) for x in (members, static_scale, scale_index)],
-        [pltpu.SemaphoreType.DMA((3,))], "fetch", far=3, cost=4 << 20,
+        [pltpu.SemaphoreType.DMA((3,))], far=3, cost=4 << 20,
     )(members, static_scale, scale_index, own)
     obs_in = jnp.stack([round_mem(obs, shift) for shift in shifts])
     code_in = jnp.stack([round_mem(code, shift) for shift in shifts])
@@ -439,11 +438,11 @@
         msg_shapes = [((size, R, X), bf16) for size in sizes]
         if first:
             back, *msgs = call(
-                part(back_kernel, p, True), p, [(back_shape, f32)] + msg_shapes, [vmem(full_shape)], "back0",
+                part(back_kernel, p, True), [(back_shape, f32)] + msg_shapes, [vmem(full_shape)],
             )(members, static_scale, scale_index, own, others)
         else:
             back, step, *msgs = call(
-                part(back_kernel, p, False), p, [(back_shape, f32), line] + msg_shapes, [vmem(full_shape)], "back1",
+                part(back_kernel, p, False), [(back_shape, f32), line] + msg_shapes, [vmem(full_shape)],
             )(members, static_scale, obs, cls, obs_in, code_in, image, sums)
         halos = [(round_row(msg, 1), round_row(msg, p.row - 1)) for msg in msgs]
         grad, norms, partial_images, gots, rest = [], [], [], [], None
@@ -462,8 +461,8 @@
             halo = vmem((count, C, 2 * SWEEPS * SUB, LANES))
             work = [halo, halo, vmem((C, p.RE * SUB, LANES)), vmem((C, p.RE * SUB, LANES))]
             g, norm, partial_image, ship, *more = call(
-                part(sweep_kernel, p, first, level), p, outs, work + [vmem((count, C, R * SUB, LANES))],
-                f"sweep{turn}_{level}", cost=8 << 20,
+                part(sweep_kernel, p, first, level), outs, work + [vmem((count, C, R * SUB, LANES))],
+                cost=8 << 20,
             )(*args)
             if level == 0 and L > 1:
                 rest, *more = more
@@ -476,16 +475,16 @@
         grads.append(grad)
         if first:
             image, send = call(
-                part(curvature_kernel, p, True), p, [(full_shape, f32), send_shape], [], "curv0",
-            )(*partial_images, *gots, *norms, obs, cls)
+                part(curvature_kernel, p, True), [(full_shape, f32), send_shape], [],
+            )(*partial_images, *gots, *norms, obs, cls, obs_in, code_in)
         else:
             last, send = call(
-                part(curvature_kernel, p, False), p, [(own_shape, f32), send_shape], [], "curv1",
+                part(curvature_kernel, p, False), [(own_shape, f32), send_shape], [],
             )(*partial_images, *gots, *norms, obs, cls, image, step)
         sums = lax.all_to_all(send, ("mem", "row"), 0, 0)
     return call(
-        part(final_kernel, p), p,
-        [((K, L, R, X), f32), (own_shape, f32), (own_shape, f32)], [], "final",
+        part(final_kernel, p),
+        [((K, L, R, X), f32), (own_shape, f32), (own_shape, f32)], [],
     )(sums, step, image, last, *grads[0], *grads[1])
 
 

time: 80.4 us -> 73.7 us (0.917)
  blocking collectives: 10.4 us -> 20.8 us
  local copies, waits for them, and re-layouts: 8.3 us -> 0 us
  waiting for transfers between devices: 18.4 us -> 11.8 us
  starting transfers between devices: 24.6 us -> 21.9 us
  Pallas kernels: 17.4 us -> 18.3 us
    all_to_all x1 -> x2, blocking collectives: 10.4 us -> 20.8 us  [local(): sums = lax.all_to_all(send, ('mem', 'row'), 0, 0)]
    unnamed x30 -> x0, local copies, waits for them, and re-layouts: 8.3 us -> none
    all_to_all x1 -> x0, waiting for transfers between devices: 7.06 us -> none  [local(): sums = lax.all_to_all(send, ('mem', 'row'), 0, 0)]
    all_to_all x1 -> x0, starting transfers between devices: 3.27 us -> none  [local(): sums = lax.all_to_all(send, ('mem', 'row'), 0, 0)]
    ppermute x7, waiting for transfers between devices: 4.92 us -> 6.81 us  [round_mem(): lax.ppermute(block, 'mem', [(i, (i + shift) % p.mem) for i in range(p.mem)])]
    ppermute x8, waiting for transfers between devices: 6.47 us -> 4.95 us  [round_row(): lax.ppermute(block, 'row', [(i, (i + shift) % p.row) for i in range(p.row)])]
    ppermute x7, starting transfers between devices: 8.26 us -> 9.27 us  [round_mem(): lax.ppermute(block, 'mem', [(i, (i + shift) % p.mem) for i in range(p.mem)])]
    pallas_call x11, Pallas kernels: 17.4 us -> 18.3 us  [run(): pl.pallas_call(kernel, out_shape=tuple((jax.ShapeDtypeStruct(shape, dtype...]
  transfers between devices with their start and end apart: 16 -> 15, of which waited for: 7 -> 7; matrix products, arithmetic and copies ran while one was open for 0% -> 0% of each run, Pallas kernels for 13% -> 16%
where the time goes in v4:
time: 73.7 us; the launch traced here: 73.5 us
  starting transfers between devices  21.9 us (30%)
  blocking collectives  20.8 us (28%)
  Pallas kernels  18.3 us (25%)
  waiting for transfers between devices  11.8 us (16%)
  between operations  0.74 us (1%)
    all_to_all x2, blocking collectives, local(): sums = lax.all_to_all(send, ('mem', 'row'), 0, 0)  20.8 us
    pallas_call x11, Pallas kernels, run(): pl.pallas_call(kernel, out_shape=tuple((jax.ShapeDtypeStruct(shape, dtype...  18.3 us
    ppermute x8, starting transfers between devices, round_row(): lax.ppermute(block, 'row', [(i, (i + shift) % p.row) for i in range(p.row)])  12.6 us
    ppermute x7, starting transfers between devices, round_mem(): lax.ppermute(block, 'mem', [(i, (i + shift) % p.mem) for i in range(p.mem)])  9.27 us
    ppermute x7, waiting for transfers between devices, round_mem(): lax.ppermute(block, 'mem', [(i, (i + shift) % p.mem) for i in range(p.mem)])  6.81 us
    ppermute x8, waiting for transfers between devices, round_row(): lax.ppermute(block, 'row', [(i, (i + shift) % p.row) for i in range(p.row)])  4.95 us
  transfers between devices with their start and end apart: 15, of which 7 were waited for; matrix products, arithmetic and copies ran while one was open for 0% of the time, Pallas kernels for 16%

profile of v4, /device:TPU:0, one launch (start us, length us, event | category | flops | bytes accessed | tf_op | source)
XLA Modules:
  0.0 73.5 jit_solution(12951556989375777399)
XLA Ops:
  0.6 1.0 %shard_map.76 = (f32[4,2,8,512]{3,2,1,0:T(8,128)S(1)}, s32[4,2,8,512]{3,2,1,0:T(8,128)S(1)}, bf16[4,2,8,512]{3,2,1,0:T(8,128)(2,1)S(1)}, bf16[4,2,8,512]{3,2,1,0:T(8,128)(2,1)S(1)}) custom-call(f32[4,2,8,512]{3,2,1,0:T(8,128)} %obs.1, s32[4,2,8,512]{3,2,1,0:T(8,128)} %cls.1), custom_call_target="tpu_custom_call" | custom-call | tf_op jit(solution)/shard_map/pallas_call | solution.py:385
  1.7 3.1 %collective-permute-start.2 = (bf16[4,2,8,512]{3,2,1,0:T(8,128)(2,1)S(1)}, bf16[4,2,8,512]{3,2,1,0:T(8,128)(2,1)S(1)}, u32[]{:S(2)}, u32[]{:S(2)}) collective-permute-start(bf16[4,2,8,512]{3,2,1,0:T(8,128)(2,1)S(1)} %get-tuple-element.40.after.refs_3_), channel_id=1, source_target_pairs={{0,16},{16,0},{1,17},{17,1},{2,18},{18,2},{3,19},{19,3},{4,20},{20... | collective-permute-start | bytes 196616 | tf_op jit(solution)/shard_map/ppermute | solution.py:404
  4.7 1.6 %shard_map.77 = (bf16[16,8,2,8,512]{4,3,2,1,0:T(8,128)(2,1)S(1)}, f32[4,2,8,512]{3,2,1,0:T(8,128)S(1)}, s32[2,8,512]{2,1,0:T(8,128)S(1)}) custom-call(bf16[16,8,2,8,512]{4,3,2,1,0:T(8,128)(2,1)} %members.1, f32[4,2,8,512]{3,2,1,0:T(8,128)} %static_scale.1, s32[2,8,512]{2,1,0:T(8,128)} %scale_index.1, bf16[4,2,8,512]{3,2,1,0:T(8,128)(2,1)S(1)} %get-tuple-element.40.after.refs_3_), custom_call_target="tpu_custom_call" | custom-call | flops 4194304 | bytes 4194304 | tf_op jit(solution)/shard_map/pallas_call | solution.py:385
  6.4 0.6 collective-permute-done.2
  7.0 0.5 shard_map.78
  7.5 3.4 %collective-permute-start.4 = (bf16[26,8,512]{2,1,0:T(8,128)(2,1)S(1)}, bf16[26,8,512]{2,1,0:T(8,128)(2,1)S(1)}, u32[]{:S(2)}, u32[]{:S(2)}) collective-permute-start(bf16[26,8,512]{2,1,0:T(8,128)(2,1)S(1)} %get-tuple-element.48), channel_id=1, source_target_pairs={{0,15},{1,0},{2,1},{3,2},{4,3},{5,4},{6,5},{7,6},{8,7},{9,8},{10,9... | collective-permute-start | bytes 638984 | tf_op jit(solution)/shard_map/ppermute | solution.py:407
  10.9 0.0 collective-permute-start.3
  10.9 4.4 %collective-permute-start.6 = (bf16[16,8,512]{2,1,0:T(8,128)(2,1)S(1)}, bf16[16,8,512]{2,1,0:T(8,128)(2,1)S(1)}, u32[]{:S(2)}, u32[]{:S(2)}) collective-permute-start(bf16[16,8,512]{2,1,0:T(8,128)(2,1)S(1)} %get-tuple-element.50), channel_id=1, source_target_pairs={{0,15},{1,0},{2,1},{3,2},{4,3},{5,4},{6,5},{7,6},{8,7},{9,8},{10,9... | collective-permute-start | bytes 393224 | tf_op jit(solution)/shard_map/ppermute | solution.py:407
  15.3 0.0 collective-permute-start.5
  15.3 1.5 %collective-permute-start = (f32[4,2,8,512]{3,2,1,0:T(8,128)S(1)}, f32[4,2,8,512]{3,2,1,0:T(8,128)S(1)}, u32[]{:S(2)}, u32[]{:S(2)}) collective-permute-start(f32[4,2,8,512]{3,2,1,0:T(8,128)S(1)} %get-tuple-element.43.refs_6_.refs_2_), channel_id=1, source_target_pairs={{0,16},{16,0},{1,17},{17,1},{2,18},{18,2},{3,19},{19,3},{4,20},{20... | collective-permute-start | bytes 393224 | tf_op jit(solution)/shard_map/ppermute | solution.py:404
  16.8 0.0 collective-permute-done.4.refs_4_
  16.9 0.5 collective-permute-start.1
  17.4 1.5 %collective-permute-done.3.refs_3_ = bf16[26,8,512]{2,1,0:T(8,128)(2,1)S(1)} collective-permute-done((bf16[26,8,512]{2,1,0:T(8,128)(2,1)S(1)}, bf16[26,8,512]{2,1,0:T(8,128)(2,1)S(1)}, u32[]{:S(2)}, u32[]{:S(2)}) %collective-permute-start.3) | collective-permute-done | bytes 213024 | tf_op jit(solution)/shard_map/ppermute | solution.py:407
  18.8 3.9 %shard_map.79 = (f32[3,4,128,128]{3,2,1,0:T(8,128)S(1)}, f32[1,128]{1,0:T(1,128)S(1)}, f32[8,8,512]{2,1,0:T(8,128)S(1)}, bf16[8,8,512]{2,1,0:T(8,128)(2,1)S(1)},...) custom-call(bf16[16,8,2,8,512]{4,3,2,1,0:T(8,128)(2,1)S(1)} %get-tuple-element.41.refs_0_, ...), custom_call_target="tpu_custom_call" | custom-call | flops 8388608 | bytes 8388608 | tf_op jit(solution)/shard_map/pallas_call | solution.py:385
  22.8 0.0 collective-permute-done.6.refs_4_
  22.8 0.0 collective-permute-done.5.refs_3_
  22.8 2.6 %shard_map.80 = (f32[2,4,128,128]{3,2,1,0:T(8,128)S(1)}, f32[1,128]{1,0:T(1,128)S(1)}, f32[8,8,512]{2,1,0:T(8,128)S(1)}, bf16[8,8,512]{2,1,0:T(8,128)(2,1)S(1)}) custom-call(bf16[16,8,2,8,512]{4,3,2,1,0:T(8,128)(2,1)S(1)} %get-tuple-element.41.refs_0_, f32[4,2,8,512]{3,2,1,0:T(8,128)S(1)} %get-tuple-element.42.refs_1_, ...), custom_call_target="tpu_custom_call" | custom-call | flops 8388608 | bytes 8388608 | tf_op jit(solution)/shard_map/pallas_call | solution.py:385
  25.4 1.6 %collective-permute-start.8 = (bf16[8,8,512]{2,1,0:T(8,128)(2,1)S(1)}, bf16[8,8,512]{2,1,0:T(8,128)(2,1)S(1)}, u32[]{:S(2)}, u32[]{:S(2)}) collective-permute-start(bf16[8,8,512]{2,1,0:T(8,128)(2,1)S(1)} %get-tuple-element.55), channel_id=1, source_target_pairs={{0,16},{16,0},{1,17},{17,1},{2,18},{18,2},{3,19},{19,3},{4,20},{20... | collective-permute-start | bytes 196616 | tf_op jit(solution)/shard_map/ppermute | solution.py:404
  27.0 0.5 collective-permute-start.7
  27.5 0.0 collective-permute-done.1
  27.5 0.0 collective-permute-done
  27.5 2.2 %collective-permute-done.8 = bf16[8,8,512]{2,1,0:T(8,128)(2,1)S(1)} collective-permute-done((bf16[8,8,512]{2,1,0:T(8,128)(2,1)S(1)}, bf16[8,8,512]{2,1,0:T(8,128)(2,1)S(1)}, u32[]{:S(2)}, u32[]{:S(2)}) %collective-permute-start.8) | collective-permute-done | bytes 65568 | tf_op jit(solution)/shard_map/ppermute | solution.py:404
  29.7 1.5 %collective-permute-done.7 = bf16[8,8,512]{2,1,0:T(8,128)(2,1)S(1)} collective-permute-done((bf16[8,8,512]{2,1,0:T(8,128)(2,1)S(1)}, bf16[8,8,512]{2,1,0:T(8,128)(2,1)S(1)}, u32[]{:S(2)}, u32[]{:S(2)}) %collective-permute-start.7) | collective-permute-done | bytes 65568 | tf_op jit(solution)/shard_map/ppermute | solution.py:404
  31.3 0.1 shard_map.81
  31.4 10.3 %all_to_all.10.refs_7_ = f32[32,1,256]{2,1,0:T(1,128)S(1)} all-to-all(f32[32,1,256]{2,1,0:T(1,128)S(1)} %get-tuple-element.59), channel_id=1, replica_groups=mesh['mem'=2,'row'=16] {'mem','row'}, dimensions={0} | all-to-all | bytes 65536 | tf_op jit(solution)/shard_map/all_to_all | solution.py:484
  41.7 0.7 shard_map.82
  42.4 0.3 collective-permute-start.10
  42.7 0.2 collective-permute-start.9
  43.0 4.2 %collective-permute-start.12 = (bf16[16,8,512]{2,1,0:T(8,128)(2,1)S(1)}, bf16[16,8,512]{2,1,0:T(8,128)(2,1)S(1)}, u32[]{:S(2)}, u32[]{:S(2)}) collective-permute-start(bf16[16,8,512]{2,1,0:T(8,128)(2,1)S(1)} %get-tuple-element.65), channel_id=1, source_target_pairs={{0,15},{1,0},{2,1},{3,2},{4,3},{5,4},{6,5},{7,6},{8,7},{9,8},{10,9... | collective-permute-start | bytes 393224 | tf_op jit(solution)/shard_map/ppermute | solution.py:407
  47.2 0.0 collective-permute-start.11
  47.2 0.0 collective-permute-done.10.refs_4_
  47.2 3.4 %collective-permute-done.9.refs_3_ = bf16[24,8,512]{2,1,0:T(8,128)(2,1)S(1)} collective-permute-done((bf16[24,8,512]{2,1,0:T(8,128)(2,1)S(1)}, bf16[24,8,512]{2,1,0:T(8,128)(2,1)S(1)}, u32[]{:S(2)}, u32[]{:S(2)}) %collective-permute-start.9) | collective-permute-done | bytes 196640 | tf_op jit(solution)/shard_map/ppermute | solution.py:407
  50.6 3.9 %shard_map.83 = (f32[3,4,128,128]{3,2,1,0:T(8,128)S(1)}, f32[1,128]{1,0:T(1,128)S(1)}, f32[8,8,512]{2,1,0:T(8,128)S(1)}, bf16[1,4,8,512]{3,2,1,0:T(8,128)(2,1)S(1)}, f32[1,4,8,512]{3,2,1,0:T(8,128)S(1)}) custom-call(bf16[16,8,2,8,512]{4,3,2,1,0:T(8,128)(2,1)S(1)} %get-tuple-element.41.refs_0_, f32[4,2,8,512]{3,2,1,0:T(8,128)S(1)} %get-tuple-element.42.refs_1_, ...), custom_call_target="tpu_custom_call" | custom-call | flops 8388608 | bytes 8388608 | tf_op jit(solution)/shard_map/pallas_call | solution.py:385
  54.5 0.0 collective-permute-done.12.refs_4_
  54.5 0.0 collective-permute-done.11.refs_3_
  54.5 2.6 %shard_map.84 = (f32[2,4,128,128]{3,2,1,0:T(8,128)S(1)}, f32[1,128]{1,0:T(1,128)S(1)}, f32[8,8,512]{2,1,0:T(8,128)S(1)}, bf16[1,4,8,512]{3,2,1,0:T(8,128)(2,1)S(1)}) custom-call(bf16[16,8,2,8,512]{4,3,2,1,0:T(8,128)(2,1)S(1)} %get-tuple-element.41.refs_0_, f32[4,2,8,512]{3,2,1,0:T(8,128)S(1)} %get-tuple-element.42.refs_1_, ...), custom_call_target="tpu_custom_call" | custom-call | flops 8388608 | bytes 8388608 | tf_op jit(solution)/shard_map/pallas_call | solution.py:385
  57.2 0.6 collective-permute-start.14
  57.8 1.5 %collective-permute-start.13 = (bf16[4,8,512]{2,1,0:T(8,128)(2,1)S(1)}, bf16[4,8,512]{2,1,0:T(8,128)(2,1)S(1)}, u32[]{:S(2)}, u32[]{:S(2)}) collective-permute-start(bf16[4,8,512]{2,1,0:T(8,128)(2,1)S(1)} %bitcast.18), channel_id=1, source_target_pairs={{0,16},{16,0},{1,17},{17,1},{2,18},{18,2},{3,19},{19,3},{4,20},{20... | collective-permute-start | bytes 98312 | tf_op jit(solution)/shard_map/ppermute | solution.py:404
  59.3 1.9 %collective-permute-done.14 = bf16[4,8,512]{2,1,0:T(8,128)(2,1)S(1)} collective-permute-done((bf16[4,8,512]{2,1,0:T(8,128)(2,1)S(1)}, bf16[4,8,512]{2,1,0:T(8,128)(2,1)S(1)}, u32[]{:S(2)}, u32[]{:S(2)}) %collective-permute-start.14) | collective-permute-done | bytes 32800 | tf_op jit(solution)/shard_map/ppermute | solution.py:404
  61.2 0.5 collective-permute-done.13
  61.7 0.1 shard_map.85
  61.9 10.5 %all_to_all.11.got = f32[32,1,256]{2,1,0:T(1,128)S(1)} all-to-all(f32[32,1,256]{2,1,0:T(1,128)S(1)} %get-tuple-element.73), channel_id=1, replica_groups=mesh['mem'=2,'row'=16] {'mem','row'}, dimensions={0} | all-to-all | bytes 65536 | tf_op jit(solution)/shard_map/all_to_all | solution.py:484
  72.3 1.2 %shard_map.86 = (f32[16,2,8,512]{3,2,1,0:T(8,128)}, f32[4,2,8,512]{3,2,1,0:T(8,128)}, f32[4,2,8,512]{3,2,1,0:T(8,128)}) custom-call(f32[32,1,256]{2,1,0:T(1,128)S(1)} %all_to_all.11.got, f32[1,128]{1,0:T(1,128)S(1)} %get-tuple-element.63.refs_7_.refs_8_.refs_9_.step, f32[8,2,8,512]{3,2,1,0:T(8,128)S(1)} %get-tuple-element.58.refs_6_.refs_8_.image0, ...), custom_call_target="tpu_custom_call" | custom-call | tf_op jit(solution)/shard_map/pallas_call | solution.py:385
Async XLA Ops:
  1.7 5.3 %collective-permute-start.2 = (bf16[4,2,8,512]{3,2,1,0:T(8,128)(2,1)S(1)}, bf16[4,2,8,512]{3,2,1,0:T(8,128)(2,1)S(1)}, u32[]{:S(2)}, u32[]{:S(2)}) collective-permute-start(bf16[4,2,8,512]{3,2,1,0:T(8,128)(2,1)S(1)} %get-tuple-element.40.after.refs_3_), channel_id=1, source_target_pairs={{0,16},{16,0},{1,17},{17,1},{2,18},{18,2},{3,19},{19,3},{4,20},{20... | collective-permute-start | bytes 196616 | tf_op jit(solution)/shard_map/ppermute | solution.py:404
  7.5 9.3 %collective-permute-start.4 = (bf16[26,8,512]{2,1,0:T(8,128)(2,1)S(1)}, bf16[26,8,512]{2,1,0:T(8,128)(2,1)S(1)}, u32[]{:S(2)}, u32[]{:S(2)}) collective-permute-start(bf16[26,8,512]{2,1,0:T(8,128)(2,1)S(1)} %get-tuple-element.48), channel_id=1, source_target_pairs={{0,15},{1,0},{2,1},{3,2},{4,3},{5,4},{6,5},{7,6},{8,7},{9,8},{10,9... | collective-permute-start | bytes 638984 | tf_op jit(solution)/shard_map/ppermute | solution.py:407
  10.9 8.0 %collective-permute-start.3 = (bf16[26,8,512]{2,1,0:T(8,128)(2,1)S(1)}, bf16[26,8,512]{2,1,0:T(8,128)(2,1)S(1)}, u32[]{:S(2)}, u32[]{:S(2)}) collective-permute-start(bf16[26,8,512]{2,1,0:T(8,128)(2,1)S(1)} %get-tuple-element.48), channel_id=1, source_target_pairs={{0,1},{1,2},{2,3},{3,4},{4,5},{5,6},{6,7},{7,8},{8,9},{9,10},{10,1... | collective-permute-start | bytes 638984 | tf_op jit(solution)/shard_map/ppermute | solution.py:407
  10.9 11.9 %collective-permute-start.6 = (bf16[16,8,512]{2,1,0:T(8,128)(2,1)S(1)}, bf16[16,8,512]{2,1,0:T(8,128)(2,1)S(1)}, u32[]{:S(2)}, u32[]{:S(2)}) collective-permute-start(bf16[16,8,512]{2,1,0:T(8,128)(2,1)S(1)} %get-tuple-element.50), channel_id=1, source_target_pairs={{0,15},{1,0},{2,1},{3,2},{4,3},{5,4},{6,5},{7,6},{8,7},{9,8},{10,9... | collective-permute-start | bytes 393224 | tf_op jit(solution)/shard_map/ppermute | solution.py:407
  15.3 7.4 %collective-permute-start.5 = (bf16[16,8,512]{2,1,0:T(8,128)(2,1)S(1)}, bf16[16,8,512]{2,1,0:T(8,128)(2,1)S(1)}, u32[]{:S(2)}, u32[]{:S(2)}) collective-permute-start(bf16[16,8,512]{2,1,0:T(8,128)(2,1)S(1)} %get-tuple-element.50), channel_id=1, source_target_pairs={{0,1},{1,2},{2,3},{3,4},{4,5},{5,6},{6,7},{7,8},{8,9},{9,10},{10,1... | collective-permute-start | bytes 393224 | tf_op jit(solution)/shard_map/ppermute | solution.py:407
  15.3 12.2 %collective-permute-start = (f32[4,2,8,512]{3,2,1,0:T(8,128)S(1)}, f32[4,2,8,512]{3,2,1,0:T(8,128)S(1)}, u32[]{:S(2)}, u32[]{:S(2)}) collective-permute-start(f32[4,2,8,512]{3,2,1,0:T(8,128)S(1)} %get-tuple-element.43.refs_6_.refs_2_), channel_id=1, source_target_pairs={{0,16},{16,0},{1,17},{17,1},{2,18},{18,2},{3,19},{19,3},{4,20},{20... | collective-permute-start | bytes 393224 | tf_op jit(solution)/shard_map/ppermute | solution.py:404
  16.9 10.6 %collective-permute-start.1 = (bf16[4,2,8,512]{3,2,1,0:T(8,128)(2,1)S(1)}, bf16[4,2,8,512]{3,2,1,0:T(8,128)(2,1)S(1)}, u32[]{:S(2)}, u32[]{:S(2)}) collective-permute-start(bf16[4,2,8,512]{3,2,1,0:T(8,128)(2,1)S(1)} %get-tuple-element.45), channel_id=1, source_target_pairs={{0,16},{16,0},{1,17},{17,1},{2,18},{18,2},{3,19},{19,3},{4,20},{20... | collective-permute-start | bytes 196616 | tf_op jit(solution)/shard_map/ppermute | solution.py:404
  25.4 4.3 %collective-permute-start.8 = (bf16[8,8,512]{2,1,0:T(8,128)(2,1)S(1)}, bf16[8,8,512]{2,1,0:T(8,128)(2,1)S(1)}, u32[]{:S(2)}, u32[]{:S(2)}) collective-permute-start(bf16[8,8,512]{2,1,0:T(8,128)(2,1)S(1)} %get-tuple-element.55), channel_id=1, source_target_pairs={{0,16},{16,0},{1,17},{17,1},{2,18},{18,2},{3,19},{19,3},{4,20},{20... | collective-permute-start | bytes 196616 | tf_op jit(solution)/shard_map/ppermute | solution.py:404
  27.0 4.3 %collective-permute-start.7 = (bf16[8,8,512]{2,1,0:T(8,128)(2,1)S(1)}, bf16[8,8,512]{2,1,0:T(8,128)(2,1)S(1)}, u32[]{:S(2)}, u32[]{:S(2)}) collective-permute-start(bf16[8,8,512]{2,1,0:T(8,128)(2,1)S(1)} %get-tuple-element.54), channel_id=1, source_target_pairs={{0,16},{16,0},{1,17},{17,1},{2,18},{18,2},{3,19},{19,3},{4,20},{20... | collective-permute-start | bytes 196616 | tf_op jit(solution)/shard_map/ppermute | solution.py:404
  42.4 4.8 %collective-permute-start.10 = (bf16[24,8,512]{2,1,0:T(8,128)(2,1)S(1)}, bf16[24,8,512]{2,1,0:T(8,128)(2,1)S(1)}, u32[]{:S(2)}, u32[]{:S(2)}) collective-permute-start(bf16[24,8,512]{2,1,0:T(8,128)(2,1)S(1)} %get-tuple-element.61), channel_id=1, source_target_pairs={{0,15},{1,0},{2,1},{3,2},{4,3},{5,4},{6,5},{7,6},{8,7},{9,8},{10,9... | collective-permute-start | bytes 589832 | tf_op jit(solution)/shard_map/ppermute | solution.py:407
  42.7 7.9 %collective-permute-start.9 = (bf16[24,8,512]{2,1,0:T(8,128)(2,1)S(1)}, bf16[24,8,512]{2,1,0:T(8,128)(2,1)S(1)}, u32[]{:S(2)}, u32[]{:S(2)}) collective-permute-start(bf16[24,8,512]{2,1,0:T(8,128)(2,1)S(1)} %get-tuple-element.61), channel_id=1, source_target_pairs={{0,1},{1,2},{2,3},{3,4},{4,5},{5,6},{6,7},{7,8},{8,9},{9,10},{10,1... | collective-permute-start | bytes 589832 | tf_op jit(solution)/shard_map/ppermute | solution.py:407
  43.0 11.5 %collective-permute-start.12 = (bf16[16,8,512]{2,1,0:T(8,128)(2,1)S(1)}, bf16[16,8,512]{2,1,0:T(8,128)(2,1)S(1)}, u32[]{:S(2)}, u32[]{:S(2)}) collective-permute-start(bf16[16,8,512]{2,1,0:T(8,128)(2,1)S(1)} %get-tuple-element.65), channel_id=1, source_target_pairs={{0,15},{1,0},{2,1},{3,2},{4,3},{5,4},{6,5},{7,6},{8,7},{9,8},{10,9... | collective-permute-start | bytes 393224 | tf_op jit(solution)/shard_map/ppermute | solution.py:407
  47.2 7.3 %collective-permute-start.11 = (bf16[16,8,512]{2,1,0:T(8,128)(2,1)S(1)}, bf16[16,8,512]{2,1,0:T(8,128)(2,1)S(1)}, u32[]{:S(2)}, u32[]{:S(2)}) collective-permute-start(bf16[16,8,512]{2,1,0:T(8,128)(2,1)S(1)} %get-tuple-element.65), channel_id=1, source_target_pairs={{0,1},{1,2},{2,3},{3,4},{4,5},{5,6},{6,7},{7,8},{8,9},{9,10},{10,1... | collective-permute-start | bytes 393224 | tf_op jit(solution)/shard_map/ppermute | solution.py:407
  57.2 4.0 %collective-permute-start.14 = (bf16[4,8,512]{2,1,0:T(8,128)(2,1)S(1)}, bf16[4,8,512]{2,1,0:T(8,128)(2,1)S(1)}, u32[]{:S(2)}, u32[]{:S(2)}) collective-permute-start(bf16[4,8,512]{2,1,0:T(8,128)(2,1)S(1)} %bitcast.19), channel_id=1, source_target_pairs={{0,16},{16,0},{1,17},{17,1},{2,18},{18,2},{3,19},{19,3},{4,20},{20... | collective-permute-start | bytes 98312 | tf_op jit(solution)/shard_map/ppermute | solution.py:404
  57.8 3.9 %collective-permute-start.13 = (bf16[4,8,512]{2,1,0:T(8,128)(2,1)S(1)}, bf16[4,8,512]{2,1,0:T(8,128)(2,1)S(1)}, u32[]{:S(2)}, u32[]{:S(2)}) collective-permute-start(bf16[4,8,512]{2,1,0:T(8,128)(2,1)S(1)} %bitcast.18), channel_id=1, source_target_pairs={{0,16},{16,0},{1,17},{17,1},{2,18},{18,2},{3,19},{19,3},{4,20},{20... | collective-permute-start | bytes 98312 | tf_op jit(solution)/shard_map/ppermute | solution.py:404

commit v5 on v4

--- a/solution.py
+++ b/solution.py
@@ -45,10 +45,10 @@
 
     def fields(self, level):
         own = [(k, level) for k in range(self.K)]
-        return own + [(self.K + s, l) for s in range(self.S) for l in range(self.L)] if level == 0 else own
+        return own + [(self.K + s, l) for s in range(self.S) for l in range(self.L)] if level == self.L - 1 else own
 
     def tiles(self, level):
-        return self.KT + self.ST if level == 0 else self.KT
+        return self.KT + self.ST if level == self.L - 1 else self.KT
 
     def inner(self, field, level):
         if field < self.K:
@@ -76,7 +76,26 @@
     return jnp.concatenate([ref[tile, c, where, :] for c in range(ref.shape[1])], axis=1)
 
 
-def load_kernel(p, obs, cls, obs_out, cls_out, sent, code, sems):
+def onehot(p):
+    source = lax.broadcasted_iota(jnp.int32, (p.X, p.X), 0)
+    target = lax.broadcasted_iota(jnp.int32, (p.X, p.X), 1)
+    return jnp.where(source == (target % LANES) * p.C + target // LANES, 1.0, 0.0).astype(bf16)
+
+
+def product(block, matrix, back=False):
+    dims = (((1,), (1 if back else 0,)), ((), ()))
+    return lax.dot_general(block, matrix, dims, preferred_element_type=f32)
+
+
+def exact(block, matrix, back=False):
+    first = block.astype(bf16)
+    left = block - first.astype(f32)
+    second = left.astype(bf16)
+    third = (left - second.astype(f32)).astype(bf16)
+    return product(first, matrix, back) + (product(second, matrix, back) + product(third, matrix, back))
+
+
+def load_kernel(p, obs, cls, obs_out, cls_out, sent, sems):
     pairs = ((obs, obs_out), (cls, cls_out))
     copies = [pltpu.make_async_copy(src, dst, sems.at[i]) for i, (src, dst) in enumerate(pairs)]
     for copy in copies:
@@ -89,23 +108,40 @@
             threshold = table(index, huber_levels)
             clipped = jnp.where(index > 0, jnp.clip(-obs_out[s, l], -threshold, threshold), 0.0)
             sent[s, l] = clipped.astype(bf16)
-            code[s, l] = index.astype(f32).astype(bf16)
-
-
-def fetch_kernel(members, static_scale, scale_index, after, members_out, static_out, scale_out, sems):
-    pairs = ((members, members_out), (static_scale, static_out), (scale_index, scale_out))
-    copies = [pltpu.make_async_copy(src, dst, sems.at[i]) for i, (src, dst) in enumerate(pairs)]
-    for copy in copies:
+
+
+def fetch_kernel(p, members, static_scale, scale_index, obs, cls, own, members_out, static_out, scale_out, pack,
+                 own_out, matrix_out, raw, static_raw, scale_raw, sems):
+    copies = [pltpu.make_async_copy(members.at[k], raw.at[k], sems.at[k]) for k in range(p.K)]
+    rest = [
+        pltpu.make_async_copy(static_scale, static_raw, sems.at[p.K]),
+        pltpu.make_async_copy(scale_index, scale_raw, sems.at[p.K + 1]),
+    ]
+    for copy in copies + rest:
         copy.start()
-    for copy in copies:
+    matrix_out[...] = onehot(p)
+    matrix = matrix_out[...]
+    rows = p.S * p.L * p.R
+    own_out[...] = product(own[...].reshape(rows, p.X), matrix).astype(bf16).reshape(own_out.shape)
+    shape = (p.S, p.L, p.R, p.X)
+    pack[0] = exact(obs[...].reshape(rows, p.X), matrix).reshape(shape)
+    pack[1] = product(cls[...].astype(f32).astype(bf16).reshape(rows, p.X), matrix).reshape(shape)
+    for copy in rest:
         copy.wait()
+    static_out[...] = exact(static_raw[...].reshape(rows, p.X), matrix).reshape(shape)
+    scale = scale_raw[...].astype(f32).astype(bf16).reshape(p.L * p.R, p.X)
+    scale_out[...] = product(scale, matrix).reshape(scale_out.shape)
+    for k in range(p.K):
+        copies[k].wait()
+        block = raw[k].reshape(p.V * p.L * p.R, p.X)
+        members_out[k] = product(block, matrix).astype(bf16).reshape(p.V, p.L, p.R, p.X)
 
 
 def back_kernel(p, first, *refs):
     if first:
-        members, static_scale, scale_index, own, others, back, *msgs, sent = refs
+        members, static_scale, scale_index, own, others, matrix, back, *msgs, sent = refs
     else:
-        members, static_scale, obs, cls, obs_in, code_in, image, got, back, step_out, *msgs, sent = refs
+        members, static_scale, pack, pack_in, image, got, back, step_out, *msgs, sent = refs
     me = lax.axis_index("mem")
     if p.pads:
         back[...] = jnp.zeros(back.shape, f32)
@@ -117,15 +153,18 @@
         step_out[...] = jnp.broadcast_to(step, step_out.shape)
     for shift in range(p.mem):
         base = lax.rem(me + (p.mem - shift), p.mem) * p.S
+        if first and shift:
+            block = product(others[shift - 1].reshape(p.S * p.L * p.R, p.X), matrix[...])
+            block = block.reshape(p.S, p.L, p.R, p.X)
         for s in range(p.S):
             for l in range(p.L):
                 if first:
-                    rounded = (own[s, l] if shift == 0 else others[shift - 1, s, l]).astype(f32)
+                    rounded = block[s, l] if shift else own[s, l].astype(f32)
                 else:
                     if shift == 0:
-                        seen, index = obs[s, l], cls[s, l]
+                        seen, index = pack[0, s, l], pack[1, s, l]
                     else:
-                        seen, index = obs_in[shift - 1, s, l], code_in[shift - 1, s, l].astype(f32)
+                        seen, index = pack_in[shift - 1, 0, s, l], pack_in[shift - 1, 1, s, l]
                     threshold = table(index, huber_levels)
                     misfit = -(step * image[base + s, l]) - seen
                     clipped = jnp.where(index > 0, jnp.clip(misfit, -threshold, threshold), 0.0)
@@ -135,10 +174,10 @@
                     tile, lane = p.slot(p.K + s, l)
                     value = p.stat * static_scale[s, l] * rounded
                     scatter(back, tile, strided(lane, p.R), value)
-                    msgs[0][p.K + s * p.L + l] = value.astype(bf16)
+                    msgs[p.L - 1][p.K + s * p.L + l] = value.astype(bf16)
     if first:
         for l in range(p.L):
-            msgs[0][p.K + p.S * p.L + l] = scale_index[l].astype(f32).astype(bf16)
+            msgs[0][len(p.fields(0)) + l] = scale_index[l].astype(bf16)
     for l in range(p.L):
         for k in range(p.K):
             value = members[k, 0, l].astype(f32) * sent[0, l]
@@ -151,14 +190,11 @@
 
 
 def sideways(u, first_lane, last_lane):
-    right = [pltpu.roll(part, 1, 1) for part in u]
-    left = [pltpu.roll(part, LANES - 1, 1) for part in u]
     zero = jnp.zeros_like(u[0])
-    before, after = [zero] + right[:-1], left[1:] + [zero]
-    return [
-        jnp.where(first_lane, before[i], right[i]) + jnp.where(last_lane, after[i], left[i])
-        for i in range(len(u))
-    ]
+    before = jnp.where(first_lane, zero, pltpu.roll(u[-1], 1, 1))
+    after = jnp.where(last_lane, zero, pltpu.roll(u[0], LANES - 1, 1))
+    around = [before] + list(u) + [after]
+    return [around[i] + around[i + 2] for i in range(len(u))]
 
 
 def stencil(above, here, below, side):
@@ -174,12 +210,11 @@
         scale_index, *refs = refs
     else:
         kap, *refs = refs
-    if level:
-        rest, *refs = refs
     if not first:
         before, step, *refs = refs
     grad, norm, part, ship, *refs = refs
-    if level == 0 and p.L > 1:
+    last = level == p.L - 1
+    if last and p.L > 1:
         rest, *refs = refs
     if first and level == 0:
         kap, *refs = refs
@@ -202,7 +237,7 @@
         for l in range(p.L):
             pieces = (
                 (table(low[len(fields) + l].astype(f32)[R - H :], kappa_table) * low_ok, 0),
-                (table(scale_index[l].astype(f32), kappa_table), H),
+                (table(scale_index[l], kappa_table), H),
                 (table(high[len(fields) + l].astype(f32)[:H], kappa_table) * high_ok, H + R),
             )
             for value, offset in pieces:
@@ -227,11 +262,10 @@
         step_tile = jnp.broadcast_to(step[0:1, 0:1], (SUB, LANES))
 
     def problem(t, total):
-        if level == 0:
-            which = jnp.where(t < p.KT, 0, t - p.KT + p.L)
-            whole = jnp.where(t < p.KT, t, t - p.KT + p.PM)
-        else:
-            which, whole = level, t + level * p.KT
+        which, whole = level, t + level * p.KT
+        if last:
+            which = jnp.where(t < p.KT, level, t - p.KT + p.L)
+            whole = jnp.where(t < p.KT, whole, t - p.KT + p.PM)
         source = None
         for sweep in range(W):
             target = (a, b)[sweep % 2]
@@ -297,20 +331,23 @@
             sums[v] = term if k == 0 else sums[v] + term
     for v in range(p.V):
         part[v] = p.ens * sums[v]
-    for s in range(p.S):
-        own = me * p.S + s
-        if level:
-            part[own] = part[own] + rest[level - 1, s]
-            continue
-        for l in range(p.L):
-            tile, j = p.inner(p.K + s, l)
-            value = p.stat * static_scale[s, l] * gather(out, tile, strided(j, R))
-            if l:
-                rest[l - 1, s] = value
-            else:
-                part[own] = part[own] + value
+    if last:
+        for s in range(p.S):
+            own = me * p.S + s
+            for l in range(p.L):
+                tile, j = p.inner(p.K + s, l)
+                value = p.stat * static_scale[s, l] * gather(out, tile, strided(j, R))
+                if l == level:
+                    part[own] = part[own] + value
+                else:
+                    rest[l, s] = value
     if first:
-        ship[...] = part[...].astype(bf16)
+        for v in range(p.V):
+            ship[v] = part[v].astype(bf16)
+        if last:
+            for l in range(p.L - 1):
+                for s in range(p.S):
+                    ship[p.V + l * p.S + s] = rest[l, s].astype(bf16)
         return
     for shift in range(1, p.mem):
         base = lax.rem(me + shift, p.mem) * p.S
@@ -320,10 +357,12 @@
 
 def curvature_kernel(p, first, *refs):
     parts, gots, norms, refs = refs[: p.L], refs[p.L : 2 * p.L], refs[2 * p.L : 3 * p.L], refs[3 * p.L :]
+    if p.L > 1:
+        rest, *refs = refs
     if first:
-        obs, cls, _, _, image, send = refs
+        pack, _, image, send = refs
     else:
-        obs, cls, image_before, step, image, send = refs
+        pack, image_before, step, image, send = refs
     me = lax.axis_index("mem")
     total = jnp.zeros((p.R, p.X), f32)
     for l in range(p.L):
@@ -333,18 +372,28 @@
                 for other in range(p.mem - 1):
                     value = value + gots[l][other, v].astype(f32)
                 image[v, l] = value
+            if l < p.L - 1:
+                for s in range(p.S):
+                    own = me * p.S + s
+                    image[own, l] = image[own, l] + rest[l, s]
+                    for other in range(p.mem - 1):
+                        theirs = lax.rem(me + (p.mem - 1 - other), p.mem) * p.S + s
+                        value = gots[p.L - 1][other, p.V + l * p.S + s].astype(f32)
+                        image[theirs, l] = image[theirs, l] + value
         for s in range(p.S):
             own = me * p.S + s
             if first:
                 value = image[own, l]
-                misfit = -obs[s, l]
+                misfit = -pack[0, s, l]
             else:
                 value = parts[l][own]
+                if l < p.L - 1:
+                    value = value + rest[l, s]
                 for other in range(p.mem - 1):
                     value = value + gots[l][other, s].astype(f32)
                 image[s, l] = value
-                misfit = -(step[0:1, 0:1] * image_before[own, l]) - obs[s, l]
-            index = cls[s, l]
+                misfit = -(step[0:1, 0:1] * image_before[own, l]) - pack[0, s, l]
+            index = pack[1, s, l]
             threshold = table(index, huber_levels)
             weight = jnp.where(index > 0, threshold / jnp.maximum(jnp.abs(misfit), threshold), 0.0)
             total = total + weight * value * value
@@ -354,7 +403,7 @@
     send[...] = jnp.broadcast_to(jnp.concatenate([norm, total], axis=1)[None], send.shape)
 
 
-def final_kernel(p, got, step, image0, image1, *refs):
+def final_kernel(p, got, step, image0, image1, matrix_ref, *refs):
     before, after, outs = refs[: p.L], refs[p.L : 2 * p.L], refs[2 * p.L :]
     control, static_control, increment = outs
     me = lax.axis_index("mem")
@@ -363,18 +412,30 @@
     curvature = jnp.sum(total[:, LANES:], axis=1, keepdims=True)
     second = norm / (norm + curvature)
     first = step[0:1, 0:1]
+    matrix = matrix_ref[...]
+
+    def natural(blocks):
+        whole = exact(jnp.concatenate(blocks, axis=0), matrix, True)
+        return [whole[i * p.R : (i + 1) * p.R] for i in range(len(blocks))]
+
     for level in range(p.L):
-        for field, l in p.fields(level):
-            tile, lane = p.inner(field, l)
-            where = strided(SWEEPS * SUB + lane, p.R)
-            value = -(first * gather(before[level], tile, where)) - second * gather(after[level], tile, where)
-            if field < p.K:
-                control[field, l] = value
-            else:
-                static_control[field - p.K, l] = value
-    for s in range(p.S):
-        for l in range(p.L):
-            increment[s, l] = -(first * image0[me * p.S + s, l]) - second * image1[s, l]
+        fields = p.fields(level)
+        for begin in range(0, len(fields), 8):
+            some = fields[begin : begin + 8]
+            blocks = []
+            for field, l in some:
+                tile, lane = p.inner(field, l)
+                where = strided(SWEEPS * SUB + lane, p.R)
+                blocks.append(-(first * gather(before[level], tile, where)) - second * gather(after[level], tile, where))
+            for (field, l), value in zip(some, natural(blocks)):
+                if field < p.K:
+                    control[field, l] = value
+                else:
+                    static_control[field - p.K, l] = value
+    some = [(s, l) for s in range(p.S) for l in range(p.L)]
+    blocks = [-(first * image0[me * p.S + s, l]) - second * image1[s, l] for s, l in some]
+    for (s, l), value in zip(some, natural(blocks)):
+        increment[s, l] = value
 
 
 def call(kernel, outs, scratch, far=0, cost=0):
@@ -415,19 +476,18 @@
     send_shape = ((p.devices, 1, 2 * LANES), f32)
     line = ((1, LANES), f32)
 
-    obs, cls, own, code = call(
-        part(load_kernel, p),
-        [(own_shape, f32), (own_shape, jnp.int32), (own_shape, bf16), (own_shape, bf16)],
+    obs, cls, own = call(
+        part(load_kernel, p), [(own_shape, f32), (own_shape, jnp.int32), (own_shape, bf16)],
         [pltpu.SemaphoreType.DMA((2,))], far=2,
     )(observed, huber_class)
     others = jnp.stack([round_mem(own, shift) for shift in shifts])
-    members, static_scale, scale_index = call(
-        fetch_kernel,
-        [(x.shape, x.dtype) for x in (members, static_scale, scale_index)],
-        [pltpu.SemaphoreType.DMA((3,))], far=3, cost=4 << 20,
-    )(members, static_scale, scale_index, own)
-    obs_in = jnp.stack([round_mem(obs, shift) for shift in shifts])
-    code_in = jnp.stack([round_mem(code, shift) for shift in shifts])
+    scratch = [pltpu.VMEM(x.shape, x.dtype) for x in (members, static_scale, scale_index)]
+    members, static_scale, scale_index, pack, own, matrix = call(
+        part(fetch_kernel, p),
+        [(members.shape, bf16), (own_shape, f32), ((L, R, X), f32), ((2,) + own_shape, f32), (own_shape, bf16), ((X, X), bf16)],
+        scratch + [pltpu.SemaphoreType.DMA((K + 2,))], far=3, cost=4 << 20,
+    )(members, static_scale, scale_index, obs, cls, own)
+    pack_in = jnp.stack([round_mem(pack, shift) for shift in shifts])
 
     grads, image, step, kap, sums = [], None, None, None, None
     for turn in range(ITERS):
@@ -439,22 +499,26 @@
         if first:
             back, *msgs = call(
                 part(back_kernel, p, True), [(back_shape, f32)] + msg_shapes, [vmem(full_shape)],
-            )(members, static_scale, scale_index, own, others)
+            )(members, static_scale, scale_index, own, others, matrix)
         else:
             back, step, *msgs = call(
                 part(back_kernel, p, False), [(back_shape, f32), line] + msg_shapes, [vmem(full_shape)],
-            )(members, static_scale, obs, cls, obs_in, code_in, image, sums)
-        halos = [(round_row(msg, 1), round_row(msg, p.row - 1)) for msg in msgs]
+            )(members, static_scale, pack, pack_in, image, sums)
+        halos = []
+        for msg in msgs:
+            low = round_row(msg, 1)
+            high = round_row(msg, p.row - 1)
+            halos.append((low, high))
         grad, norms, partial_images, gots, rest = [], [], [], [], None
         for level in range(L):
             count = p.tiles(level)
             args = [members, static_scale, back, *halos[level]]
             args += [scale_index] if first and level == 0 else [kap]
-            args += [rest] if level else []
             args += [] if first else [grads[0][level], step]
-            ship_shape = (V, R, X) if first else (p.mem - 1, S, R, X)
+            last = level == L - 1
+            ship_shape = (V + (L - 1) * S if last else V, R, X) if first else (p.mem - 1, S, R, X)
             outs = [((count, C, p.RG * SUB, LANES), f32), line, ((V, R, X), f32), (ship_shape, bf16)]
-            if level == 0 and L > 1:
+            if last and L > 1:
                 outs.append(((L - 1, S, R, X), f32))
             if first and level == 0:
                 outs.append(((L + p.ST, C, p.RE * SUB, LANES), f32))
@@ -464,7 +528,7 @@
                 part(sweep_kernel, p, first, level), outs, work + [vmem((count, C, R * SUB, LANES))],
                 cost=8 << 20,
             )(*args)
-            if level == 0 and L > 1:
+            if last and L > 1:
                 rest, *more = more
             if first and level == 0:
                 kap = more[0]
@@ -473,19 +537,20 @@
             partial_images.append(partial_image)
             gots.append(jnp.stack([round_mem(ship if first else ship[shift - 1], shift) for shift in shifts]))
         grads.append(grad)
+        extra = [rest] if L > 1 else []
         if first:
             image, send = call(
                 part(curvature_kernel, p, True), [(full_shape, f32), send_shape], [],
-            )(*partial_images, *gots, *norms, obs, cls, obs_in, code_in)
+            )(*partial_images, *gots, *norms, *extra, pack, pack_in)
         else:
-            last, send = call(
+            final_image, send = call(
                 part(curvature_kernel, p, False), [(own_shape, f32), send_shape], [],
-            )(*partial_images, *gots, *norms, obs, cls, image, step)
+            )(*partial_images, *gots, *norms, *extra, pack, image, step)
         sums = lax.all_to_all(send, ("mem", "row"), 0, 0)
     return call(
         part(final_kernel, p),
         [((K, L, R, X), f32), (own_shape, f32), (own_shape, f32)], [],
-    )(sums, step, image, last, *grads[0], *grads[1])
+    )(sums, step, image, final_image, matrix, *grads[0], *grads[1])
 
 
 def solution(mesh):

time: 73.7 us -> 82.4 us (1.12)
  Pallas kernels: 18.3 us -> 21.6 us
  starting transfers between devices: 21.9 us -> 25.2 us
  blocking collectives: 20.8 us -> 22.4 us
    ppermute x8, starting transfers between devices: 12.6 us -> 17.9 us  [round_row(): lax.ppermute(block, 'row', [(i, (i + shift) % p.row) for i in range(p.row)])]
    pallas_call x11, Pallas kernels: 18.3 us -> 21.6 us  [run(): pl.pallas_call(kernel, out_shape=tuple((jax.ShapeDtypeStruct(shape, dtype...]
    ppermute x7 -> x6, starting transfers between devices: 9.27 us -> 7.33 us  [round_mem(): lax.ppermute(block, 'mem', [(i, (i + shift) % p.mem) for i in range(p.mem)])]
    all_to_all x2, blocking collectives: 20.8 us -> 22.4 us  [local(): sums = lax.all_to_all(send, ('mem', 'row'), 0, 0)]
    ppermute x7 -> x6, waiting for transfers between devices: 6.81 us -> 6.72 us  [round_mem(): lax.ppermute(block, 'mem', [(i, (i + shift) % p.mem) for i in range(p.mem)])]
  transfers between devices with their start and end apart: 15 -> 14, of which waited for: 7 -> 4; matrix products, arithmetic and copies ran while one was open for 0% -> 0% of each run, Pallas kernels for 16% -> 18%
where the time goes in v5:
time: 82.4 us; the launch traced here: 82.2 us
  starting transfers between devices  25.2 us (31%)
  blocking collectives  22.4 us (27%)
  Pallas kernels  21.6 us (26%)
  waiting for transfers between devices  12.3 us (15%)
    all_to_all x2, blocking collectives, local(): sums = lax.all_to_all(send, ('mem', 'row'), 0, 0)  22.4 us
    pallas_call x11, Pallas kernels, run(): pl.pallas_call(kernel, out_shape=tuple((jax.ShapeDtypeStruct(shape, dtype...  21.6 us
    ppermute x8, starting transfers between devices, round_row(): lax.ppermute(block, 'row', [(i, (i + shift) % p.row) for i in range(p.row)])  17.9 us
    ppermute x6, starting transfers between devices, round_mem(): lax.ppermute(block, 'mem', [(i, (i + shift) % p.mem) for i in range(p.mem)])  7.33 us
    ppermute x6, waiting for transfers between devices, round_mem(): lax.ppermute(block, 'mem', [(i, (i + shift) % p.mem) for i in range(p.mem)])  6.72 us
    ppermute x8, waiting for transfers between devices, round_row(): lax.ppermute(block, 'row', [(i, (i + shift) % p.row) for i in range(p.row)])  5.58 us
  transfers between devices with their start and end apart: 14, of which 4 were waited for; matrix products, arithmetic and copies ran while one was open for 0% of the time, Pallas kernels for 18%

profile of v5, /device:TPU:0, one launch (start us, length us, event | category | flops | bytes accessed | tf_op | source)
XLA Modules:
  0.0 82.2 jit_solution(11425225481693134667)
XLA Ops:
  0.6 1.0 %shard_map.76 = (f32[4,2,8,512]{3,2,1,0:T(8,128)S(1)}, s32[4,2,8,512]{3,2,1,0:T(8,128)S(1)}, bf16[4,2,8,512]{3,2,1,0:T(8,128)(2,1)S(1)}) custom-call(f32[4,2,8,512]{3,2,1,0:T(8,128)} %obs.1, s32[4,2,8,512]{3,2,1,0:T(8,128)} %cls.1), custom_call_target="tpu_custom_call" | custom-call | tf_op jit(solution)/shard_map/pallas_call | solution.py:446
  1.7 3.1 %collective-permute-start.1 = (bf16[4,2,8,512]{3,2,1,0:T(8,128)(2,1)S(1)}, bf16[4,2,8,512]{3,2,1,0:T(8,128)(2,1)S(1)}, u32[]{:S(2)}, u32[]{:S(2)}) collective-permute-start(bf16[4,2,8,512]{3,2,1,0:T(8,128)(2,1)S(1)} %get-tuple-element.44.own), channel_id=1, source_target_pairs={{0,16},{16,0},{1,17},{17,1},{2,18},{18,2},{3,19},{19,3},{4,20},{20... | collective-permute-start | bytes 196616 | tf_op jit(solution)/shard_map/ppermute | solution.py:465
  4.7 6.3 %shard_map.77 = (bf16[16,8,2,8,512]{4,3,2,1,0:T(8,128)(2,1)S(1)}, f32[4,2,8,512]{3,2,1,0:T(8,128)S(1)}, f32[2,8,512]{2,1,0:T(8,128)S(1)}, f32[2,4,2,8,512]{4,3,2...) custom-call(bf16[16,8,2,8,512]{4,3,2,1,0:T(8,128)(2,1)} %members.1, ...), custom_call_target="tpu_custom_call" | custom-call | flops 4194304 | bytes 4194304 | tf_op jit(solution)/shard_map/pallas_call | solution.py:446
  11.1 0.0 collective-permute-done.1
  11.1 0.8 %shard_map.78 = (f32[5,4,64,128]{3,2,1,0:T(8,128)S(1)}, bf16[18,8,512]{2,1,0:T(8,128)(2,1)S(1)}, bf16[24,8,512]{2,1,0:T(8,128)(2,1)S(1)}) custom-call(bf16[16,8,2,8,512]{4,3,2,1,0:T(8,128)(2,1)S(1)} %get-tuple-element.45.refs_0_, f32[4,2,8,512]{3,2,1,0:T(8,128)S(1)} %get-tuple-element.46.refs_1_, f32[2,8,512]{2,1,0:T(8,128)S(1)} %get-tuple-element.48.refs_2_.refs_5_, ...), custom_call_target="tpu_custom_call" | custom-call | tf_op jit(solution)/shard_map/pallas_call | solution.py:446
  11.9 0.1 collective-permute-start.4
  12.0 4.4 %collective-permute-start.5 = (bf16[24,8,512]{2,1,0:T(8,128)(2,1)S(1)}, bf16[24,8,512]{2,1,0:T(8,128)(2,1)S(1)}, u32[]{:S(2)}, u32[]{:S(2)}) collective-permute-start(bf16[24,8,512]{2,1,0:T(8,128)(2,1)S(1)} %get-tuple-element.54), channel_id=1, source_target_pairs={{0,15},{1,0},{2,1},{3,2},{4,3},{5,4},{6,5},{7,6},{8,7},{9,8},{10,9... | collective-permute-start | bytes 589832 | tf_op jit(solution)/shard_map/ppermute | solution.py:468
  16.4 0.0 collective-permute-start
  16.4 0.0 collective-permute-start.2
  16.4 4.4 %collective-permute-start.3 = (bf16[18,8,512]{2,1,0:T(8,128)(2,1)S(1)}, bf16[18,8,512]{2,1,0:T(8,128)(2,1)S(1)}, u32[]{:S(2)}, u32[]{:S(2)}) collective-permute-start(bf16[18,8,512]{2,1,0:T(8,128)(2,1)S(1)} %get-tuple-element.52), channel_id=1, source_target_pairs={{0,15},{1,0},{2,1},{3,2},{4,3},{5,4},{6,5},{7,6},{8,7},{9,8},{10,9... | collective-permute-start | bytes 442376 | tf_op jit(solution)/shard_map/ppermute | solution.py:468
  20.9 2.9 %collective-permute-done.2.refs_3_ = bf16[18,8,512]{2,1,0:T(8,128)(2,1)S(1)} collective-permute-done((bf16[18,8,512]{2,1,0:T(8,128)(2,1)S(1)}, bf16[18,8,512]{2,1,0:T(8,128)(2,1)S(1)}, u32[]{:S(2)}, u32[]{:S(2)}) %collective-permute-start.2) | collective-permute-done | bytes 147488 | tf_op jit(solution)/shard_map/ppermute | solution.py:468
  23.8 0.0 collective-permute-done.3.refs_4_
  23.8 1.8 %shard_map.79 = (f32[2,4,128,128]{3,2,1,0:T(8,128)S(1)}, f32[1,128]{1,0:T(1,128)S(1)}, f32[8,8,512]{2,1,0:T(8,128)S(1)}, bf16[8,8,512]{2,1,0:T(8,128)(2,1)S(1)}, f32[3,4,192,128]{3,2,1,0:T(8,128)S(1)}) custom-call(bf16[16,8,2,8,512]{4,3,2,1,0:T(8,128)(2,1)S(1)} %get-tuple-element.45.refs_0_, f32[4,2,8,512]{3,2,1,0:T(8,128)S(1)} %get-tuple-element.46.refs_1_, ...), custom_call_target="tpu_custom_call" | custom-call | flops 8388608 | bytes 8388608 | tf_op jit(solution)/shard_map/pallas_call | solution.py:446
  25.7 0.0 collective-permute-done.4.refs_3_
  25.7 0.0 collective-permute-done.5.refs_4_
  25.7 2.5 %shard_map.80 = (f32[3,4,128,128]{3,2,1,0:T(8,128)S(1)}, f32[1,128]{1,0:T(1,128)S(1)}, f32[8,8,512]{2,1,0:T(8,128)S(1)}, bf16[12,8,512]{2,1,0:T(8,128)(2,1)S(1)}, f32[1,4,8,512]{3,2,1,0:T(8,128)S(1)}) custom-call(bf16[16,8,2,8,512]{4,3,2,1,0:T(8,128)(2,1)S(1)} %get-tuple-element.45.refs_0_, f32[4,2,8,512]{3,2,1,0:T(8,128)S(1)} %get-tuple-element.46.refs_1_, ...), custom_call_target="tpu_custom_call" | custom-call | flops 8388608 | bytes 8388608 | tf_op jit(solution)/shard_map/pallas_call | solution.py:446
  28.2 2.0 %collective-permute-start.7 = (bf16[12,8,512]{2,1,0:T(8,128)(2,1)S(1)}, bf16[12,8,512]{2,1,0:T(8,128)(2,1)S(1)}, u32[]{:S(2)}, u32[]{:S(2)}) collective-permute-start(bf16[12,8,512]{2,1,0:T(8,128)(2,1)S(1)} %get-tuple-element.58), channel_id=1, source_target_pairs={{0,16},{16,0},{1,17},{17,1},{2,18},{18,2},{3,19},{19,3},{4,20},{20... | collective-permute-start | bytes 294920 | tf_op jit(solution)/shard_map/ppermute | solution.py:465
  30.2 0.1 collective-permute-start.6
  30.3 0.0 collective-permute-done
  30.3 4.2 %collective-permute-done.6 = bf16[8,8,512]{2,1,0:T(8,128)(2,1)S(1)} collective-permute-done((bf16[8,8,512]{2,1,0:T(8,128)(2,1)S(1)}, bf16[8,8,512]{2,1,0:T(8,128)(2,1)S(1)}, u32[]{:S(2)}, u32[]{:S(2)}) %collective-permute-start.6) | collective-permute-done | bytes 65568 | tf_op jit(solution)/shard_map/ppermute | solution.py:465
  34.5 0.0 collective-permute-done.7
  34.5 0.1 shard_map.81
  34.7 11.1 %all_to_all.10.refs_5_ = f32[32,1,256]{2,1,0:T(1,128)S(1)} all-to-all(f32[32,1,256]{2,1,0:T(1,128)S(1)} %get-tuple-element.63), channel_id=1, replica_groups=mesh['mem'=2,'row'=16] {'mem','row'}, dimensions={0} | all-to-all | bytes 65536 | tf_op jit(solution)/shard_map/all_to_all | solution.py:549
  45.8 0.7 shard_map.82
  46.5 0.2 collective-permute-start.10
  46.7 4.3 %collective-permute-start.11 = (bf16[24,8,512]{2,1,0:T(8,128)(2,1)S(1)}, bf16[24,8,512]{2,1,0:T(8,128)(2,1)S(1)}, u32[]{:S(2)}, u32[]{:S(2)}) collective-permute-start(bf16[24,8,512]{2,1,0:T(8,128)(2,1)S(1)} %get-tuple-element.69), channel_id=1, source_target_pairs={{0,15},{1,0},{2,1},{3,2},{4,3},{5,4},{6,5},{7,6},{8,7},{9,8},{10,9... | collective-permute-start | bytes 589832 | tf_op jit(solution)/shard_map/ppermute | solution.py:468
  51.0 0.0 collective-permute-start.8
  51.0 4.4 %collective-permute-start.9 = (bf16[16,8,512]{2,1,0:T(8,128)(2,1)S(1)}, bf16[16,8,512]{2,1,0:T(8,128)(2,1)S(1)}, u32[]{:S(2)}, u32[]{:S(2)}) collective-permute-start(bf16[16,8,512]{2,1,0:T(8,128)(2,1)S(1)} %get-tuple-element.65), channel_id=1, source_target_pairs={{0,15},{1,0},{2,1},{3,2},{4,3},{5,4},{6,5},{7,6},{8,7},{9,8},{10,9... | collective-permute-start | bytes 393224 | tf_op jit(solution)/shard_map/ppermute | solution.py:468
  55.4 2.6 %collective-permute-done.8.refs_3_ = bf16[16,8,512]{2,1,0:T(8,128)(2,1)S(1)} collective-permute-done((bf16[16,8,512]{2,1,0:T(8,128)(2,1)S(1)}, bf16[16,8,512]{2,1,0:T(8,128)(2,1)S(1)}, u32[]{:S(2)}, u32[]{:S(2)}) %collective-permute-start.8) | collective-permute-done | bytes 131104 | tf_op jit(solution)/shard_map/ppermute | solution.py:468
  58.1 0.0 collective-permute-done.9.refs_4_
  58.1 1.8 %shard_map.83 = (f32[2,4,128,128]{3,2,1,0:T(8,128)S(1)}, f32[1,128]{1,0:T(1,128)S(1)}, f32[8,8,512]{2,1,0:T(8,128)S(1)}, bf16[1,4,8,512]{3,2,1,0:T(8,128)(2,1)S(1)}) custom-call(bf16[16,8,2,8,512]{4,3,2,1,0:T(8,128)(2,1)S(1)} %get-tuple-element.45.refs_0_, f32[4,2,8,512]{3,2,1,0:T(8,128)S(1)} %get-tuple-element.46.refs_1_, ...), custom_call_target="tpu_custom_call" | custom-call | flops 8388608 | bytes 8388608 | tf_op jit(solution)/shard_map/pallas_call | solution.py:446
  59.9 0.7 collective-permute-start.12
  60.5 0.0 collective-permute-done.10.refs_3_
  60.6 0.0 collective-permute-done.11.refs_4_
  60.6 2.5 %shard_map.84 = (f32[3,4,128,128]{3,2,1,0:T(8,128)S(1)}, f32[1,128]{1,0:T(1,128)S(1)}, f32[8,8,512]{2,1,0:T(8,128)S(1)}, bf16[1,4,8,512]{3,2,1,0:T(8,128)(2,1)S(1)}, f32[1,4,8,512]{3,2,1,0:T(8,128)S(1)}) custom-call(bf16[16,8,2,8,512]{4,3,2,1,0:T(8,128)(2,1)S(1)} %get-tuple-element.45.refs_0_, f32[4,2,8,512]{3,2,1,0:T(8,128)S(1)} %get-tuple-element.46.refs_1_, ...), custom_call_target="tpu_custom_call" | custom-call | flops 8388608 | bytes 8388608 | tf_op jit(solution)/shard_map/pallas_call | solution.py:446
  63.1 1.5 %collective-permute-start.13 = (bf16[4,8,512]{2,1,0:T(8,128)(2,1)S(1)}, bf16[4,8,512]{2,1,0:T(8,128)(2,1)S(1)}, u32[]{:S(2)}, u32[]{:S(2)}) collective-permute-start(bf16[4,8,512]{2,1,0:T(8,128)(2,1)S(1)} %bitcast.16), channel_id=1, source_target_pairs={{0,16},{16,0},{1,17},{17,1},{2,18},{18,2},{3,19},{19,3},{4,20},{20... | collective-permute-start | bytes 98312 | tf_op jit(solution)/shard_map/ppermute | solution.py:465
  64.6 0.0 collective-permute-done.12
  64.6 2.5 %collective-permute-done.13 = bf16[4,8,512]{2,1,0:T(8,128)(2,1)S(1)} collective-permute-done((bf16[4,8,512]{2,1,0:T(8,128)(2,1)S(1)}, bf16[4,8,512]{2,1,0:T(8,128)(2,1)S(1)}, u32[]{:S(2)}, u32[]{:S(2)}) %collective-permute-start.13) | collective-permute-done | bytes 32800 | tf_op jit(solution)/shard_map/ppermute | solution.py:465
  67.1 0.2 shard_map.85
  67.2 11.3 %all_to_all.11.got = f32[32,1,256]{2,1,0:T(1,128)S(1)} all-to-all(f32[32,1,256]{2,1,0:T(1,128)S(1)} %get-tuple-element.77), channel_id=1, replica_groups=mesh['mem'=2,'row'=16] {'mem','row'}, dimensions={0} | all-to-all | bytes 65536 | tf_op jit(solution)/shard_map/all_to_all | solution.py:549
  78.5 3.7 %shard_map.86 = (f32[16,2,8,512]{3,2,1,0:T(8,128)}, f32[4,2,8,512]{3,2,1,0:T(8,128)}, f32[4,2,8,512]{3,2,1,0:T(8,128)}) custom-call(f32[32,1,256]{2,1,0:T(1,128)S(1)} %all_to_all.11.got, f32[1,128]{1,0:T(1,128)S(1)} %get-tuple-element.67.refs_7_.refs_9_.step, f32[8,2,8,512]{3,2,1,0:T(8,128)S(1)} %get-tuple-element.62.refs_4_.refs_8_.image0, ...), custom_call_target="tpu_custom_call" | custom-call | tf_op jit(solution)/shard_map/pallas_call | solution.py:446
Async XLA Ops:
  1.7 9.4 %collective-permute-start.1 = (bf16[4,2,8,512]{3,2,1,0:T(8,128)(2,1)S(1)}, bf16[4,2,8,512]{3,2,1,0:T(8,128)(2,1)S(1)}, u32[]{:S(2)}, u32[]{:S(2)}) collective-permute-start(bf16[4,2,8,512]{3,2,1,0:T(8,128)(2,1)S(1)} %get-tuple-element.44.own), channel_id=1, source_target_pairs={{0,16},{16,0},{1,17},{17,1},{2,18},{18,2},{3,19},{19,3},{4,20},{20... | collective-permute-start | bytes 196616 | tf_op jit(solution)/shard_map/ppermute | solution.py:465
  11.9 13.7 %collective-permute-start.4 = (bf16[24,8,512]{2,1,0:T(8,128)(2,1)S(1)}, bf16[24,8,512]{2,1,0:T(8,128)(2,1)S(1)}, u32[]{:S(2)}, u32[]{:S(2)}) collective-permute-start(bf16[24,8,512]{2,1,0:T(8,128)(2,1)S(1)} %get-tuple-element.54), channel_id=1, source_target_pairs={{0,1},{1,2},{2,3},{3,4},{4,5},{5,6},{6,7},{7,8},{8,9},{9,10},{10,1... | collective-permute-start | bytes 589832 | tf_op jit(solution)/shard_map/ppermute | solution.py:468
  12.0 13.7 %collective-permute-start.5 = (bf16[24,8,512]{2,1,0:T(8,128)(2,1)S(1)}, bf16[24,8,512]{2,1,0:T(8,128)(2,1)S(1)}, u32[]{:S(2)}, u32[]{:S(2)}) collective-permute-start(bf16[24,8,512]{2,1,0:T(8,128)(2,1)S(1)} %get-tuple-element.54), channel_id=1, source_target_pairs={{0,15},{1,0},{2,1},{3,2},{4,3},{5,4},{6,5},{7,6},{8,7},{9,8},{10,9... | collective-permute-start | bytes 589832 | tf_op jit(solution)/shard_map/ppermute | solution.py:468
  16.4 13.9 %collective-permute-start = (f32[2,4,2,8,512]{4,3,2,1,0:T(8,128)S(1)}, f32[2,4,2,8,512]{4,3,2,1,0:T(8,128)S(1)}, u32[]{:S(2)}, u32[]{:S(2)}) collective-permute-start(f32[2,4,2,8,512]{4,3,2,1,0:T(8,128)S(1)} %get-tuple-element.47.refs_7_.refs_2_), channel_id=1, source_target_pairs={{0,16},{16,0},{1,17},{17,1},{2,18},{18,2},{3,19},{19,3},{4,20},{20... | collective-permute-start | bytes 786440 | tf_op jit(solution)/shard_map/ppermute | solution.py:465
  16.4 7.4 %collective-permute-start.2 = (bf16[18,8,512]{2,1,0:T(8,128)(2,1)S(1)}, bf16[18,8,512]{2,1,0:T(8,128)(2,1)S(1)}, u32[]{:S(2)}, u32[]{:S(2)}) collective-permute-start(bf16[18,8,512]{2,1,0:T(8,128)(2,1)S(1)} %get-tuple-element.52), channel_id=1, source_target_pairs={{0,1},{1,2},{2,3},{3,4},{4,5},{5,6},{6,7},{7,8},{8,9},{9,10},{10,1... | collective-permute-start | bytes 442376 | tf_op jit(solution)/shard_map/ppermute | solution.py:468
  16.4 7.4 %collective-permute-start.3 = (bf16[18,8,512]{2,1,0:T(8,128)(2,1)S(1)}, bf16[18,8,512]{2,1,0:T(8,128)(2,1)S(1)}, u32[]{:S(2)}, u32[]{:S(2)}) collective-permute-start(bf16[18,8,512]{2,1,0:T(8,128)(2,1)S(1)} %get-tuple-element.52), channel_id=1, source_target_pairs={{0,15},{1,0},{2,1},{3,2},{4,3},{5,4},{6,5},{7,6},{8,7},{9,8},{10,9... | collective-permute-start | bytes 442376 | tf_op jit(solution)/shard_map/ppermute | solution.py:468
  28.2 6.3 %collective-permute-start.7 = (bf16[12,8,512]{2,1,0:T(8,128)(2,1)S(1)}, bf16[12,8,512]{2,1,0:T(8,128)(2,1)S(1)}, u32[]{:S(2)}, u32[]{:S(2)}) collective-permute-start(bf16[12,8,512]{2,1,0:T(8,128)(2,1)S(1)} %get-tuple-element.58), channel_id=1, source_target_pairs={{0,16},{16,0},{1,17},{17,1},{2,18},{18,2},{3,19},{19,3},{4,20},{20... | collective-permute-start | bytes 294920 | tf_op jit(solution)/shard_map/ppermute | solution.py:465
  30.2 4.3 %collective-permute-start.6 = (bf16[8,8,512]{2,1,0:T(8,128)(2,1)S(1)}, bf16[8,8,512]{2,1,0:T(8,128)(2,1)S(1)}, u32[]{:S(2)}, u32[]{:S(2)}) collective-permute-start(bf16[8,8,512]{2,1,0:T(8,128)(2,1)S(1)} %get-tuple-element.57), channel_id=1, source_target_pairs={{0,16},{16,0},{1,17},{17,1},{2,18},{18,2},{3,19},{19,3},{4,20},{20... | collective-permute-start | bytes 196616 | tf_op jit(solution)/shard_map/ppermute | solution.py:465
  46.5 14.0 %collective-permute-start.10 = (bf16[24,8,512]{2,1,0:T(8,128)(2,1)S(1)}, bf16[24,8,512]{2,1,0:T(8,128)(2,1)S(1)}, u32[]{:S(2)}, u32[]{:S(2)}) collective-permute-start(bf16[24,8,512]{2,1,0:T(8,128)(2,1)S(1)} %get-tuple-element.69), channel_id=1, source_target_pairs={{0,1},{1,2},{2,3},{3,4},{4,5},{5,6},{6,7},{7,8},{8,9},{9,10},{10,1... | collective-permute-start | bytes 589832 | tf_op jit(solution)/shard_map/ppermute | solution.py:468
  46.7 13.9 %collective-permute-start.11 = (bf16[24,8,512]{2,1,0:T(8,128)(2,1)S(1)}, bf16[24,8,512]{2,1,0:T(8,128)(2,1)S(1)}, u32[]{:S(2)}, u32[]{:S(2)}) collective-permute-start(bf16[24,8,512]{2,1,0:T(8,128)(2,1)S(1)} %get-tuple-element.69), channel_id=1, source_target_pairs={{0,15},{1,0},{2,1},{3,2},{4,3},{5,4},{6,5},{7,6},{8,7},{9,8},{10,9... | collective-permute-start | bytes 589832 | tf_op jit(solution)/shard_map/ppermute | solution.py:468
  51.0 7.1 %collective-permute-start.8 = (bf16[16,8,512]{2,1,0:T(8,128)(2,1)S(1)}, bf16[16,8,512]{2,1,0:T(8,128)(2,1)S(1)}, u32[]{:S(2)}, u32[]{:S(2)}) collective-permute-start(bf16[16,8,512]{2,1,0:T(8,128)(2,1)S(1)} %get-tuple-element.65), channel_id=1, source_target_pairs={{0,1},{1,2},{2,3},{3,4},{4,5},{5,6},{6,7},{7,8},{8,9},{9,10},{10,1... | collective-permute-start | bytes 393224 | tf_op jit(solution)/shard_map/ppermute | solution.py:468
  51.0 7.1 %collective-permute-start.9 = (bf16[16,8,512]{2,1,0:T(8,128)(2,1)S(1)}, bf16[16,8,512]{2,1,0:T(8,128)(2,1)S(1)}, u32[]{:S(2)}, u32[]{:S(2)}) collective-permute-start(bf16[16,8,512]{2,1,0:T(8,128)(2,1)S(1)} %get-tuple-element.65), channel_id=1, source_target_pairs={{0,15},{1,0},{2,1},{3,2},{4,3},{5,4},{6,5},{7,6},{8,7},{9,8},{10,9... | collective-permute-start | bytes 393224 | tf_op jit(solution)/shard_map/ppermute | solution.py:468
  59.9 4.7 %collective-permute-start.12 = (bf16[4,8,512]{2,1,0:T(8,128)(2,1)S(1)}, bf16[4,8,512]{2,1,0:T(8,128)(2,1)S(1)}, u32[]{:S(2)}, u32[]{:S(2)}) collective-permute-start(bf16[4,8,512]{2,1,0:T(8,128)(2,1)S(1)} %bitcast.15), channel_id=1, source_target_pairs={{0,16},{16,0},{1,17},{17,1},{2,18},{18,2},{3,19},{19,3},{4,20},{20... | collective-permute-start | bytes 98312 | tf_op jit(solution)/shard_map/ppermute | solution.py:465
  63.1 4.0 %collective-permute-start.13 = (bf16[4,8,512]{2,1,0:T(8,128)(2,1)S(1)}, bf16[4,8,512]{2,1,0:T(8,128)(2,1)S(1)}, u32[]{:S(2)}, u32[]{:S(2)}) collective-permute-start(bf16[4,8,512]{2,1,0:T(8,128)(2,1)S(1)} %bitcast.16), channel_id=1, source_target_pairs={{0,16},{16,0},{1,17},{17,1},{2,18},{18,2},{3,19},{19,3},{4,20},{20... | collective-permute-start | bytes 98312 | tf_op jit(solution)/shard_map/ppermute | solution.py:465

commit v6 on v5

--- a/solution.py
+++ b/solution.py
@@ -87,12 +87,24 @@
     return lax.dot_general(block, matrix, dims, preferred_element_type=f32)
 
 
-def exact(block, matrix, back=False):
+def pieces(block):
     first = block.astype(bf16)
     left = block - first.astype(f32)
     second = left.astype(bf16)
-    third = (left - second.astype(f32)).astype(bf16)
-    return product(first, matrix, back) + (product(second, matrix, back) + product(third, matrix, back))
+    return [first, second, (left - second.astype(f32)).astype(bf16)]
+
+
+def products(blocks, matrix, back=False):
+    parts = [pieces(block) if block.dtype == f32 else [block] for block in blocks]
+    flat = [one for part in parts for one in part]
+    whole = product(jnp.concatenate(flat, axis=0), matrix, back)
+    out, at = [], 0
+    for part in parts:
+        rows = part[0].shape[0]
+        cut = [whole[at + i * rows : at + (i + 1) * rows] for i in range(len(part))]
+        out.append(cut[0] if len(cut) == 1 else cut[0] + (cut[1] + cut[2]))
+        at += rows * len(part)
+    return out
 
 
 def load_kernel(p, obs, cls, obs_out, cls_out, sent, sems):
@@ -122,19 +134,26 @@
     matrix_out[...] = onehot(p)
     matrix = matrix_out[...]
     rows = p.S * p.L * p.R
-    own_out[...] = product(own[...].reshape(rows, p.X), matrix).astype(bf16).reshape(own_out.shape)
     shape = (p.S, p.L, p.R, p.X)
-    pack[0] = exact(obs[...].reshape(rows, p.X), matrix).reshape(shape)
-    pack[1] = product(cls[...].astype(f32).astype(bf16).reshape(rows, p.X), matrix).reshape(shape)
+    flat = lambda x: x.reshape(rows, p.X)
     for copy in rest:
         copy.wait()
-    static_out[...] = exact(static_raw[...].reshape(rows, p.X), matrix).reshape(shape)
     scale = scale_raw[...].astype(f32).astype(bf16).reshape(p.L * p.R, p.X)
-    scale_out[...] = product(scale, matrix).reshape(scale_out.shape)
-    for k in range(p.K):
-        copies[k].wait()
-        block = raw[k].reshape(p.V * p.L * p.R, p.X)
-        members_out[k] = product(block, matrix).astype(bf16).reshape(p.V, p.L, p.R, p.X)
+    blocks = [flat(own[...]), flat(obs[...]), flat(cls[...].astype(f32).astype(bf16)), flat(static_raw[...]), scale]
+    blocks = products(blocks, matrix)
+    own_out[...] = blocks[0].astype(bf16).reshape(shape)
+    pack[0] = blocks[1].reshape(shape)
+    pack[1] = blocks[2].reshape(shape)
+    static_out[...] = blocks[3].reshape(shape)
+    scale_out[...] = blocks[4].reshape(scale_out.shape)
+    step = -(-p.K // 1)
+    for k in range(0, p.K, step):
+        some = min(step, p.K - k)
+        for copy in copies[k : k + some]:
+            copy.wait()
+        block = raw[k : k + some].reshape(some * p.V * p.L * p.R, p.X)
+        block = product(block, matrix).astype(bf16)
+        members_out[k : k + some] = block.reshape(some, p.V, p.L, p.R, p.X)
 
 
 def back_kernel(p, first, *refs):
@@ -204,7 +223,7 @@
 
 def sweep_kernel(p, first, level, *refs):
     refs = list(refs)
-    members, static_scale, back, low, high = refs[:5]
+    members, static_scale, back, near, far = refs[:5]
     refs = refs[5:]
     if first and level == 0:
         scale_index, *refs = refs
@@ -218,7 +237,7 @@
         rest, *refs = refs
     if first and level == 0:
         kap, *refs = refs
-    lo, hi, a, b, out = refs
+    ends, a, b, out = refs
     me, at = lax.axis_index("mem"), lax.axis_index("row")
     low_ok = jnp.where(at > 0, 1.0, 0.0).astype(f32)
     high_ok = jnp.where(at < p.row - 1, 1.0, 0.0).astype(f32)
@@ -226,26 +245,32 @@
     H = 2 * W
     fields = p.fields(level)
     count = p.tiles(level)
-    for ref, dst in ((low, lo), (high, hi)):
-        if p.pads:
-            dst[...] = jnp.zeros(dst.shape, f32)
-        skip = R - H if ref is low else 0
+    odd = lax.rem(at, 2)
+    if p.pads:
+        ends[...] = jnp.zeros(ends.shape, f32)
+
+    def edge(value, side):
+        if R == H:
+            return value
+        return jnp.where(side == 0, value[R - H :], value[:H])
+
+    for ref, side in ((near, 1 - odd), (far, odd)):
         for i, (field, l) in enumerate(fields):
             tile, lane = p.inner(field, l)
-            scatter(dst, tile, strided(lane, H), ref[i].astype(f32)[skip : skip + H])
+            scatter(ends.at[side], tile, strided(lane, H), edge(ref[i].astype(f32), side))
     if first and level == 0:
         for l in range(p.L):
-            pieces = (
-                (table(low[len(fields) + l].astype(f32)[R - H :], kappa_table) * low_ok, 0),
-                (table(scale_index[l], kappa_table), H),
-                (table(high[len(fields) + l].astype(f32)[:H], kappa_table) * high_ok, H + R),
-            )
-            for value, offset in pieces:
+            pieces_of = [(table(scale_index[l], kappa_table), H)]
+            for ref, side in ((near, 1 - odd), (far, odd)):
+                value = table(edge(ref[len(fields) + l].astype(f32), side), kappa_table)
+                pieces_of.append((value * jnp.where(side == 0, low_ok, high_ok), side * (H + R)))
+            for value, offset in pieces_of:
+                start = offset * SUB if isinstance(offset, int) else pl.multiple_of(offset * SUB, SUB)
                 for r in range(value.shape[0]):
-                    scatter(kap, l, pl.ds((offset + r) * SUB, SUB), jnp.broadcast_to(value[r : r + 1], (SUB, p.X)))
+                    scatter(kap, l, pl.ds(start + r * SUB, SUB), jnp.broadcast_to(value[r : r + 1], (SUB, p.X)))
                 for j in range(p.ST * SUB):
                     if (j % p.L) == l:
-                        scatter(kap, p.L + j // SUB, strided(offset * SUB + j % SUB, value.shape[0]), value)
+                        scatter(kap, p.L + j // SUB, strided(start + j % SUB, value.shape[0]), value)
     lane = lax.broadcasted_iota(jnp.int32, (SUB, LANES), 1)
     first_lane, last_lane = lane == 0, lane == LANES - 1
     side = functools.partial(sideways, first_lane=first_lane, last_lane=last_lane)
@@ -274,11 +299,11 @@
                 if sweep:
                     u = tiles(source, r)
                 elif r < H:
-                    u = tiles(lo, r, t)
+                    u = tiles(ends, r, 0, t)
                 elif r < H + R:
                     u = tiles(back, r - H, whole)
                 else:
-                    u = tiles(hi, r - H - R, t)
+                    u = tiles(ends, r - H - R, 1, t)
                 factor = tiles(kap, r, which)
                 w = [factor[c] * u[c] for c in cols]
                 held = (held + [(u, w)])[-3:]
@@ -414,31 +439,23 @@
     first = step[0:1, 0:1]
     matrix = matrix_ref[...]
 
-    def natural(blocks):
-        whole = exact(jnp.concatenate(blocks, axis=0), matrix, True)
-        return [whole[i * p.R : (i + 1) * p.R] for i in range(len(blocks))]
-
+    targets, blocks = [], []
     for level in range(p.L):
-        fields = p.fields(level)
-        for begin in range(0, len(fields), 8):
-            some = fields[begin : begin + 8]
-            blocks = []
-            for field, l in some:
-                tile, lane = p.inner(field, l)
-                where = strided(SWEEPS * SUB + lane, p.R)
-                blocks.append(-(first * gather(before[level], tile, where)) - second * gather(after[level], tile, where))
-            for (field, l), value in zip(some, natural(blocks)):
-                if field < p.K:
-                    control[field, l] = value
-                else:
-                    static_control[field - p.K, l] = value
-    some = [(s, l) for s in range(p.S) for l in range(p.L)]
-    blocks = [-(first * image0[me * p.S + s, l]) - second * image1[s, l] for s, l in some]
-    for (s, l), value in zip(some, natural(blocks)):
-        increment[s, l] = value
-
-
-def call(kernel, outs, scratch, far=0, cost=0):
+        for field, l in p.fields(level):
+            tile, lane = p.inner(field, l)
+            where = strided(SWEEPS * SUB + lane, p.R)
+            blocks.append(-(first * gather(before[level], tile, where)) - second * gather(after[level], tile, where))
+            targets.append((control, field, l) if field < p.K else (static_control, field - p.K, l))
+    for s in range(p.S):
+        for l in range(p.L):
+            blocks.append(-(first * image0[me * p.S + s, l]) - second * image1[s, l])
+            targets.append((increment, s, l))
+    (whole,) = products([jnp.concatenate(blocks, axis=0)], matrix, True)
+    for i, (ref, index, l) in enumerate(targets):
+        ref[index, l] = whole[i * p.R : (i + 1) * p.R]
+
+
+def call(kernel, outs, scratch, far=0, cost=0, grant=8):
     vmem = pl.BlockSpec(memory_space=pltpu.VMEM)
     anywhere = pl.BlockSpec(memory_space=pltpu.MemorySpace.HBM)
 
@@ -449,7 +466,7 @@
             in_specs=[anywhere] * far + [vmem] * (len(args) - far),
             out_specs=tuple(vmem for _ in outs),
             scratch_shapes=scratch,
-            compiler_params=pltpu.CompilerParams(vmem_limit_bytes=8 << 20),
+            compiler_params=pltpu.CompilerParams(vmem_limit_bytes=grant << 20),
             cost_estimate=pl.CostEstimate(flops=cost, bytes_accessed=cost, transcendentals=0),
         )(*[pltpu.with_memory_space_constraint(x, pltpu.MemorySpace.HBM) for x in args[:far]], *args[far:])
 
@@ -459,13 +476,21 @@
 def local(members, static_scale, observed, huber_class, scale_index):
     p = Plan(members, static_scale, lax.axis_size("mem"), lax.axis_size("row"))
     K, V, L, R, X, S, C = p.K, p.V, p.L, p.R, p.X, p.S, p.C
-    assert R >= 2 * SWEEPS
+    assert R >= 2 * SWEEPS and p.row % 2 == 0
 
     def round_mem(block, shift):
         return lax.ppermute(block, "mem", [(i, (i + shift) % p.mem) for i in range(p.mem)])
 
-    def round_row(block, shift):
-        return lax.ppermute(block, "row", [(i, (i + shift) % p.row) for i in range(p.row)])
+    def inside(block):
+        return lax.ppermute(block, "row", [(i, i ^ 1) for i in range(p.row)])
+
+    def across(block):
+        n, pairs = p.row, []
+        for m in range(p.mem):
+            pairs += [(m * n + i, m * n + (i + 1 if i % 2 else i - 1)) for i in range(1, n - 1)]
+            other = m ^ 1 if p.mem % 2 == 0 else m
+            pairs += [(m * n + i, other * n + i) for i in (0, n - 1)]
+        return lax.ppermute(block, ("mem", "row"), pairs)
 
     vmem = lambda shape: pltpu.VMEM(shape, f32)
     part = functools.partial
@@ -485,7 +510,7 @@
     members, static_scale, scale_index, pack, own, matrix = call(
         part(fetch_kernel, p),
         [(members.shape, bf16), (own_shape, f32), ((L, R, X), f32), ((2,) + own_shape, f32), (own_shape, bf16), ((X, X), bf16)],
-        scratch + [pltpu.SemaphoreType.DMA((K + 2,))], far=3, cost=4 << 20,
+        scratch + [pltpu.SemaphoreType.DMA((K + 2,))], far=3, cost=4 << 20, grant=20,
     )(members, static_scale, scale_index, obs, cls, own)
     pack_in = jnp.stack([round_mem(pack, shift) for shift in shifts])
 
@@ -506,9 +531,9 @@
             )(members, static_scale, pack, pack_in, image, sums)
         halos = []
         for msg in msgs:
-            low = round_row(msg, 1)
-            high = round_row(msg, p.row - 1)
-            halos.append((low, high))
+            near = inside(msg)
+            far = across(msg)
+            halos.append((near, far))
         grad, norms, partial_images, gots, rest = [], [], [], [], None
         for level in range(L):
             count = p.tiles(level)
@@ -522,8 +547,8 @@
                 outs.append(((L - 1, S, R, X), f32))
             if first and level == 0:
                 outs.append(((L + p.ST, C, p.RE * SUB, LANES), f32))
-            halo = vmem((count, C, 2 * SWEEPS * SUB, LANES))
-            work = [halo, halo, vmem((C, p.RE * SUB, LANES)), vmem((C, p.RE * SUB, LANES))]
+            halo = vmem((2, count, C, 2 * SWEEPS * SUB, LANES))
+            work = [halo, vmem((C, p.RE * SUB, LANES)), vmem((C, p.RE * SUB, LANES))]
             g, norm, partial_image, ship, *more = call(
                 part(sweep_kernel, p, first, level), outs, work + [vmem((count, C, R * SUB, LANES))],
                 cost=8 << 20,

time: 82.4 us -> 72.9 us (0.88)
  starting transfers between devices: 25.2 us -> 13 us
  waiting for transfers between devices: 12.3 us -> 20.5 us
  Pallas kernels: 21.6 us -> 16.9 us
  blocking collectives: 22.4 us -> 21.5 us
    ppermute x8, starting transfers between devices: 17.9 us -> 4.38 us  [the longest x4 4.08 us: across(): return lax.ppermute(block, ('mem', 'row'), pairs)]
    ppermute x8, waiting for transfers between devices: 5.58 us -> 14.6 us  [the longest x4 14.5 us: across(): return lax.ppermute(block, ('mem', 'row'), pairs)]
    pallas_call x11, Pallas kernels: 21.6 us -> 16.9 us  [run(): pl.pallas_call(kernel, out_shape=tuple((jax.ShapeDtypeStruct(shape, dtype...]
    ppermute x6, starting transfers between devices: 7.33 us -> 8.62 us  [round_mem(): lax.ppermute(block, 'mem', [(i, (i + shift) % p.mem) for i in range(p.mem)])]
    all_to_all x2, blocking collectives: 22.4 us -> 21.5 us  [local(): sums = lax.all_to_all(send, ('mem', 'row'), 0, 0)]
  transfers between devices with their start and end apart: 14 -> 14, of which waited for: 4 -> 4; matrix products, arithmetic and copies ran while one was open for 0% -> 0% of each run, Pallas kernels for 18% -> 17%
where the time goes in v6:
time: 72.9 us; the launch traced here: 72.7 us
  blocking collectives  21.5 us (29%)
  waiting for transfers between devices  20.5 us (28%)
  Pallas kernels  16.9 us (23%)
  starting transfers between devices  13 us (18%)
  between operations  0.74 us (1%)
    all_to_all x2, blocking collectives, local(): sums = lax.all_to_all(send, ('mem', 'row'), 0, 0)  21.5 us
    pallas_call x11, Pallas kernels, run(): pl.pallas_call(kernel, out_shape=tuple((jax.ShapeDtypeStruct(shape, dtype...  16.9 us
    ppermute x4, waiting for transfers between devices, across(): return lax.ppermute(block, ('mem', 'row'), pairs)  14.5 us
    ppermute x6, starting transfers between devices, round_mem(): lax.ppermute(block, 'mem', [(i, (i + shift) % p.mem) for i in range(p.mem)])  8.62 us
    ppermute x6, waiting for transfers between devices, round_mem(): lax.ppermute(block, 'mem', [(i, (i + shift) % p.mem) for i in range(p.mem)])  5.97 us
    ppermute x4, starting transfers between devices, across(): return lax.ppermute(block, ('mem', 'row'), pairs)  4.08 us
  transfers between devices with their start and end apart: 14, of which 4 were waited for; matrix products, arithmetic and copies ran while one was open for 0% of the time, Pallas kernels for 17%

profile of v6, /device:TPU:0, one launch (start us, length us, event | category | flops | bytes accessed | tf_op | source)
XLA Modules:
  0.0 72.7 jit_solution(16105882283700495188)
XLA Ops:
  0.6 1.0 %shard_map.76 = (f32[4,2,8,512]{3,2,1,0:T(8,128)S(1)}, s32[4,2,8,512]{3,2,1,0:T(8,128)S(1)}, bf16[4,2,8,512]{3,2,1,0:T(8,128)(2,1)S(1)}) custom-call(f32[4,2,8,512]{3,2,1,0:T(8,128)} %obs.1, s32[4,2,8,512]{3,2,1,0:T(8,128)} %cls.1), custom_call_target="tpu_custom_call" | custom-call | tf_op jit(solution)/shard_map/pallas_call | solution.py:463
  1.7 3.1 %collective-permute-start.1 = (bf16[4,2,8,512]{3,2,1,0:T(8,128)(2,1)S(1)}, bf16[4,2,8,512]{3,2,1,0:T(8,128)(2,1)S(1)}, u32[]{:S(2)}, u32[]{:S(2)}) collective-permute-start(bf16[4,2,8,512]{3,2,1,0:T(8,128)(2,1)S(1)} %get-tuple-element.44.own), channel_id=1, source_target_pairs={{0,16},{16,0},{1,17},{17,1},{2,18},{18,2},{3,19},{19,3},{4,20},{20... | collective-permute-start | bytes 196616 | tf_op jit(solution)/shard_map/ppermute | solution.py:482
  4.7 3.5 %shard_map.77 = (bf16[16,8,2,8,512]{4,3,2,1,0:T(8,128)(2,1)S(1)}, f32[4,2,8,512]{3,2,1,0:T(8,128)S(1)}, f32[2,8,512]{2,1,0:T(8,128)S(1)}, f32[2,4,2,8,512]{4,3,2...) custom-call(bf16[16,8,2,8,512]{4,3,2,1,0:T(8,128)(2,1)} %members.1, ...), custom_call_target="tpu_custom_call" | custom-call | flops 4194304 | bytes 4194304 | tf_op jit(solution)/shard_map/pallas_call | solution.py:463
  8.3 0.0 collective-permute-done.1
  8.3 0.8 %shard_map.78 = (f32[5,4,64,128]{3,2,1,0:T(8,128)S(1)}, bf16[18,8,512]{2,1,0:T(8,128)(2,1)S(1)}, bf16[24,8,512]{2,1,0:T(8,128)(2,1)S(1)}) custom-call(bf16[16,8,2,8,512]{4,3,2,1,0:T(8,128)(2,1)S(1)} %get-tuple-element.45.refs_0_, f32[4,2,8,512]{3,2,1,0:T(8,128)S(1)} %get-tuple-element.46.refs_1_, f32[2,8,512]{2,1,0:T(8,128)S(1)} %get-tuple-element.48.refs_2_.refs_5_, ...), custom_call_target="tpu_custom_call" | custom-call | tf_op jit(solution)/shard_map/pallas_call | solution.py:463
  9.1 0.1 collective-permute-start.4
  9.2 0.8 %collective-permute-start.5 = (bf16[24,8,512]{2,1,0:T(8,128)(2,1)S(1)}, bf16[24,8,512]{2,1,0:T(8,128)(2,1)S(1)}, u32[]{:S(2)}, u32[]{:S(2)}) collective-permute-start(bf16[24,8,512]{2,1,0:T(8,128)(2,1)S(1)} %get-tuple-element.54), channel_id=1, source_target_pairs={{1,2},{2,1},{3,4},{4,3},{5,6},{6,5},{7,8},{8,7},{9,10},{10,9},{11,... | collective-permute-start | bytes 589832 | tf_op jit(solution)/shard_map/ppermute | solution.py:493
  10.0 1.3 %collective-permute-start = (f32[2,4,2,8,512]{4,3,2,1,0:T(8,128)S(1)}, f32[2,4,2,8,512]{4,3,2,1,0:T(8,128)S(1)}, u32[]{:S(2)}, u32[]{:S(2)}) collective-permute-start(f32[2,4,2,8,512]{4,3,2,1,0:T(8,128)S(1)} %get-tuple-element.47.refs_7_.refs_2_), channel_id=1, source_target_pairs={{0,16},{16,0},{1,17},{17,1},{2,18},{18,2},{3,19},{19,3},{4,20},{20... | collective-permute-start | bytes 786440 | tf_op jit(solution)/shard_map/ppermute | solution.py:482
  11.3 0.0 collective-permute-start.2
  11.3 1.3 %collective-permute-start.3 = (bf16[18,8,512]{2,1,0:T(8,128)(2,1)S(1)}, bf16[18,8,512]{2,1,0:T(8,128)(2,1)S(1)}, u32[]{:S(2)}, u32[]{:S(2)}) collective-permute-start(bf16[18,8,512]{2,1,0:T(8,128)(2,1)S(1)} %get-tuple-element.52), channel_id=1, source_target_pairs={{1,2},{2,1},{3,4},{4,3},{5,6},{6,5},{7,8},{8,7},{9,10},{10,9},{11,... | collective-permute-start | bytes 442376 | tf_op jit(solution)/shard_map/ppermute | solution.py:493
  12.6 0.0 collective-permute-done.2.refs_3_
  12.6 9.5 %collective-permute-done.3.refs_4_ = bf16[18,8,512]{2,1,0:T(8,128)(2,1)S(1)} collective-permute-done((bf16[18,8,512]{2,1,0:T(8,128)(2,1)S(1)}, bf16[18,8,512]{2,1,0:T(8,128)(2,1)S(1)}, u32[]{:S(2)}, u32[]{:S(2)}) %collective-permute-start.3) | collective-permute-done | bytes 147488 | tf_op jit(solution)/shard_map/ppermute | solution.py:493
  22.1 1.9 %shard_map.79 = (f32[2,4,128,128]{3,2,1,0:T(8,128)S(1)}, f32[1,128]{1,0:T(1,128)S(1)}, f32[8,8,512]{2,1,0:T(8,128)S(1)}, bf16[8,8,512]{2,1,0:T(8,128)(2,1)S(1)}, f32[3,4,192,128]{3,2,1,0:T(8,128)S(1)}) custom-call(bf16[16,8,2,8,512]{4,3,2,1,0:T(8,128)(2,1)S(1)} %get-tuple-element.45.refs_0_, f32[4,2,8,512]{3,2,1,0:T(8,128)S(1)} %get-tuple-element.46.refs_1_, ...), custom_call_target="tpu_custom_call" | custom-call | flops 8388608 | bytes 8388608 | tf_op jit(solution)/shard_map/pallas_call | solution.py:463
  24.0 0.0 collective-permute-done.4.refs_3_
  24.0 0.0 collective-permute-done.5.refs_4_
  24.0 2.5 %shard_map.80 = (f32[3,4,128,128]{3,2,1,0:T(8,128)S(1)}, f32[1,128]{1,0:T(1,128)S(1)}, f32[8,8,512]{2,1,0:T(8,128)S(1)}, bf16[12,8,512]{2,1,0:T(8,128)(2,1)S(1)}, f32[1,4,8,512]{3,2,1,0:T(8,128)S(1)}) custom-call(bf16[16,8,2,8,512]{4,3,2,1,0:T(8,128)(2,1)S(1)} %get-tuple-element.45.refs_0_, f32[4,2,8,512]{3,2,1,0:T(8,128)S(1)} %get-tuple-element.46.refs_1_, ...), custom_call_target="tpu_custom_call" | custom-call | flops 8388608 | bytes 8388608 | tf_op jit(solution)/shard_map/pallas_call | solution.py:463
  26.5 0.8 %collective-permute-start.7 = (bf16[12,8,512]{2,1,0:T(8,128)(2,1)S(1)}, bf16[12,8,512]{2,1,0:T(8,128)(2,1)S(1)}, u32[]{:S(2)}, u32[]{:S(2)}) collective-permute-start(bf16[12,8,512]{2,1,0:T(8,128)(2,1)S(1)} %get-tuple-element.58), channel_id=1, source_target_pairs={{0,16},{16,0},{1,17},{17,1},{2,18},{18,2},{3,19},{19,3},{4,20},{20... | collective-permute-start | bytes 294920 | tf_op jit(solution)/shard_map/ppermute | solution.py:482
  27.3 1.3 %collective-permute-start.6 = (bf16[8,8,512]{2,1,0:T(8,128)(2,1)S(1)}, bf16[8,8,512]{2,1,0:T(8,128)(2,1)S(1)}, u32[]{:S(2)}, u32[]{:S(2)}) collective-permute-start(bf16[8,8,512]{2,1,0:T(8,128)(2,1)S(1)} %get-tuple-element.57), channel_id=1, source_target_pairs={{0,16},{16,0},{1,17},{17,1},{2,18},{18,2},{3,19},{19,3},{4,20},{20... | collective-permute-start | bytes 196616 | tf_op jit(solution)/shard_map/ppermute | solution.py:482
  28.6 0.0 collective-permute-done
  28.6 3.3 %collective-permute-done.6 = bf16[8,8,512]{2,1,0:T(8,128)(2,1)S(1)} collective-permute-done((bf16[8,8,512]{2,1,0:T(8,128)(2,1)S(1)}, bf16[8,8,512]{2,1,0:T(8,128)(2,1)S(1)}, u32[]{:S(2)}, u32[]{:S(2)}) %collective-permute-start.6) | collective-permute-done | bytes 65568 | tf_op jit(solution)/shard_map/ppermute | solution.py:482
  31.9 0.0 collective-permute-done.7
  31.9 0.1 shard_map.81
  32.1 9.8 %all_to_all.10.refs_5_ = f32[32,1,256]{2,1,0:T(1,128)S(1)} all-to-all(f32[32,1,256]{2,1,0:T(1,128)S(1)} %get-tuple-element.63), channel_id=1, replica_groups=mesh['mem'=2,'row'=16] {'mem','row'}, dimensions={0} | all-to-all | bytes 65536 | tf_op jit(solution)/shard_map/all_to_all | solution.py:574
  41.9 0.7 shard_map.82
  42.6 0.2 collective-permute-start.10
  42.8 0.6 collective-permute-start.11
  43.3 0.0 collective-permute-start.8
  43.4 1.4 %collective-permute-start.9 = (bf16[16,8,512]{2,1,0:T(8,128)(2,1)S(1)}, bf16[16,8,512]{2,1,0:T(8,128)(2,1)S(1)}, u32[]{:S(2)}, u32[]{:S(2)}) collective-permute-start(bf16[16,8,512]{2,1,0:T(8,128)(2,1)S(1)} %get-tuple-element.65), channel_id=1, source_target_pairs={{1,2},{2,1},{3,4},{4,3},{5,6},{6,5},{7,8},{8,7},{9,10},{10,9},{11,... | collective-permute-start | bytes 393224 | tf_op jit(solution)/shard_map/ppermute | solution.py:493
  44.8 0.0 collective-permute-done.8.refs_3_
  44.8 5.0 %collective-permute-done.9.refs_4_ = bf16[16,8,512]{2,1,0:T(8,128)(2,1)S(1)} collective-permute-done((bf16[16,8,512]{2,1,0:T(8,128)(2,1)S(1)}, bf16[16,8,512]{2,1,0:T(8,128)(2,1)S(1)}, u32[]{:S(2)}, u32[]{:S(2)}) %collective-permute-start.9) | collective-permute-done | bytes 131104 | tf_op jit(solution)/shard_map/ppermute | solution.py:493
  49.8 1.8 %shard_map.83 = (f32[2,4,128,128]{3,2,1,0:T(8,128)S(1)}, f32[1,128]{1,0:T(1,128)S(1)}, f32[8,8,512]{2,1,0:T(8,128)S(1)}, bf16[1,4,8,512]{3,2,1,0:T(8,128)(2,1)S(1)}) custom-call(bf16[16,8,2,8,512]{4,3,2,1,0:T(8,128)(2,1)S(1)} %get-tuple-element.45.refs_0_, f32[4,2,8,512]{3,2,1,0:T(8,128)S(1)} %get-tuple-element.46.refs_1_, ...), custom_call_target="tpu_custom_call" | custom-call | flops 8388608 | bytes 8388608 | tf_op jit(solution)/shard_map/pallas_call | solution.py:463
  51.6 0.6 collective-permute-start.12
  52.3 0.0 collective-permute-done.10.refs_3_
  52.3 0.0 collective-permute-done.11.refs_4_
  52.3 2.5 %shard_map.84 = (f32[3,4,128,128]{3,2,1,0:T(8,128)S(1)}, f32[1,128]{1,0:T(1,128)S(1)}, f32[8,8,512]{2,1,0:T(8,128)S(1)}, bf16[1,4,8,512]{3,2,1,0:T(8,128)(2,1)S(1)}, f32[1,4,8,512]{3,2,1,0:T(8,128)S(1)}) custom-call(bf16[16,8,2,8,512]{4,3,2,1,0:T(8,128)(2,1)S(1)} %get-tuple-element.45.refs_0_, f32[4,2,8,512]{3,2,1,0:T(8,128)S(1)} %get-tuple-element.46.refs_1_, ...), custom_call_target="tpu_custom_call" | custom-call | flops 8388608 | bytes 8388608 | tf_op jit(solution)/shard_map/pallas_call | solution.py:463
  54.8 1.5 %collective-permute-start.13 = (bf16[4,8,512]{2,1,0:T(8,128)(2,1)S(1)}, bf16[4,8,512]{2,1,0:T(8,128)(2,1)S(1)}, u32[]{:S(2)}, u32[]{:S(2)}) collective-permute-start(bf16[4,8,512]{2,1,0:T(8,128)(2,1)S(1)} %bitcast.16), channel_id=1, source_target_pairs={{0,16},{16,0},{1,17},{17,1},{2,18},{18,2},{3,19},{19,3},{4,20},{20... | collective-permute-start | bytes 98312 | tf_op jit(solution)/shard_map/ppermute | solution.py:482
  56.3 0.0 collective-permute-done.12
  56.3 2.7 %collective-permute-done.13 = bf16[4,8,512]{2,1,0:T(8,128)(2,1)S(1)} collective-permute-done((bf16[4,8,512]{2,1,0:T(8,128)(2,1)S(1)}, bf16[4,8,512]{2,1,0:T(8,128)(2,1)S(1)}, u32[]{:S(2)}, u32[]{:S(2)}) %collective-permute-start.13) | collective-permute-done | bytes 32800 | tf_op jit(solution)/shard_map/ppermute | solution.py:482
  59.0 0.1 shard_map.85
  59.2 11.7 %all_to_all.11.got = f32[32,1,256]{2,1,0:T(1,128)S(1)} all-to-all(f32[32,1,256]{2,1,0:T(1,128)S(1)} %get-tuple-element.77), channel_id=1, replica_groups=mesh['mem'=2,'row'=16] {'mem','row'}, dimensions={0} | all-to-all | bytes 65536 | tf_op jit(solution)/shard_map/all_to_all | solution.py:574
  70.8 1.9 %shard_map.86 = (f32[16,2,8,512]{3,2,1,0:T(8,128)}, f32[4,2,8,512]{3,2,1,0:T(8,128)}, f32[4,2,8,512]{3,2,1,0:T(8,128)}) custom-call(f32[32,1,256]{2,1,0:T(1,128)S(1)} %all_to_all.11.got, f32[1,128]{1,0:T(1,128)S(1)} %get-tuple-element.67.refs_7_.refs_9_.step, f32[8,2,8,512]{3,2,1,0:T(8,128)S(1)} %get-tuple-element.62.refs_4_.refs_8_.image0, ...), custom_call_target="tpu_custom_call" | custom-call | tf_op jit(solution)/shard_map/pallas_call | solution.py:463
Async XLA Ops:
  1.7 6.6 %collective-permute-start.1 = (bf16[4,2,8,512]{3,2,1,0:T(8,128)(2,1)S(1)}, bf16[4,2,8,512]{3,2,1,0:T(8,128)(2,1)S(1)}, u32[]{:S(2)}, u32[]{:S(2)}) collective-permute-start(bf16[4,2,8,512]{3,2,1,0:T(8,128)(2,1)S(1)} %get-tuple-element.44.own), channel_id=1, source_target_pairs={{0,16},{16,0},{1,17},{17,1},{2,18},{18,2},{3,19},{19,3},{4,20},{20... | collective-permute-start | bytes 196616 | tf_op jit(solution)/shard_map/ppermute | solution.py:482
  9.1 14.9 %collective-permute-start.4 = (bf16[24,8,512]{2,1,0:T(8,128)(2,1)S(1)}, bf16[24,8,512]{2,1,0:T(8,128)(2,1)S(1)}, u32[]{:S(2)}, u32[]{:S(2)}) collective-permute-start(bf16[24,8,512]{2,1,0:T(8,128)(2,1)S(1)} %get-tuple-element.54), channel_id=1, source_target_pairs={{0,1},{1,0},{2,3},{3,2},{4,5},{5,4},{6,7},{7,6},{8,9},{9,8},{10,11... | collective-permute-start | bytes 589832 | tf_op jit(solution)/shard_map/ppermute | solution.py:485
  9.2 14.8 %collective-permute-start.5 = (bf16[24,8,512]{2,1,0:T(8,128)(2,1)S(1)}, bf16[24,8,512]{2,1,0:T(8,128)(2,1)S(1)}, u32[]{:S(2)}, u32[]{:S(2)}) collective-permute-start(bf16[24,8,512]{2,1,0:T(8,128)(2,1)S(1)} %get-tuple-element.54), channel_id=1, source_target_pairs={{1,2},{2,1},{3,4},{4,3},{5,6},{6,5},{7,8},{8,7},{9,10},{10,9},{11,... | collective-permute-start | bytes 589832 | tf_op jit(solution)/shard_map/ppermute | solution.py:493
  10.0 18.7 %collective-permute-start = (f32[2,4,2,8,512]{4,3,2,1,0:T(8,128)S(1)}, f32[2,4,2,8,512]{4,3,2,1,0:T(8,128)S(1)}, u32[]{:S(2)}, u32[]{:S(2)}) collective-permute-start(f32[2,4,2,8,512]{4,3,2,1,0:T(8,128)S(1)} %get-tuple-element.47.refs_7_.refs_2_), channel_id=1, source_target_pairs={{0,16},{16,0},{1,17},{17,1},{2,18},{18,2},{3,19},{19,3},{4,20},{20... | collective-permute-start | bytes 786440 | tf_op jit(solution)/shard_map/ppermute | solution.py:482
  11.3 1.4 %collective-permute-start.2 = (bf16[18,8,512]{2,1,0:T(8,128)(2,1)S(1)}, bf16[18,8,512]{2,1,0:T(8,128)(2,1)S(1)}, u32[]{:S(2)}, u32[]{:S(2)}) collective-permute-start(bf16[18,8,512]{2,1,0:T(8,128)(2,1)S(1)} %get-tuple-element.52), channel_id=1, source_target_pairs={{0,1},{1,0},{2,3},{3,2},{4,5},{5,4},{6,7},{7,6},{8,9},{9,8},{10,11... | collective-permute-start | bytes 442376 | tf_op jit(solution)/shard_map/ppermute | solution.py:485
  11.3 10.8 %collective-permute-start.3 = (bf16[18,8,512]{2,1,0:T(8,128)(2,1)S(1)}, bf16[18,8,512]{2,1,0:T(8,128)(2,1)S(1)}, u32[]{:S(2)}, u32[]{:S(2)}) collective-permute-start(bf16[18,8,512]{2,1,0:T(8,128)(2,1)S(1)} %get-tuple-element.52), channel_id=1, source_target_pairs={{1,2},{2,1},{3,4},{4,3},{5,6},{6,5},{7,8},{8,7},{9,10},{10,9},{11,... | collective-permute-start | bytes 442376 | tf_op jit(solution)/shard_map/ppermute | solution.py:493
  26.5 5.4 %collective-permute-start.7 = (bf16[12,8,512]{2,1,0:T(8,128)(2,1)S(1)}, bf16[12,8,512]{2,1,0:T(8,128)(2,1)S(1)}, u32[]{:S(2)}, u32[]{:S(2)}) collective-permute-start(bf16[12,8,512]{2,1,0:T(8,128)(2,1)S(1)} %get-tuple-element.58), channel_id=1, source_target_pairs={{0,16},{16,0},{1,17},{17,1},{2,18},{18,2},{3,19},{19,3},{4,20},{20... | collective-permute-start | bytes 294920 | tf_op jit(solution)/shard_map/ppermute | solution.py:482
  27.3 4.6 %collective-permute-start.6 = (bf16[8,8,512]{2,1,0:T(8,128)(2,1)S(1)}, bf16[8,8,512]{2,1,0:T(8,128)(2,1)S(1)}, u32[]{:S(2)}, u32[]{:S(2)}) collective-permute-start(bf16[8,8,512]{2,1,0:T(8,128)(2,1)S(1)} %get-tuple-element.57), channel_id=1, source_target_pairs={{0,16},{16,0},{1,17},{17,1},{2,18},{18,2},{3,19},{19,3},{4,20},{20... | collective-permute-start | bytes 196616 | tf_op jit(solution)/shard_map/ppermute | solution.py:482
  42.6 9.7 %collective-permute-start.10 = (bf16[24,8,512]{2,1,0:T(8,128)(2,1)S(1)}, bf16[24,8,512]{2,1,0:T(8,128)(2,1)S(1)}, u32[]{:S(2)}, u32[]{:S(2)}) collective-permute-start(bf16[24,8,512]{2,1,0:T(8,128)(2,1)S(1)} %get-tuple-element.69), channel_id=1, source_target_pairs={{0,1},{1,0},{2,3},{3,2},{4,5},{5,4},{6,7},{7,6},{8,9},{9,8},{10,11... | collective-permute-start | bytes 589832 | tf_op jit(solution)/shard_map/ppermute | solution.py:485
  42.8 9.5 %collective-permute-start.11 = (bf16[24,8,512]{2,1,0:T(8,128)(2,1)S(1)}, bf16[24,8,512]{2,1,0:T(8,128)(2,1)S(1)}, u32[]{:S(2)}, u32[]{:S(2)}) collective-permute-start(bf16[24,8,512]{2,1,0:T(8,128)(2,1)S(1)} %get-tuple-element.69), channel_id=1, source_target_pairs={{1,2},{2,1},{3,4},{4,3},{5,6},{6,5},{7,8},{8,7},{9,10},{10,9},{11,... | collective-permute-start | bytes 589832 | tf_op jit(solution)/shard_map/ppermute | solution.py:493
  43.3 1.5 %collective-permute-start.8 = (bf16[16,8,512]{2,1,0:T(8,128)(2,1)S(1)}, bf16[16,8,512]{2,1,0:T(8,128)(2,1)S(1)}, u32[]{:S(2)}, u32[]{:S(2)}) collective-permute-start(bf16[16,8,512]{2,1,0:T(8,128)(2,1)S(1)} %get-tuple-element.65), channel_id=1, source_target_pairs={{0,1},{1,0},{2,3},{3,2},{4,5},{5,4},{6,7},{7,6},{8,9},{9,8},{10,11... | collective-permute-start | bytes 393224 | tf_op jit(solution)/shard_map/ppermute | solution.py:485
  43.4 6.4 %collective-permute-start.9 = (bf16[16,8,512]{2,1,0:T(8,128)(2,1)S(1)}, bf16[16,8,512]{2,1,0:T(8,128)(2,1)S(1)}, u32[]{:S(2)}, u32[]{:S(2)}) collective-permute-start(bf16[16,8,512]{2,1,0:T(8,128)(2,1)S(1)} %get-tuple-element.65), channel_id=1, source_target_pairs={{1,2},{2,1},{3,4},{4,3},{5,6},{6,5},{7,8},{8,7},{9,10},{10,9},{11,... | collective-permute-start | bytes 393224 | tf_op jit(solution)/shard_map/ppermute | solution.py:493
  51.6 4.7 %collective-permute-start.12 = (bf16[4,8,512]{2,1,0:T(8,128)(2,1)S(1)}, bf16[4,8,512]{2,1,0:T(8,128)(2,1)S(1)}, u32[]{:S(2)}, u32[]{:S(2)}) collective-permute-start(bf16[4,8,512]{2,1,0:T(8,128)(2,1)S(1)} %bitcast.15), channel_id=1, source_target_pairs={{0,16},{16,0},{1,17},{17,1},{2,18},{18,2},{3,19},{19,3},{4,20},{20... | collective-permute-start | bytes 98312 | tf_op jit(solution)/shard_map/ppermute | solution.py:482
  54.8 4.2 %collective-permute-start.13 = (bf16[4,8,512]{2,1,0:T(8,128)(2,1)S(1)}, bf16[4,8,512]{2,1,0:T(8,128)(2,1)S(1)}, u32[]{:S(2)}, u32[]{:S(2)}) collective-permute-start(bf16[4,8,512]{2,1,0:T(8,128)(2,1)S(1)} %bitcast.16), channel_id=1, source_target_pairs={{0,16},{16,0},{1,17},{17,1},{2,18},{18,2},{3,19},{19,3},{4,20},{20... | collective-permute-start | bytes 98312 | tf_op jit(solution)/shard_map/ppermute | solution.py:482

commit v7 on v6

--- a/solution.py
+++ b/solution.py
@@ -152,7 +152,7 @@
         for copy in copies[k : k + some]:
             copy.wait()
         block = raw[k : k + some].reshape(some * p.V * p.L * p.R, p.X)
-        block = product(block, matrix).astype(bf16)
+        block = product(block, matrix)
         members_out[k : k + some] = block.reshape(some, p.V, p.L, p.R, p.X)
 
 
@@ -199,9 +199,9 @@
             msgs[0][len(p.fields(0)) + l] = scale_index[l].astype(bf16)
     for l in range(p.L):
         for k in range(p.K):
-            value = members[k, 0, l].astype(f32) * sent[0, l]
+            value = members[k, 0, l] * sent[0, l]
             for v in range(1, p.V):
-                value = value + members[k, v, l].astype(f32) * sent[v, l]
+                value = value + members[k, v, l] * sent[v, l]
             value = p.ens * value
             tile, lane = p.slot(k, l)
             scatter(back, tile, strided(lane, p.R), value)
@@ -352,7 +352,7 @@
         tile, j = p.inner(k, level)
         spread = gather(out, tile, strided(j, R)).astype(bf16).astype(f32)
         for v in range(p.V):
-            term = members[k, v, level].astype(f32) * spread
+            term = members[k, v, level] * spread
             sums[v] = term if k == 0 else sums[v] + term
     for v in range(p.V):
         part[v] = p.ens * sums[v]
@@ -509,7 +509,7 @@
     scratch = [pltpu.VMEM(x.shape, x.dtype) for x in (members, static_scale, scale_index)]
     members, static_scale, scale_index, pack, own, matrix = call(
         part(fetch_kernel, p),
-        [(members.shape, bf16), (own_shape, f32), ((L, R, X), f32), ((2,) + own_shape, f32), (own_shape, bf16), ((X, X), bf16)],
+        [(members.shape, f32), (own_shape, f32), ((L, R, X), f32), ((2,) + own_shape, f32), (own_shape, bf16), ((X, X), bf16)],
         scratch + [pltpu.SemaphoreType.DMA((K + 2,))], far=3, cost=4 << 20, grant=20,
     )(members, static_scale, scale_index, obs, cls, own)
     pack_in = jnp.stack([round_mem(pack, shift) for shift in shifts])

time: 72.9 us -> 72.5 us (level)
  no operation moved by 1% of the time
where the time goes in v7:
time: 72.5 us; the launch traced here: 72.3 us
  blocking collectives  21.5 us (30%)
  waiting for transfers between devices  20.5 us (28%)
  Pallas kernels  16.5 us (23%)
  starting transfers between devices  13 us (18%)
  between operations  0.74 us (1%)
    all_to_all x2, blocking collectives, local(): sums = lax.all_to_all(send, ('mem', 'row'), 0, 0)  21.5 us
    pallas_call x11, Pallas kernels, run(): pl.pallas_call(kernel, out_shape=tuple((jax.ShapeDtypeStruct(shape, dtype...  16.5 us
    ppermute x4, waiting for transfers between devices, across(): return lax.ppermute(block, ('mem', 'row'), pairs)  14.5 us
    ppermute x6, starting transfers between devices, round_mem(): lax.ppermute(block, 'mem', [(i, (i + shift) % p.mem) for i in range(p.mem)])  8.63 us
    ppermute x6, waiting for transfers between devices, round_mem(): lax.ppermute(block, 'mem', [(i, (i + shift) % p.mem) for i in range(p.mem)])  5.97 us
    ppermute x4, starting transfers between devices, across(): return lax.ppermute(block, ('mem', 'row'), pairs)  4.08 us
  transfers between devices with their start and end apart: 14, of which 4 were waited for; matrix products, arithmetic and copies ran while one was open for 0% of the time, Pallas kernels for 17%

profile of v7, /device:TPU:0, one launch (start us, length us, event | category | flops | bytes accessed | tf_op | source)
XLA Modules:
  0.0 72.3 jit_solution(4241148624374756768)
XLA Ops:
  0.6 1.0 %shard_map.76 = (f32[4,2,8,512]{3,2,1,0:T(8,128)S(1)}, s32[4,2,8,512]{3,2,1,0:T(8,128)S(1)}, bf16[4,2,8,512]{3,2,1,0:T(8,128)(2,1)S(1)}) custom-call(f32[4,2,8,512]{3,2,1,0:T(8,128)} %obs.1, s32[4,2,8,512]{3,2,1,0:T(8,128)} %cls.1), custom_call_target="tpu_custom_call" | custom-call | tf_op jit(solution)/shard_map/pallas_call | solution.py:463
  1.7 3.1 %collective-permute-start.1 = (bf16[4,2,8,512]{3,2,1,0:T(8,128)(2,1)S(1)}, bf16[4,2,8,512]{3,2,1,0:T(8,128)(2,1)S(1)}, u32[]{:S(2)}, u32[]{:S(2)}) collective-permute-start(bf16[4,2,8,512]{3,2,1,0:T(8,128)(2,1)S(1)} %get-tuple-element.44.own), channel_id=1, source_target_pairs={{0,16},{16,0},{1,17},{17,1},{2,18},{18,2},{3,19},{19,3},{4,20},{20... | collective-permute-start | bytes 196616 | tf_op jit(solution)/shard_map/ppermute | solution.py:482
  4.7 3.5 %shard_map.77 = (f32[16,8,2,8,512]{4,3,2,1,0:T(8,128)S(1)}, f32[4,2,8,512]{3,2,1,0:T(8,128)S(1)}, f32[2,8,512]{2,1,0:T(8,128)S(1)}, f32[2,4,2,8,512]{4,3,2,1,0:T...) custom-call(bf16[16,8,2,8,512]{4,3,2,1,0:T(8,128)(2,1)} %members.1, ...), custom_call_target="tpu_custom_call" | custom-call | flops 4194304 | bytes 4194304 | tf_op jit(solution)/shard_map/pallas_call | solution.py:463
  8.3 0.0 collective-permute-done.1
  8.3 0.8 %shard_map.78 = (f32[5,4,64,128]{3,2,1,0:T(8,128)S(1)}, bf16[18,8,512]{2,1,0:T(8,128)(2,1)S(1)}, bf16[24,8,512]{2,1,0:T(8,128)(2,1)S(1)}) custom-call(f32[16,8,2,8,512]{4,3,2,1,0:T(8,128)S(1)} %get-tuple-element.45.refs_0_, f32[4,2,8,512]{3,2,1,0:T(8,128)S(1)} %get-tuple-element.46.refs_1_, f32[2,8,512]{2,1,0:T(8,128)S(1)} %get-tuple-element.48.refs_2_.refs_5_, ...), custom_call_target="tpu_custom_call" | custom-call | tf_op jit(solution)/shard_map/pallas_call | solution.py:463
  9.1 0.1 collective-permute-start.4
  9.2 0.8 %collective-permute-start.5 = (bf16[24,8,512]{2,1,0:T(8,128)(2,1)S(1)}, bf16[24,8,512]{2,1,0:T(8,128)(2,1)S(1)}, u32[]{:S(2)}, u32[]{:S(2)}) collective-permute-start(bf16[24,8,512]{2,1,0:T(8,128)(2,1)S(1)} %get-tuple-element.54), channel_id=1, source_target_pairs={{1,2},{2,1},{3,4},{4,3},{5,6},{6,5},{7,8},{8,7},{9,10},{10,9},{11,... | collective-permute-start | bytes 589832 | tf_op jit(solution)/shard_map/ppermute | solution.py:493
  9.9 1.3 %collective-permute-start = (f32[2,4,2,8,512]{4,3,2,1,0:T(8,128)S(1)}, f32[2,4,2,8,512]{4,3,2,1,0:T(8,128)S(1)}, u32[]{:S(2)}, u32[]{:S(2)}) collective-permute-start(f32[2,4,2,8,512]{4,3,2,1,0:T(8,128)S(1)} %get-tuple-element.47.refs_7_.refs_2_), channel_id=1, source_target_pairs={{0,16},{16,0},{1,17},{17,1},{2,18},{18,2},{3,19},{19,3},{4,20},{20... | collective-permute-start | bytes 786440 | tf_op jit(solution)/shard_map/ppermute | solution.py:482
  11.2 0.0 collective-permute-start.2
  11.3 1.3 %collective-permute-start.3 = (bf16[18,8,512]{2,1,0:T(8,128)(2,1)S(1)}, bf16[18,8,512]{2,1,0:T(8,128)(2,1)S(1)}, u32[]{:S(2)}, u32[]{:S(2)}) collective-permute-start(bf16[18,8,512]{2,1,0:T(8,128)(2,1)S(1)} %get-tuple-element.52), channel_id=1, source_target_pairs={{1,2},{2,1},{3,4},{4,3},{5,6},{6,5},{7,8},{8,7},{9,10},{10,9},{11,... | collective-permute-start | bytes 442376 | tf_op jit(solution)/shard_map/ppermute | solution.py:493
  12.6 0.0 collective-permute-done.2.refs_3_
  12.6 9.5 %collective-permute-done.3.refs_4_ = bf16[18,8,512]{2,1,0:T(8,128)(2,1)S(1)} collective-permute-done((bf16[18,8,512]{2,1,0:T(8,128)(2,1)S(1)}, bf16[18,8,512]{2,1,0:T(8,128)(2,1)S(1)}, u32[]{:S(2)}, u32[]{:S(2)}) %collective-permute-start.3) | collective-permute-done | bytes 147488 | tf_op jit(solution)/shard_map/ppermute | solution.py:493
  22.1 1.8 %shard_map.79 = (f32[2,4,128,128]{3,2,1,0:T(8,128)S(1)}, f32[1,128]{1,0:T(1,128)S(1)}, f32[8,8,512]{2,1,0:T(8,128)S(1)}, bf16[8,8,512]{2,1,0:T(8,128)(2,1)S(1)}, f32[3,4,192,128]{3,2,1,0:T(8,128)S(1)}) custom-call(f32[16,8,2,8,512]{4,3,2,1,0:T(8,128)S(1)} %get-tuple-element.45.refs_0_, f32[4,2,8,512]{3,2,1,0:T(8,128)S(1)} %get-tuple-element.46.refs_1_, ...), custom_call_target="tpu_custom_call" | custom-call | flops 8388608 | bytes 8388608 | tf_op jit(solution)/shard_map/pallas_call | solution.py:463
  23.9 0.0 collective-permute-done.4.refs_3_
  23.9 0.0 collective-permute-done.5.refs_4_
  23.9 2.5 %shard_map.80 = (f32[3,4,128,128]{3,2,1,0:T(8,128)S(1)}, f32[1,128]{1,0:T(1,128)S(1)}, f32[8,8,512]{2,1,0:T(8,128)S(1)}, bf16[12,8,512]{2,1,0:T(8,128)(2,1)S(1)}, f32[1,4,8,512]{3,2,1,0:T(8,128)S(1)}) custom-call(f32[16,8,2,8,512]{4,3,2,1,0:T(8,128)S(1)} %get-tuple-element.45.refs_0_, f32[4,2,8,512]{3,2,1,0:T(8,128)S(1)} %get-tuple-element.46.refs_1_, ...), custom_call_target="tpu_custom_call" | custom-call | flops 8388608 | bytes 8388608 | tf_op jit(solution)/shard_map/pallas_call | solution.py:463
  26.4 0.8 %collective-permute-start.7 = (bf16[12,8,512]{2,1,0:T(8,128)(2,1)S(1)}, bf16[12,8,512]{2,1,0:T(8,128)(2,1)S(1)}, u32[]{:S(2)}, u32[]{:S(2)}) collective-permute-start(bf16[12,8,512]{2,1,0:T(8,128)(2,1)S(1)} %get-tuple-element.58), channel_id=1, source_target_pairs={{0,16},{16,0},{1,17},{17,1},{2,18},{18,2},{3,19},{19,3},{4,20},{20... | collective-permute-start | bytes 294920 | tf_op jit(solution)/shard_map/ppermute | solution.py:482
  27.2 1.3 %collective-permute-start.6 = (bf16[8,8,512]{2,1,0:T(8,128)(2,1)S(1)}, bf16[8,8,512]{2,1,0:T(8,128)(2,1)S(1)}, u32[]{:S(2)}, u32[]{:S(2)}) collective-permute-start(bf16[8,8,512]{2,1,0:T(8,128)(2,1)S(1)} %get-tuple-element.57), channel_id=1, source_target_pairs={{0,16},{16,0},{1,17},{17,1},{2,18},{18,2},{3,19},{19,3},{4,20},{20... | collective-permute-start | bytes 196616 | tf_op jit(solution)/shard_map/ppermute | solution.py:482
  28.5 0.0 collective-permute-done
  28.5 3.3 %collective-permute-done.6 = bf16[8,8,512]{2,1,0:T(8,128)(2,1)S(1)} collective-permute-done((bf16[8,8,512]{2,1,0:T(8,128)(2,1)S(1)}, bf16[8,8,512]{2,1,0:T(8,128)(2,1)S(1)}, u32[]{:S(2)}, u32[]{:S(2)}) %collective-permute-start.6) | collective-permute-done | bytes 65568 | tf_op jit(solution)/shard_map/ppermute | solution.py:482
  31.8 0.0 collective-permute-done.7
  31.8 0.1 shard_map.81
  31.9 9.8 %all_to_all.10.refs_5_ = f32[32,1,256]{2,1,0:T(1,128)S(1)} all-to-all(f32[32,1,256]{2,1,0:T(1,128)S(1)} %get-tuple-element.63), channel_id=1, replica_groups=mesh['mem'=2,'row'=16] {'mem','row'}, dimensions={0} | all-to-all | bytes 65536 | tf_op jit(solution)/shard_map/all_to_all | solution.py:574
  41.7 0.6 shard_map.82
  42.3 0.2 collective-permute-start.10
  42.5 0.6 collective-permute-start.11
  43.1 0.0 collective-permute-start.8
  43.1 1.4 %collective-permute-start.9 = (bf16[16,8,512]{2,1,0:T(8,128)(2,1)S(1)}, bf16[16,8,512]{2,1,0:T(8,128)(2,1)S(1)}, u32[]{:S(2)}, u32[]{:S(2)}) collective-permute-start(bf16[16,8,512]{2,1,0:T(8,128)(2,1)S(1)} %get-tuple-element.65), channel_id=1, source_target_pairs={{1,2},{2,1},{3,4},{4,3},{5,6},{6,5},{7,8},{8,7},{9,10},{10,9},{11,... | collective-permute-start | bytes 393224 | tf_op jit(solution)/shard_map/ppermute | solution.py:493
  44.5 0.0 collective-permute-done.8.refs_3_
  44.5 5.0 %collective-permute-done.9.refs_4_ = bf16[16,8,512]{2,1,0:T(8,128)(2,1)S(1)} collective-permute-done((bf16[16,8,512]{2,1,0:T(8,128)(2,1)S(1)}, bf16[16,8,512]{2,1,0:T(8,128)(2,1)S(1)}, u32[]{:S(2)}, u32[]{:S(2)}) %collective-permute-start.9) | collective-permute-done | bytes 131104 | tf_op jit(solution)/shard_map/ppermute | solution.py:493
  49.6 1.7 %shard_map.83 = (f32[2,4,128,128]{3,2,1,0:T(8,128)S(1)}, f32[1,128]{1,0:T(1,128)S(1)}, f32[8,8,512]{2,1,0:T(8,128)S(1)}, bf16[1,4,8,512]{3,2,1,0:T(8,128)(2,1)S(1)}) custom-call(f32[16,8,2,8,512]{4,3,2,1,0:T(8,128)S(1)} %get-tuple-element.45.refs_0_, f32[4,2,8,512]{3,2,1,0:T(8,128)S(1)} %get-tuple-element.46.refs_1_, ...), custom_call_target="tpu_custom_call" | custom-call | flops 8388608 | bytes 8388608 | tf_op jit(solution)/shard_map/pallas_call | solution.py:463
  51.3 0.6 collective-permute-start.12
  51.9 0.0 collective-permute-done.10.refs_3_
  51.9 0.0 collective-permute-done.11.refs_4_
  51.9 2.5 %shard_map.84 = (f32[3,4,128,128]{3,2,1,0:T(8,128)S(1)}, f32[1,128]{1,0:T(1,128)S(1)}, f32[8,8,512]{2,1,0:T(8,128)S(1)}, bf16[1,4,8,512]{3,2,1,0:T(8,128)(2,1)S(1)}, f32[1,4,8,512]{3,2,1,0:T(8,128)S(1)}) custom-call(f32[16,8,2,8,512]{4,3,2,1,0:T(8,128)S(1)} %get-tuple-element.45.refs_0_, f32[4,2,8,512]{3,2,1,0:T(8,128)S(1)} %get-tuple-element.46.refs_1_, ...), custom_call_target="tpu_custom_call" | custom-call | flops 8388608 | bytes 8388608 | tf_op jit(solution)/shard_map/pallas_call | solution.py:463
  54.4 1.5 %collective-permute-start.13 = (bf16[4,8,512]{2,1,0:T(8,128)(2,1)S(1)}, bf16[4,8,512]{2,1,0:T(8,128)(2,1)S(1)}, u32[]{:S(2)}, u32[]{:S(2)}) collective-permute-start(bf16[4,8,512]{2,1,0:T(8,128)(2,1)S(1)} %bitcast.16), channel_id=1, source_target_pairs={{0,16},{16,0},{1,17},{17,1},{2,18},{18,2},{3,19},{19,3},{4,20},{20... | collective-permute-start | bytes 98312 | tf_op jit(solution)/shard_map/ppermute | solution.py:482
  55.9 0.0 collective-permute-done.12
  55.9 2.7 %collective-permute-done.13 = bf16[4,8,512]{2,1,0:T(8,128)(2,1)S(1)} collective-permute-done((bf16[4,8,512]{2,1,0:T(8,128)(2,1)S(1)}, bf16[4,8,512]{2,1,0:T(8,128)(2,1)S(1)}, u32[]{:S(2)}, u32[]{:S(2)}) %collective-permute-start.13) | collective-permute-done | bytes 32800 | tf_op jit(solution)/shard_map/ppermute | solution.py:482
  58.6 0.1 shard_map.85
  58.8 11.7 %all_to_all.11.got = f32[32,1,256]{2,1,0:T(1,128)S(1)} all-to-all(f32[32,1,256]{2,1,0:T(1,128)S(1)} %get-tuple-element.77), channel_id=1, replica_groups=mesh['mem'=2,'row'=16] {'mem','row'}, dimensions={0} | all-to-all | bytes 65536 | tf_op jit(solution)/shard_map/all_to_all | solution.py:574
  70.4 1.9 %shard_map.86 = (f32[16,2,8,512]{3,2,1,0:T(8,128)}, f32[4,2,8,512]{3,2,1,0:T(8,128)}, f32[4,2,8,512]{3,2,1,0:T(8,128)}) custom-call(f32[32,1,256]{2,1,0:T(1,128)S(1)} %all_to_all.11.got, f32[1,128]{1,0:T(1,128)S(1)} %get-tuple-element.67.refs_7_.refs_9_.step, f32[8,2,8,512]{3,2,1,0:T(8,128)S(1)} %get-tuple-element.62.refs_4_.refs_8_.image0, ...), custom_call_target="tpu_custom_call" | custom-call | tf_op jit(solution)/shard_map/pallas_call | solution.py:463
Async XLA Ops:
  1.7 6.6 %collective-permute-start.1 = (bf16[4,2,8,512]{3,2,1,0:T(8,128)(2,1)S(1)}, bf16[4,2,8,512]{3,2,1,0:T(8,128)(2,1)S(1)}, u32[]{:S(2)}, u32[]{:S(2)}) collective-permute-start(bf16[4,2,8,512]{3,2,1,0:T(8,128)(2,1)S(1)} %get-tuple-element.44.own), channel_id=1, source_target_pairs={{0,16},{16,0},{1,17},{17,1},{2,18},{18,2},{3,19},{19,3},{4,20},{20... | collective-permute-start | bytes 196616 | tf_op jit(solution)/shard_map/ppermute | solution.py:482
  9.1 14.8 %collective-permute-start.4 = (bf16[24,8,512]{2,1,0:T(8,128)(2,1)S(1)}, bf16[24,8,512]{2,1,0:T(8,128)(2,1)S(1)}, u32[]{:S(2)}, u32[]{:S(2)}) collective-permute-start(bf16[24,8,512]{2,1,0:T(8,128)(2,1)S(1)} %get-tuple-element.54), channel_id=1, source_target_pairs={{0,1},{1,0},{2,3},{3,2},{4,5},{5,4},{6,7},{7,6},{8,9},{9,8},{10,11... | collective-permute-start | bytes 589832 | tf_op jit(solution)/shard_map/ppermute | solution.py:485
  9.2 14.8 %collective-permute-start.5 = (bf16[24,8,512]{2,1,0:T(8,128)(2,1)S(1)}, bf16[24,8,512]{2,1,0:T(8,128)(2,1)S(1)}, u32[]{:S(2)}, u32[]{:S(2)}) collective-permute-start(bf16[24,8,512]{2,1,0:T(8,128)(2,1)S(1)} %get-tuple-element.54), channel_id=1, source_target_pairs={{1,2},{2,1},{3,4},{4,3},{5,6},{6,5},{7,8},{8,7},{9,10},{10,9},{11,... | collective-permute-start | bytes 589832 | tf_op jit(solution)/shard_map/ppermute | solution.py:493
  9.9 18.6 %collective-permute-start = (f32[2,4,2,8,512]{4,3,2,1,0:T(8,128)S(1)}, f32[2,4,2,8,512]{4,3,2,1,0:T(8,128)S(1)}, u32[]{:S(2)}, u32[]{:S(2)}) collective-permute-start(f32[2,4,2,8,512]{4,3,2,1,0:T(8,128)S(1)} %get-tuple-element.47.refs_7_.refs_2_), channel_id=1, source_target_pairs={{0,16},{16,0},{1,17},{17,1},{2,18},{18,2},{3,19},{19,3},{4,20},{20... | collective-permute-start | bytes 786440 | tf_op jit(solution)/shard_map/ppermute | solution.py:482
  11.2 1.4 %collective-permute-start.2 = (bf16[18,8,512]{2,1,0:T(8,128)(2,1)S(1)}, bf16[18,8,512]{2,1,0:T(8,128)(2,1)S(1)}, u32[]{:S(2)}, u32[]{:S(2)}) collective-permute-start(bf16[18,8,512]{2,1,0:T(8,128)(2,1)S(1)} %get-tuple-element.52), channel_id=1, source_target_pairs={{0,1},{1,0},{2,3},{3,2},{4,5},{5,4},{6,7},{7,6},{8,9},{9,8},{10,11... | collective-permute-start | bytes 442376 | tf_op jit(solution)/shard_map/ppermute | solution.py:485
  11.3 10.8 %collective-permute-start.3 = (bf16[18,8,512]{2,1,0:T(8,128)(2,1)S(1)}, bf16[18,8,512]{2,1,0:T(8,128)(2,1)S(1)}, u32[]{:S(2)}, u32[]{:S(2)}) collective-permute-start(bf16[18,8,512]{2,1,0:T(8,128)(2,1)S(1)} %get-tuple-element.52), channel_id=1, source_target_pairs={{1,2},{2,1},{3,4},{4,3},{5,6},{6,5},{7,8},{8,7},{9,10},{10,9},{11,... | collective-permute-start | bytes 442376 | tf_op jit(solution)/shard_map/ppermute | solution.py:493
  26.4 5.4 %collective-permute-start.7 = (bf16[12,8,512]{2,1,0:T(8,128)(2,1)S(1)}, bf16[12,8,512]{2,1,0:T(8,128)(2,1)S(1)}, u32[]{:S(2)}, u32[]{:S(2)}) collective-permute-start(bf16[12,8,512]{2,1,0:T(8,128)(2,1)S(1)} %get-tuple-element.58), channel_id=1, source_target_pairs={{0,16},{16,0},{1,17},{17,1},{2,18},{18,2},{3,19},{19,3},{4,20},{20... | collective-permute-start | bytes 294920 | tf_op jit(solution)/shard_map/ppermute | solution.py:482
  27.2 4.6 %collective-permute-start.6 = (bf16[8,8,512]{2,1,0:T(8,128)(2,1)S(1)}, bf16[8,8,512]{2,1,0:T(8,128)(2,1)S(1)}, u32[]{:S(2)}, u32[]{:S(2)}) collective-permute-start(bf16[8,8,512]{2,1,0:T(8,128)(2,1)S(1)} %get-tuple-element.57), channel_id=1, source_target_pairs={{0,16},{16,0},{1,17},{17,1},{2,18},{18,2},{3,19},{19,3},{4,20},{20... | collective-permute-start | bytes 196616 | tf_op jit(solution)/shard_map/ppermute | solution.py:482
  42.3 9.6 %collective-permute-start.10 = (bf16[24,8,512]{2,1,0:T(8,128)(2,1)S(1)}, bf16[24,8,512]{2,1,0:T(8,128)(2,1)S(1)}, u32[]{:S(2)}, u32[]{:S(2)}) collective-permute-start(bf16[24,8,512]{2,1,0:T(8,128)(2,1)S(1)} %get-tuple-element.69), channel_id=1, source_target_pairs={{0,1},{1,0},{2,3},{3,2},{4,5},{5,4},{6,7},{7,6},{8,9},{9,8},{10,11... | collective-permute-start | bytes 589832 | tf_op jit(solution)/shard_map/ppermute | solution.py:485
  42.5 9.4 %collective-permute-start.11 = (bf16[24,8,512]{2,1,0:T(8,128)(2,1)S(1)}, bf16[24,8,512]{2,1,0:T(8,128)(2,1)S(1)}, u32[]{:S(2)}, u32[]{:S(2)}) collective-permute-start(bf16[24,8,512]{2,1,0:T(8,128)(2,1)S(1)} %get-tuple-element.69), channel_id=1, source_target_pairs={{1,2},{2,1},{3,4},{4,3},{5,6},{6,5},{7,8},{8,7},{9,10},{10,9},{11,... | collective-permute-start | bytes 589832 | tf_op jit(solution)/shard_map/ppermute | solution.py:493
  43.1 1.5 %collective-permute-start.8 = (bf16[16,8,512]{2,1,0:T(8,128)(2,1)S(1)}, bf16[16,8,512]{2,1,0:T(8,128)(2,1)S(1)}, u32[]{:S(2)}, u32[]{:S(2)}) collective-permute-start(bf16[16,8,512]{2,1,0:T(8,128)(2,1)S(1)} %get-tuple-element.65), channel_id=1, source_target_pairs={{0,1},{1,0},{2,3},{3,2},{4,5},{5,4},{6,7},{7,6},{8,9},{9,8},{10,11... | collective-permute-start | bytes 393224 | tf_op jit(solution)/shard_map/ppermute | solution.py:485
  43.1 6.4 %collective-permute-start.9 = (bf16[16,8,512]{2,1,0:T(8,128)(2,1)S(1)}, bf16[16,8,512]{2,1,0:T(8,128)(2,1)S(1)}, u32[]{:S(2)}, u32[]{:S(2)}) collective-permute-start(bf16[16,8,512]{2,1,0:T(8,128)(2,1)S(1)} %get-tuple-element.65), channel_id=1, source_target_pairs={{1,2},{2,1},{3,4},{4,3},{5,6},{6,5},{7,8},{8,7},{9,10},{10,9},{11,... | collective-permute-start | bytes 393224 | tf_op jit(solution)/shard_map/ppermute | solution.py:493
  51.3 4.7 %collective-permute-start.12 = (bf16[4,8,512]{2,1,0:T(8,128)(2,1)S(1)}, bf16[4,8,512]{2,1,0:T(8,128)(2,1)S(1)}, u32[]{:S(2)}, u32[]{:S(2)}) collective-permute-start(bf16[4,8,512]{2,1,0:T(8,128)(2,1)S(1)} %bitcast.15), channel_id=1, source_target_pairs={{0,16},{16,0},{1,17},{17,1},{2,18},{18,2},{3,19},{19,3},{4,20},{20... | collective-permute-start | bytes 98312 | tf_op jit(solution)/shard_map/ppermute | solution.py:482
  54.4 4.2 %collective-permute-start.13 = (bf16[4,8,512]{2,1,0:T(8,128)(2,1)S(1)}, bf16[4,8,512]{2,1,0:T(8,128)(2,1)S(1)}, u32[]{:S(2)}, u32[]{:S(2)}) collective-permute-start(bf16[4,8,512]{2,1,0:T(8,128)(2,1)S(1)} %bitcast.16), channel_id=1, source_target_pairs={{0,16},{16,0},{1,17},{17,1},{2,18},{18,2},{3,19},{19,3},{4,20},{20... | collective-permute-start | bytes 98312 | tf_op jit(solution)/shard_map/ppermute | solution.py:482

commit v8 on v7

--- a/solution.py
+++ b/solution.py
@@ -36,6 +36,7 @@
         self.ST = -(-(self.S * self.L) // SUB)
         self.PM = self.L * self.KT
         self.PN = self.PM + self.ST
+        self.chunks = self.L + 1
         self.C = self.X // LANES
         self.RE = self.R + 4 * SWEEPS
         self.RG = self.R + 2 * SWEEPS
@@ -43,18 +44,17 @@
         self.ens = math.sqrt(0.7 / (self.K * mem - 1))
         self.stat = math.sqrt(0.3)
 
-    def fields(self, level):
-        own = [(k, level) for k in range(self.K)]
-        return own + [(self.K + s, l) for s in range(self.S) for l in range(self.L)] if level == self.L - 1 else own
-
-    def tiles(self, level):
-        return self.KT + self.ST if level == self.L - 1 else self.KT
+    def fields(self, chunk):
+        if chunk == 0:
+            return [(self.K + s, l) for s in range(self.S) for l in range(self.L)]
+        return [(k, chunk - 1) for k in range(self.K)]
+
+    def tiles(self, chunk):
+        return self.KT if chunk else self.ST
 
     def inner(self, field, level):
-        if field < self.K:
-            return field // SUB, field % SUB
-        at = (field - self.K) * self.L + level
-        return self.KT + at // SUB, at % SUB
+        at = field if field < self.K else (field - self.K) * self.L + level
+        return at // SUB, at % SUB
 
     def slot(self, field, level):
         if field < self.K:
@@ -193,7 +193,7 @@
                     tile, lane = p.slot(p.K + s, l)
                     value = p.stat * static_scale[s, l] * rounded
                     scatter(back, tile, strided(lane, p.R), value)
-                    msgs[p.L - 1][p.K + s * p.L + l] = value.astype(bf16)
+                    msgs[0][s * p.L + l] = value.astype(bf16)
     if first:
         for l in range(p.L):
             msgs[0][len(p.fields(0)) + l] = scale_index[l].astype(bf16)
@@ -205,7 +205,7 @@
             value = p.ens * value
             tile, lane = p.slot(k, l)
             scatter(back, tile, strided(lane, p.R), value)
-            msgs[l][k] = value.astype(bf16)
+            msgs[l + 1][k] = value.astype(bf16)
 
 
 def sideways(u, first_lane, last_lane):
@@ -221,21 +221,28 @@
     return [(above[c] + below[c]) + across[c] - 4.0 * here[c] for c in range(len(here))]
 
 
-def sweep_kernel(p, first, level, *refs):
+def sweep_kernel(p, first, chunk, *refs):
     refs = list(refs)
-    members, static_scale, back, near, far = refs[:5]
-    refs = refs[5:]
-    if first and level == 0:
+    source_of, back, near, far = refs[:4]
+    refs = refs[4:]
+    builds = first and chunk == 0
+    if builds:
         scale_index, *refs = refs
     else:
         kap, *refs = refs
+    if chunk:
+        members, level = source_of, chunk - 1
+        rest, *refs = refs
+    else:
+        static_scale = source_of
     if not first:
         before, step, *refs = refs
-    grad, norm, part, ship, *refs = refs
-    last = level == p.L - 1
-    if last and p.L > 1:
+    grad, norm, *refs = refs
+    if chunk:
+        part, ship, *refs = refs
+    else:
         rest, *refs = refs
-    if first and level == 0:
+    if builds:
         kap, *refs = refs
     ends, a, b, out = refs
     me, at = lax.axis_index("mem"), lax.axis_index("row")
@@ -243,8 +250,8 @@
     high_ok = jnp.where(at < p.row - 1, 1.0, 0.0).astype(f32)
     R, RE, W = p.R, p.RE, SWEEPS
     H = 2 * W
-    fields = p.fields(level)
-    count = p.tiles(level)
+    fields = p.fields(chunk)
+    count = p.tiles(chunk)
     odd = lax.rem(at, 2)
     if p.pads:
         ends[...] = jnp.zeros(ends.shape, f32)
@@ -258,7 +265,7 @@
         for i, (field, l) in enumerate(fields):
             tile, lane = p.inner(field, l)
             scatter(ends.at[side], tile, strided(lane, H), edge(ref[i].astype(f32), side))
-    if first and level == 0:
+    if builds:
         for l in range(p.L):
             pieces_of = [(table(scale_index[l], kappa_table), H)]
             for ref, side in ((near, 1 - odd), (far, odd)):
@@ -287,10 +294,7 @@
         step_tile = jnp.broadcast_to(step[0:1, 0:1], (SUB, LANES))
 
     def problem(t, total):
-        which, whole = level, t + level * p.KT
-        if last:
-            which = jnp.where(t < p.KT, level, t - p.KT + p.L)
-            whole = jnp.where(t < p.KT, whole, t - p.KT + p.PM)
+        which, whole = (level, t + level * p.KT) if chunk else (t + p.L, t + p.PM)
         source = None
         for sweep in range(W):
             target = (a, b)[sweep % 2]
@@ -347,6 +351,12 @@
 
     total = lax.fori_loop(0, count, problem, jnp.zeros((SUB, LANES), f32))
     norm[...] = jnp.sum(total, axis=0, keepdims=True)
+    if chunk == 0:
+        for s in range(p.S):
+            for l in range(p.L):
+                tile, j = p.inner(p.K + s, l)
+                rest[l, s] = p.stat * static_scale[s, l] * gather(out, tile, strided(j, R))
+        return
     sums = [None] * p.V
     for k in range(p.K):
         tile, j = p.inner(k, level)
@@ -356,23 +366,12 @@
             sums[v] = term if k == 0 else sums[v] + term
     for v in range(p.V):
         part[v] = p.ens * sums[v]
-    if last:
-        for s in range(p.S):
-            own = me * p.S + s
-            for l in range(p.L):
-                tile, j = p.inner(p.K + s, l)
-                value = p.stat * static_scale[s, l] * gather(out, tile, strided(j, R))
-                if l == level:
-                    part[own] = part[own] + value
-                else:
-                    rest[l, s] = value
+    for s in range(p.S):
+        own = me * p.S + s
+        part[own] = part[own] + rest[level, s]
     if first:
         for v in range(p.V):
             ship[v] = part[v].astype(bf16)
-        if last:
-            for l in range(p.L - 1):
-                for s in range(p.S):
-                    ship[p.V + l * p.S + s] = rest[l, s].astype(bf16)
         return
     for shift in range(1, p.mem):
         base = lax.rem(me + shift, p.mem) * p.S
@@ -381,9 +380,8 @@
 
 
 def curvature_kernel(p, first, *refs):
-    parts, gots, norms, refs = refs[: p.L], refs[p.L : 2 * p.L], refs[2 * p.L : 3 * p.L], refs[3 * p.L :]
-    if p.L > 1:
-        rest, *refs = refs
+    parts, gots, norms = refs[: p.L], refs[p.L : 2 * p.L], refs[2 * p.L : 3 * p.L + 1]
+    refs = refs[3 * p.L + 1 :]
     if first:
         pack, _, image, send = refs
     else:
@@ -397,14 +395,6 @@
                 for other in range(p.mem - 1):
                     value = value + gots[l][other, v].astype(f32)
                 image[v, l] = value
-            if l < p.L - 1:
-                for s in range(p.S):
-                    own = me * p.S + s
-                    image[own, l] = image[own, l] + rest[l, s]
-                    for other in range(p.mem - 1):
-                        theirs = lax.rem(me + (p.mem - 1 - other), p.mem) * p.S + s
-                        value = gots[p.L - 1][other, p.V + l * p.S + s].astype(f32)
-                        image[theirs, l] = image[theirs, l] + value
         for s in range(p.S):
             own = me * p.S + s
             if first:
@@ -412,8 +402,6 @@
                 misfit = -pack[0, s, l]
             else:
                 value = parts[l][own]
-                if l < p.L - 1:
-                    value = value + rest[l, s]
                 for other in range(p.mem - 1):
                     value = value + gots[l][other, s].astype(f32)
                 image[s, l] = value
@@ -429,7 +417,7 @@
 
 
 def final_kernel(p, got, step, image0, image1, matrix_ref, *refs):
-    before, after, outs = refs[: p.L], refs[p.L : 2 * p.L], refs[2 * p.L :]
+    before, after, outs = refs[: p.chunks], refs[p.chunks : 2 * p.chunks], refs[2 * p.chunks :]
     control, static_control, increment = outs
     me = lax.axis_index("mem")
     total = jnp.sum(got[...], axis=0)
@@ -440,11 +428,11 @@
     matrix = matrix_ref[...]
 
     targets, blocks = [], []
-    for level in range(p.L):
-        for field, l in p.fields(level):
+    for chunk in range(p.chunks):
+        for field, l in p.fields(chunk):
             tile, lane = p.inner(field, l)
             where = strided(SWEEPS * SUB + lane, p.R)
-            blocks.append(-(first * gather(before[level], tile, where)) - second * gather(after[level], tile, where))
+            blocks.append(-(first * gather(before[chunk], tile, where)) - second * gather(after[chunk], tile, where))
             targets.append((control, field, l) if field < p.K else (static_control, field - p.K, l))
     for s in range(p.S):
         for l in range(p.L):
@@ -517,7 +505,7 @@
     grads, image, step, kap, sums = [], None, None, None, None
     for turn in range(ITERS):
         first = turn == 0
-        sizes = [len(p.fields(level)) for level in range(L)]
+        sizes = [len(p.fields(chunk)) for chunk in range(p.chunks)]
         if first:
             sizes[0] += L
         msg_shapes = [((size, R, X), bf16) for size in sizes]
@@ -535,42 +523,44 @@
             far = across(msg)
             halos.append((near, far))
         grad, norms, partial_images, gots, rest = [], [], [], [], None
-        for level in range(L):
-            count = p.tiles(level)
-            args = [members, static_scale, back, *halos[level]]
-            args += [scale_index] if first and level == 0 else [kap]
-            args += [] if first else [grads[0][level], step]
-            last = level == L - 1
-            ship_shape = (V + (L - 1) * S if last else V, R, X) if first else (p.mem - 1, S, R, X)
-            outs = [((count, C, p.RG * SUB, LANES), f32), line, ((V, R, X), f32), (ship_shape, bf16)]
-            if last and L > 1:
-                outs.append(((L - 1, S, R, X), f32))
-            if first and level == 0:
+        for chunk in range(p.chunks):
+            count = p.tiles(chunk)
+            builds = first and chunk == 0
+            args = [members if chunk else static_scale, back, *halos[chunk], scale_index if builds else kap]
+            args += [rest] if chunk else []
+            args += [] if first else [grads[0][chunk], step]
+            outs = [((count, C, p.RG * SUB, LANES), f32), line]
+            if chunk:
+                outs += [((V, R, X), f32), ((V, R, X) if first else (p.mem - 1, S, R, X), bf16)]
+            else:
+                outs.append(((L, S, R, X), f32))
+            if builds:
                 outs.append(((L + p.ST, C, p.RE * SUB, LANES), f32))
             halo = vmem((2, count, C, 2 * SWEEPS * SUB, LANES))
             work = [halo, vmem((C, p.RE * SUB, LANES)), vmem((C, p.RE * SUB, LANES))]
-            g, norm, partial_image, ship, *more = call(
-                part(sweep_kernel, p, first, level), outs, work + [vmem((count, C, R * SUB, LANES))],
+            g, norm, *more = call(
+                part(sweep_kernel, p, first, chunk), outs, work + [vmem((count, C, R * SUB, LANES))],
                 cost=8 << 20,
             )(*args)
-            if last and L > 1:
-                rest, *more = more
-            if first and level == 0:
-                kap = more[0]
             grad.append(g)
             norms.append(norm)
-            partial_images.append(partial_image)
-            gots.append(jnp.stack([round_mem(ship if first else ship[shift - 1], shift) for shift in shifts]))
+            if builds:
+                rest, kap = more
+            elif chunk == 0:
+                (rest,) = more
+            else:
+                partial_image, ship = more
+                partial_images.append(partial_image)
+                gots.append(jnp.stack([round_mem(ship if first else ship[shift - 1], shift) for shift in shifts]))
         grads.append(grad)
-        extra = [rest] if L > 1 else []
         if first:
             image, send = call(
                 part(curvature_kernel, p, True), [(full_shape, f32), send_shape], [],
-            )(*partial_images, *gots, *norms, *extra, pack, pack_in)
+            )(*partial_images, *gots, *norms, pack, pack_in)
         else:
             final_image, send = call(
                 part(curvature_kernel, p, False), [(own_shape, f32), send_shape], [],
-            )(*partial_images, *gots, *norms, *extra, pack, image, step)
+            )(*partial_images, *gots, *norms, pack, image, step)
         sums = lax.all_to_all(send, ("mem", "row"), 0, 0)
     return call(
         part(final_kernel, p),

time: 72.5 us -> 67.7 us (0.934)
  waiting for transfers between devices: 20.5 us -> 12.6 us
  starting transfers between devices: 13 us -> 16.6 us
    ppermute x4 -> x6, waiting for transfers between devices: 14.5 us -> 5.82 us  [across(): return lax.ppermute(block, ('mem', 'row'), pairs)]
    ppermute x4 -> x6, starting transfers between devices: 0.3 us -> 3.04 us  [inside(): return lax.ppermute(block, 'row', [(i, i ^ 1) for i in range(p.row)])]
    ppermute x4 -> x6, starting transfers between devices: 4.08 us -> 5.43 us  [across(): return lax.ppermute(block, ('mem', 'row'), pairs)]
    ppermute x4 -> x6, waiting for transfers between devices: 0.05 us -> 1.26 us  [inside(): return lax.ppermute(block, 'row', [(i, i ^ 1) for i in range(p.row)])]
    pallas_call x11 -> x13, Pallas kernels: 16.5 us -> 16.4 us  [run(): pl.pallas_call(kernel, out_shape=tuple((jax.ShapeDtypeStruct(shape, dtype...]
  transfers between devices with their start and end apart: 14 -> 18, of which waited for: 4 -> 8; matrix products, arithmetic and copies ran while one was open for 0% -> 0% of each run, Pallas kernels for 17% -> 18%
where the time goes in v8:
time: 67.7 us; the launch traced here: 67.5 us
  blocking collectives  21.2 us (31%)
  starting transfers between devices  16.6 us (25%)
  Pallas kernels  16.4 us (24%)
  waiting for transfers between devices  12.6 us (19%)
  between operations  0.75 us (1%)
    all_to_all x2, blocking collectives, local(): sums = lax.all_to_all(send, ('mem', 'row'), 0, 0)  21.2 us
    pallas_call x13, Pallas kernels, run(): pl.pallas_call(kernel, out_shape=tuple((jax.ShapeDtypeStruct(shape, dtype...  16.4 us
    ppermute x6, starting transfers between devices, round_mem(): lax.ppermute(block, 'mem', [(i, (i + shift) % p.mem) for i in range(p.mem)])  8.08 us
    ppermute x6, waiting for transfers between devices, across(): return lax.ppermute(block, ('mem', 'row'), pairs)  5.82 us
    ppermute x6, waiting for transfers between devices, round_mem(): lax.ppermute(block, 'mem', [(i, (i + shift) % p.mem) for i in range(p.mem)])  5.5 us
    ppermute x6, starting transfers between devices, across(): return lax.ppermute(block, ('mem', 'row'), pairs)  5.43 us
    ppermute x6, starting transfers between devices, inside(): return lax.ppermute(block, 'row', [(i, i ^ 1) for i in range(p.row)])  3.04 us
  transfers between devices with their start and end apart: 18, of which 8 were waited for; matrix products, arithmetic and copies ran while one was open for 0% of the time, Pallas kernels for 18%

profile of v8, /device:TPU:0, one launch (start us, length us, event | category | flops | bytes accessed | tf_op | source)
XLA Modules:
  0.0 67.5 jit_solution(10285683575492903878)
XLA Ops:
  0.6 1.0 %shard_map.76 = (f32[4,2,8,512]{3,2,1,0:T(8,128)S(1)}, s32[4,2,8,512]{3,2,1,0:T(8,128)S(1)}, bf16[4,2,8,512]{3,2,1,0:T(8,128)(2,1)S(1)}) custom-call(f32[4,2,8,512]{3,2,1,0:T(8,128)} %obs.1, s32[4,2,8,512]{3,2,1,0:T(8,128)} %cls.1), custom_call_target="tpu_custom_call" | custom-call | tf_op jit(solution)/shard_map/pallas_call | solution.py:451
  1.7 3.1 %collective-permute-start.1 = (bf16[4,2,8,512]{3,2,1,0:T(8,128)(2,1)S(1)}, bf16[4,2,8,512]{3,2,1,0:T(8,128)(2,1)S(1)}, u32[]{:S(2)}, u32[]{:S(2)}) collective-permute-start(bf16[4,2,8,512]{3,2,1,0:T(8,128)(2,1)S(1)} %get-tuple-element.50.own), channel_id=1, source_target_pairs={{0,16},{16,0},{1,17},{17,1},{2,18},{18,2},{3,19},{19,3},{4,20},{20... | collective-permute-start | bytes 196616 | tf_op jit(solution)/shard_map/ppermute | solution.py:470
  4.7 3.5 %shard_map.77 = (f32[16,8,2,8,512]{4,3,2,1,0:T(8,128)S(1)}, f32[4,2,8,512]{3,2,1,0:T(8,128)S(1)}, f32[2,8,512]{2,1,0:T(8,128)S(1)}, f32[2,4,2,8,512]{4,3,2,1,0:T...) custom-call(bf16[16,8,2,8,512]{4,3,2,1,0:T(8,128)(2,1)} %members.1, ...), custom_call_target="tpu_custom_call" | custom-call | flops 4194304 | bytes 4194304 | tf_op jit(solution)/shard_map/pallas_call | solution.py:451
  8.3 0.0 collective-permute-done.1
  8.3 0.8 %shard_map.78 = (f32[5,4,64,128]{3,2,1,0:T(8,128)S(1)}, bf16[10,8,512]{2,1,0:T(8,128)(2,1)S(1)}, bf16[16,8,512]{2,1,0:T(8,128)(2,1)S(1)}, bf16[16,8,512]{2,1,0:T(8,128)(2,1)S(1)}) custom-call(f32[16,8,2,8,512]{4,3,2,1,0:T(8,128)S(1)} %get-tuple-element.51.refs_0_, f32[4,2,8,512]{3,2,1,0:T(8,128)S(1)} %get-tuple-element.52.refs_1_.refs_0_, ...), custom_call_target="tpu_custom_call" | custom-call | tf_op jit(solution)/shard_map/pallas_call | solution.py:451
  9.1 0.8 %collective-permute-start.5 = (bf16[10,8,512]{2,1,0:T(8,128)(2,1)S(1)}, bf16[10,8,512]{2,1,0:T(8,128)(2,1)S(1)}, u32[]{:S(2)}, u32[]{:S(2)}) collective-permute-start(bf16[10,8,512]{2,1,0:T(8,128)(2,1)S(1)} %get-tuple-element.59), channel_id=1, source_target_pairs={{1,2},{2,1},{3,4},{4,3},{5,6},{6,5},{7,8},{8,7},{9,10},{10,9},{11,... | collective-permute-start | bytes 245768 | tf_op jit(solution)/shard_map/ppermute | solution.py:481
  9.9 0.9 %collective-permute-start.4 = (bf16[10,8,512]{2,1,0:T(8,128)(2,1)S(1)}, bf16[10,8,512]{2,1,0:T(8,128)(2,1)S(1)}, u32[]{:S(2)}, u32[]{:S(2)}) collective-permute-start(bf16[10,8,512]{2,1,0:T(8,128)(2,1)S(1)} %get-tuple-element.59), channel_id=1, source_target_pairs={{0,1},{1,0},{2,3},{3,2},{4,5},{5,4},{6,7},{7,6},{8,9},{9,8},{10,11... | collective-permute-start | bytes 245768 | tf_op jit(solution)/shard_map/ppermute | solution.py:473
  10.8 0.7 %collective-permute-start = (f32[2,4,2,8,512]{4,3,2,1,0:T(8,128)S(1)}, f32[2,4,2,8,512]{4,3,2,1,0:T(8,128)S(1)}, u32[]{:S(2)}, u32[]{:S(2)}) collective-permute-start(f32[2,4,2,8,512]{4,3,2,1,0:T(8,128)S(1)} %get-tuple-element.53.refs_7_.refs_2_), channel_id=1, source_target_pairs={{0,16},{16,0},{1,17},{17,1},{2,18},{18,2},{3,19},{19,3},{4,20},{20... | collective-permute-start | bytes 786440 | tf_op jit(solution)/shard_map/ppermute | solution.py:470
  11.5 1.3 %collective-permute-start.7 = (bf16[16,8,512]{2,1,0:T(8,128)(2,1)S(1)}, bf16[16,8,512]{2,1,0:T(8,128)(2,1)S(1)}, u32[]{:S(2)}, u32[]{:S(2)}) collective-permute-start(bf16[16,8,512]{2,1,0:T(8,128)(2,1)S(1)} %get-tuple-element.63), channel_id=1, source_target_pairs={{1,2},{2,1},{3,4},{4,3},{5,6},{6,5},{7,8},{8,7},{9,10},{10,9},{11,... | collective-permute-start | bytes 393224 | tf_op jit(solution)/shard_map/ppermute | solution.py:481
  12.8 0.3 collective-permute-start.6
  13.1 0.7 %collective-permute-done.5.refs_3_ = bf16[10,8,512]{2,1,0:T(8,128)(2,1)S(1)} collective-permute-done((bf16[10,8,512]{2,1,0:T(8,128)(2,1)S(1)}, bf16[10,8,512]{2,1,0:T(8,128)(2,1)S(1)}, u32[]{:S(2)}, u32[]{:S(2)}) %collective-permute-start.5) | collective-permute-done | bytes 81952 | tf_op jit(solution)/shard_map/ppermute | solution.py:481
  13.8 0.6 collective-permute-start.3
  14.5 1.1 %collective-permute-start.2 = (bf16[16,8,512]{2,1,0:T(8,128)(2,1)S(1)}, bf16[16,8,512]{2,1,0:T(8,128)(2,1)S(1)}, u32[]{:S(2)}, u32[]{:S(2)}) collective-permute-start(bf16[16,8,512]{2,1,0:T(8,128)(2,1)S(1)} %get-tuple-element.58), channel_id=1, source_target_pairs={{0,1},{1,0},{2,3},{3,2},{4,5},{5,4},{6,7},{7,6},{8,9},{9,8},{10,11... | collective-permute-start | bytes 393224 | tf_op jit(solution)/shard_map/ppermute | solution.py:473
  15.5 0.9 %shard_map.79 = (f32[1,4,128,128]{3,2,1,0:T(8,128)S(1)}, f32[1,128]{1,0:T(1,128)S(1)}, f32[2,4,8,512]{3,2,1,0:T(8,128)S(1)}, f32[3,4,192,128]{3,2,1,0:T(8,128)S(1)}) custom-call(f32[4,2,8,512]{3,2,1,0:T(8,128)S(1)} %get-tuple-element.52.refs_1_.refs_0_, f32[5,4,64,128]{3,2,1,0:T(8,128)S(1)} %get-tuple-element.57.refs_1_, ...), custom_call_target="tpu_custom_call" | custom-call | flops 8388608 | bytes 8388608 | tf_op jit(solution)/shard_map/pallas_call | solution.py:451
  16.4 4.2 %collective-permute-done.7.refs_3_ = bf16[16,8,512]{2,1,0:T(8,128)(2,1)S(1)} collective-permute-done((bf16[16,8,512]{2,1,0:T(8,128)(2,1)S(1)}, bf16[16,8,512]{2,1,0:T(8,128)(2,1)S(1)}, u32[]{:S(2)}, u32[]{:S(2)}) %collective-permute-start.7) | collective-permute-done | bytes 131104 | tf_op jit(solution)/shard_map/ppermute | solution.py:481
  20.6 1.7 %shard_map.81 = (f32[2,4,128,128]{3,2,1,0:T(8,128)S(1)}, f32[1,128]{1,0:T(1,128)S(1)}, f32[8,8,512]{2,1,0:T(8,128)S(1)}, bf16[8,8,512]{2,1,0:T(8,128)(2,1)S(1)}) custom-call(f32[16,8,2,8,512]{4,3,2,1,0:T(8,128)S(1)} %get-tuple-element.51.refs_0_, f32[5,4,64,128]{3,2,1,0:T(8,128)S(1)} %get-tuple-element.57.refs_1_, ...), custom_call_target="tpu_custom_call" | custom-call | flops 8388608 | bytes 8388608 | tf_op jit(solution)/shard_map/pallas_call | solution.py:451
  22.3 0.8 %collective-permute-start.9 = (bf16[8,8,512]{2,1,0:T(8,128)(2,1)S(1)}, bf16[8,8,512]{2,1,0:T(8,128)(2,1)S(1)}, u32[]{:S(2)}, u32[]{:S(2)}) collective-permute-start(bf16[8,8,512]{2,1,0:T(8,128)(2,1)S(1)} %get-tuple-element.66), channel_id=1, source_target_pairs={{0,16},{16,0},{1,17},{17,1},{2,18},{18,2},{3,19},{19,3},{4,20},{20... | collective-permute-start | bytes 196616 | tf_op jit(solution)/shard_map/ppermute | solution.py:470
  23.1 0.0 collective-permute-done.3.refs_3_
  23.1 0.0 collective-permute-done.2.refs_2_
  23.1 1.7 %shard_map.80 = (f32[2,4,128,128]{3,2,1,0:T(8,128)S(1)}, f32[1,128]{1,0:T(1,128)S(1)}, f32[8,8,512]{2,1,0:T(8,128)S(1)}, bf16[8,8,512]{2,1,0:T(8,128)(2,1)S(1)}) custom-call(f32[16,8,2,8,512]{4,3,2,1,0:T(8,128)S(1)} %get-tuple-element.51.refs_0_, f32[5,4,64,128]{3,2,1,0:T(8,128)S(1)} %get-tuple-element.57.refs_1_, ...), custom_call_target="tpu_custom_call" | custom-call | flops 8388608 | bytes 8388608 | tf_op jit(solution)/shard_map/pallas_call | solution.py:451
  24.8 1.4 %collective-permute-start.8 = (bf16[8,8,512]{2,1,0:T(8,128)(2,1)S(1)}, bf16[8,8,512]{2,1,0:T(8,128)(2,1)S(1)}, u32[]{:S(2)}, u32[]{:S(2)}) collective-permute-start(bf16[8,8,512]{2,1,0:T(8,128)(2,1)S(1)} %get-tuple-element.65), channel_id=1, source_target_pairs={{0,16},{16,0},{1,17},{17,1},{2,18},{18,2},{3,19},{19,3},{4,20},{20... | collective-permute-start | bytes 196616 | tf_op jit(solution)/shard_map/ppermute | solution.py:470
  26.1 0.0 collective-permute-done
  26.1 0.5 collective-permute-done.9
  26.6 2.5 %collective-permute-done.8 = bf16[8,8,512]{2,1,0:T(8,128)(2,1)S(1)} collective-permute-done((bf16[8,8,512]{2,1,0:T(8,128)(2,1)S(1)}, bf16[8,8,512]{2,1,0:T(8,128)(2,1)S(1)}, u32[]{:S(2)}, u32[]{:S(2)}) %collective-permute-start.8) | collective-permute-done | bytes 65568 | tf_op jit(solution)/shard_map/ppermute | solution.py:470
  29.1 0.1 shard_map.82
  29.2 9.7 %all_to_all.10.refs_5_ = f32[32,1,256]{2,1,0:T(1,128)S(1)} all-to-all(f32[32,1,256]{2,1,0:T(1,128)S(1)} %get-tuple-element.71), channel_id=1, replica_groups=mesh['mem'=2,'row'=16] {'mem','row'}, dimensions={0} | all-to-all | bytes 65536 | tf_op jit(solution)/shard_map/all_to_all | solution.py:564
  38.9 0.6 shard_map.83
  39.5 0.7 %collective-permute-start.13 = (bf16[8,8,512]{2,1,0:T(8,128)(2,1)S(1)}, bf16[8,8,512]{2,1,0:T(8,128)(2,1)S(1)}, u32[]{:S(2)}, u32[]{:S(2)}) collective-permute-start(bf16[8,8,512]{2,1,0:T(8,128)(2,1)S(1)} %get-tuple-element.74), channel_id=1, source_target_pairs={{1,2},{2,1},{3,4},{4,3},{5,6},{6,5},{7,8},{8,7},{9,10},{10,9},{11,... | collective-permute-start | bytes 196616 | tf_op jit(solution)/shard_map/ppermute | solution.py:481
  40.1 1.4 %collective-permute-start.15 = (bf16[16,8,512]{2,1,0:T(8,128)(2,1)S(1)}, bf16[16,8,512]{2,1,0:T(8,128)(2,1)S(1)}, u32[]{:S(2)}, u32[]{:S(2)}) collective-permute-start(bf16[16,8,512]{2,1,0:T(8,128)(2,1)S(1)} %get-tuple-element.80), channel_id=1, source_target_pairs={{1,2},{2,1},{3,4},{4,3},{5,6},{6,5},{7,8},{8,7},{9,10},{10,9},{11,... | collective-permute-start | bytes 393224 | tf_op jit(solution)/shard_map/ppermute | solution.py:481
  41.5 0.0 collective-permute-start.14
  41.5 0.6 collective-permute-start.11
  42.2 0.7 %collective-permute-start.10 = (bf16[16,8,512]{2,1,0:T(8,128)(2,1)S(1)}, bf16[16,8,512]{2,1,0:T(8,128)(2,1)S(1)}, u32[]{:S(2)}, u32[]{:S(2)}) collective-permute-start(bf16[16,8,512]{2,1,0:T(8,128)(2,1)S(1)} %get-tuple-element.73), channel_id=1, source_target_pairs={{0,1},{1,0},{2,3},{3,2},{4,5},{5,4},{6,7},{7,6},{8,9},{9,8},{10,11... | collective-permute-start | bytes 393224 | tf_op jit(solution)/shard_map/ppermute | solution.py:473
  42.9 0.9 %collective-permute-done.13.refs_3_ = bf16[8,8,512]{2,1,0:T(8,128)(2,1)S(1)} collective-permute-done((bf16[8,8,512]{2,1,0:T(8,128)(2,1)S(1)}, bf16[8,8,512]{2,1,0:T(8,128)(2,1)S(1)}, u32[]{:S(2)}, u32[]{:S(2)}) %collective-permute-start.13) | collective-permute-done | bytes 65568 | tf_op jit(solution)/shard_map/ppermute | solution.py:481
  43.8 0.0 collective-permute-start.12
  43.8 1.3 %collective-permute-done.12.refs_2_ = bf16[8,8,512]{2,1,0:T(8,128)(2,1)S(1)} collective-permute-done((bf16[8,8,512]{2,1,0:T(8,128)(2,1)S(1)}, bf16[8,8,512]{2,1,0:T(8,128)(2,1)S(1)}, u32[]{:S(2)}, u32[]{:S(2)}) %collective-permute-start.12) | collective-permute-done | bytes 65568 | tf_op jit(solution)/shard_map/ppermute | solution.py:473
  45.0 0.8 %shard_map.84 = (f32[1,4,128,128]{3,2,1,0:T(8,128)S(1)}, f32[1,128]{1,0:T(1,128)S(1)}, f32[2,4,8,512]{3,2,1,0:T(8,128)S(1)}) custom-call(f32[4,2,8,512]{3,2,1,0:T(8,128)S(1)} %get-tuple-element.52.refs_1_.refs_0_, f32[5,4,64,128]{3,2,1,0:T(8,128)S(1)} %get-tuple-element.72.refs_1_, bf16[8,8,512]{2,1,0:T(8,128)(2,1)S(1)} %collective-permute-done.12.refs_2_, ...), custom_call_target="tpu_custom_call" | custom-call | flops 8388608 | bytes 8388608 | tf_op jit(solution)/shard_map/pallas_call | solution.py:451
  45.8 0.0 collective-permute-done.15.refs_3_
  45.8 1.7 %shard_map.86 = (f32[2,4,128,128]{3,2,1,0:T(8,128)S(1)}, f32[1,128]{1,0:T(1,128)S(1)}, f32[8,8,512]{2,1,0:T(8,128)S(1)}, bf16[1,4,8,512]{3,2,1,0:T(8,128)(2,1)S(1)}) custom-call(f32[16,8,2,8,512]{4,3,2,1,0:T(8,128)S(1)} %get-tuple-element.51.refs_0_, f32[5,4,64,128]{3,2,1,0:T(8,128)S(1)} %get-tuple-element.72.refs_1_, ...), custom_call_target="tpu_custom_call" | custom-call | flops 8388608 | bytes 8388608 | tf_op jit(solution)/shard_map/pallas_call | solution.py:451
  47.6 0.7 %collective-permute-start.17 = (bf16[4,8,512]{2,1,0:T(8,128)(2,1)S(1)}, bf16[4,8,512]{2,1,0:T(8,128)(2,1)S(1)}, u32[]{:S(2)}, u32[]{:S(2)}) collective-permute-start(bf16[4,8,512]{2,1,0:T(8,128)(2,1)S(1)} %bitcast.15), channel_id=1, source_target_pairs={{0,16},{16,0},{1,17},{17,1},{2,18},{18,2},{3,19},{19,3},{4,20},{20... | collective-permute-start | bytes 98312 | tf_op jit(solution)/shard_map/ppermute | solution.py:470
  48.3 0.0 collective-permute-done.11.refs_3_
  48.3 0.0 collective-permute-done.10.refs_2_
  48.3 1.7 %shard_map.85 = (f32[2,4,128,128]{3,2,1,0:T(8,128)S(1)}, f32[1,128]{1,0:T(1,128)S(1)}, f32[8,8,512]{2,1,0:T(8,128)S(1)}, bf16[1,4,8,512]{3,2,1,0:T(8,128)(2,1)S(1)}) custom-call(f32[16,8,2,8,512]{4,3,2,1,0:T(8,128)S(1)} %get-tuple-element.51.refs_0_, f32[5,4,64,128]{3,2,1,0:T(8,128)S(1)} %get-tuple-element.72.refs_1_, ...), custom_call_target="tpu_custom_call" | custom-call | flops 8388608 | bytes 8388608 | tf_op jit(solution)/shard_map/pallas_call | solution.py:451
  50.0 1.4 %collective-permute-start.16 = (bf16[4,8,512]{2,1,0:T(8,128)(2,1)S(1)}, bf16[4,8,512]{2,1,0:T(8,128)(2,1)S(1)}, u32[]{:S(2)}, u32[]{:S(2)}) collective-permute-start(bf16[4,8,512]{2,1,0:T(8,128)(2,1)S(1)} %bitcast.16), channel_id=1, source_target_pairs={{0,16},{16,0},{1,17},{17,1},{2,18},{18,2},{3,19},{19,3},{4,20},{20... | collective-permute-start | bytes 98312 | tf_op jit(solution)/shard_map/ppermute | solution.py:470
  51.4 0.4 collective-permute-done.17
  51.8 2.2 %collective-permute-done.16 = bf16[4,8,512]{2,1,0:T(8,128)(2,1)S(1)} collective-permute-done((bf16[4,8,512]{2,1,0:T(8,128)(2,1)S(1)}, bf16[4,8,512]{2,1,0:T(8,128)(2,1)S(1)}, u32[]{:S(2)}, u32[]{:S(2)}) %collective-permute-start.16) | collective-permute-done | bytes 32800 | tf_op jit(solution)/shard_map/ppermute | solution.py:470
  54.0 0.1 shard_map.87
  54.2 11.5 %all_to_all.11.got = f32[32,1,256]{2,1,0:T(1,128)S(1)} all-to-all(f32[32,1,256]{2,1,0:T(1,128)S(1)} %get-tuple-element.88), channel_id=1, replica_groups=mesh['mem'=2,'row'=16] {'mem','row'}, dimensions={0} | all-to-all | bytes 65536 | tf_op jit(solution)/shard_map/all_to_all | solution.py:564
  65.7 1.8 %shard_map.88 = (f32[16,2,8,512]{3,2,1,0:T(8,128)}, f32[4,2,8,512]{3,2,1,0:T(8,128)}, f32[4,2,8,512]{3,2,1,0:T(8,128)}) custom-call(f32[32,1,256]{2,1,0:T(1,128)S(1)} %all_to_all.11.got, f32[1,128]{1,0:T(1,128)S(1)} %get-tuple-element.76.refs_6_.refs_7_.refs_9_.step, f32[8,2,8,512]{3,2,1,0:T(8,128)S(1)} %get-tuple-element.70.refs_4_.refs_8_.image0, ...), custom_call_target="tpu_custom_call" | custom-call | tf_op jit(solution)/shard_map/pallas_call | solution.py:451
  (3 shorter events, 0.0 us)
Async XLA Ops:
  1.7 6.6 %collective-permute-start.1 = (bf16[4,2,8,512]{3,2,1,0:T(8,128)(2,1)S(1)}, bf16[4,2,8,512]{3,2,1,0:T(8,128)(2,1)S(1)}, u32[]{:S(2)}, u32[]{:S(2)}) collective-permute-start(bf16[4,2,8,512]{3,2,1,0:T(8,128)(2,1)S(1)} %get-tuple-element.50.own), channel_id=1, source_target_pairs={{0,16},{16,0},{1,17},{17,1},{2,18},{18,2},{3,19},{19,3},{4,20},{20... | collective-permute-start | bytes 196616 | tf_op jit(solution)/shard_map/ppermute | solution.py:470
  9.1 4.7 %collective-permute-start.5 = (bf16[10,8,512]{2,1,0:T(8,128)(2,1)S(1)}, bf16[10,8,512]{2,1,0:T(8,128)(2,1)S(1)}, u32[]{:S(2)}, u32[]{:S(2)}) collective-permute-start(bf16[10,8,512]{2,1,0:T(8,128)(2,1)S(1)} %get-tuple-element.59), channel_id=1, source_target_pairs={{1,2},{2,1},{3,4},{4,3},{5,6},{6,5},{7,8},{8,7},{9,10},{10,9},{11,... | collective-permute-start | bytes 245768 | tf_op jit(solution)/shard_map/ppermute | solution.py:481
  9.9 4.6 %collective-permute-start.4 = (bf16[10,8,512]{2,1,0:T(8,128)(2,1)S(1)}, bf16[10,8,512]{2,1,0:T(8,128)(2,1)S(1)}, u32[]{:S(2)}, u32[]{:S(2)}) collective-permute-start(bf16[10,8,512]{2,1,0:T(8,128)(2,1)S(1)} %get-tuple-element.59), channel_id=1, source_target_pairs={{0,1},{1,0},{2,3},{3,2},{4,5},{5,4},{6,7},{7,6},{8,9},{9,8},{10,11... | collective-permute-start | bytes 245768 | tf_op jit(solution)/shard_map/ppermute | solution.py:473
  10.8 15.4 %collective-permute-start = (f32[2,4,2,8,512]{4,3,2,1,0:T(8,128)S(1)}, f32[2,4,2,8,512]{4,3,2,1,0:T(8,128)S(1)}, u32[]{:S(2)}, u32[]{:S(2)}) collective-permute-start(f32[2,4,2,8,512]{4,3,2,1,0:T(8,128)S(1)} %get-tuple-element.53.refs_7_.refs_2_), channel_id=1, source_target_pairs={{0,16},{16,0},{1,17},{17,1},{2,18},{18,2},{3,19},{19,3},{4,20},{20... | collective-permute-start | bytes 786440 | tf_op jit(solution)/shard_map/ppermute | solution.py:470
  11.5 9.2 %collective-permute-start.7 = (bf16[16,8,512]{2,1,0:T(8,128)(2,1)S(1)}, bf16[16,8,512]{2,1,0:T(8,128)(2,1)S(1)}, u32[]{:S(2)}, u32[]{:S(2)}) collective-permute-start(bf16[16,8,512]{2,1,0:T(8,128)(2,1)S(1)} %get-tuple-element.63), channel_id=1, source_target_pairs={{1,2},{2,1},{3,4},{4,3},{5,6},{6,5},{7,8},{8,7},{9,10},{10,9},{11,... | collective-permute-start | bytes 393224 | tf_op jit(solution)/shard_map/ppermute | solution.py:481
  12.8 7.8 %collective-permute-start.6 = (bf16[16,8,512]{2,1,0:T(8,128)(2,1)S(1)}, bf16[16,8,512]{2,1,0:T(8,128)(2,1)S(1)}, u32[]{:S(2)}, u32[]{:S(2)}) collective-permute-start(bf16[16,8,512]{2,1,0:T(8,128)(2,1)S(1)} %get-tuple-element.63), channel_id=1, source_target_pairs={{0,1},{1,0},{2,3},{3,2},{4,5},{5,4},{6,7},{7,6},{8,9},{9,8},{10,11... | collective-permute-start | bytes 393224 | tf_op jit(solution)/shard_map/ppermute | solution.py:473
  13.8 9.3 %collective-permute-start.3 = (bf16[16,8,512]{2,1,0:T(8,128)(2,1)S(1)}, bf16[16,8,512]{2,1,0:T(8,128)(2,1)S(1)}, u32[]{:S(2)}, u32[]{:S(2)}) collective-permute-start(bf16[16,8,512]{2,1,0:T(8,128)(2,1)S(1)} %get-tuple-element.58), channel_id=1, source_target_pairs={{1,2},{2,1},{3,4},{4,3},{5,6},{6,5},{7,8},{8,7},{9,10},{10,9},{11,... | collective-permute-start | bytes 393224 | tf_op jit(solution)/shard_map/ppermute | solution.py:481
  14.5 8.6 %collective-permute-start.2 = (bf16[16,8,512]{2,1,0:T(8,128)(2,1)S(1)}, bf16[16,8,512]{2,1,0:T(8,128)(2,1)S(1)}, u32[]{:S(2)}, u32[]{:S(2)}) collective-permute-start(bf16[16,8,512]{2,1,0:T(8,128)(2,1)S(1)} %get-tuple-element.58), channel_id=1, source_target_pairs={{0,1},{1,0},{2,3},{3,2},{4,5},{5,4},{6,7},{7,6},{8,9},{9,8},{10,11... | collective-permute-start | bytes 393224 | tf_op jit(solution)/shard_map/ppermute | solution.py:473
  22.3 4.3 %collective-permute-start.9 = (bf16[8,8,512]{2,1,0:T(8,128)(2,1)S(1)}, bf16[8,8,512]{2,1,0:T(8,128)(2,1)S(1)}, u32[]{:S(2)}, u32[]{:S(2)}) collective-permute-start(bf16[8,8,512]{2,1,0:T(8,128)(2,1)S(1)} %get-tuple-element.66), channel_id=1, source_target_pairs={{0,16},{16,0},{1,17},{17,1},{2,18},{18,2},{3,19},{19,3},{4,20},{20... | collective-permute-start | bytes 196616 | tf_op jit(solution)/shard_map/ppermute | solution.py:470
  24.8 4.3 %collective-permute-start.8 = (bf16[8,8,512]{2,1,0:T(8,128)(2,1)S(1)}, bf16[8,8,512]{2,1,0:T(8,128)(2,1)S(1)}, u32[]{:S(2)}, u32[]{:S(2)}) collective-permute-start(bf16[8,8,512]{2,1,0:T(8,128)(2,1)S(1)} %get-tuple-element.65), channel_id=1, source_target_pairs={{0,16},{16,0},{1,17},{17,1},{2,18},{18,2},{3,19},{19,3},{4,20},{20... | collective-permute-start | bytes 196616 | tf_op jit(solution)/shard_map/ppermute | solution.py:470
  39.5 4.3 %collective-permute-start.13 = (bf16[8,8,512]{2,1,0:T(8,128)(2,1)S(1)}, bf16[8,8,512]{2,1,0:T(8,128)(2,1)S(1)}, u32[]{:S(2)}, u32[]{:S(2)}) collective-permute-start(bf16[8,8,512]{2,1,0:T(8,128)(2,1)S(1)} %get-tuple-element.74), channel_id=1, source_target_pairs={{1,2},{2,1},{3,4},{4,3},{5,6},{6,5},{7,8},{8,7},{9,10},{10,9},{11,... | collective-permute-start | bytes 196616 | tf_op jit(solution)/shard_map/ppermute | solution.py:481
  40.1 5.7 %collective-permute-start.15 = (bf16[16,8,512]{2,1,0:T(8,128)(2,1)S(1)}, bf16[16,8,512]{2,1,0:T(8,128)(2,1)S(1)}, u32[]{:S(2)}, u32[]{:S(2)}) collective-permute-start(bf16[16,8,512]{2,1,0:T(8,128)(2,1)S(1)} %get-tuple-element.80), channel_id=1, source_target_pairs={{1,2},{2,1},{3,4},{4,3},{5,6},{6,5},{7,8},{8,7},{9,10},{10,9},{11,... | collective-permute-start | bytes 393224 | tf_op jit(solution)/shard_map/ppermute | solution.py:481
  41.5 4.3 %collective-permute-start.14 = (bf16[16,8,512]{2,1,0:T(8,128)(2,1)S(1)}, bf16[16,8,512]{2,1,0:T(8,128)(2,1)S(1)}, u32[]{:S(2)}, u32[]{:S(2)}) collective-permute-start(bf16[16,8,512]{2,1,0:T(8,128)(2,1)S(1)} %get-tuple-element.80), channel_id=1, source_target_pairs={{0,1},{1,0},{2,3},{3,2},{4,5},{5,4},{6,7},{7,6},{8,9},{9,8},{10,11... | collective-permute-start | bytes 393224 | tf_op jit(solution)/shard_map/ppermute | solution.py:473
  41.5 6.7 %collective-permute-start.11 = (bf16[16,8,512]{2,1,0:T(8,128)(2,1)S(1)}, bf16[16,8,512]{2,1,0:T(8,128)(2,1)S(1)}, u32[]{:S(2)}, u32[]{:S(2)}) collective-permute-start(bf16[16,8,512]{2,1,0:T(8,128)(2,1)S(1)} %get-tuple-element.73), channel_id=1, source_target_pairs={{1,2},{2,1},{3,4},{4,3},{5,6},{6,5},{7,8},{8,7},{9,10},{10,9},{11,... | collective-permute-start | bytes 393224 | tf_op jit(solution)/shard_map/ppermute | solution.py:481
  42.2 6.1 %collective-permute-start.10 = (bf16[16,8,512]{2,1,0:T(8,128)(2,1)S(1)}, bf16[16,8,512]{2,1,0:T(8,128)(2,1)S(1)}, u32[]{:S(2)}, u32[]{:S(2)}) collective-permute-start(bf16[16,8,512]{2,1,0:T(8,128)(2,1)S(1)} %get-tuple-element.73), channel_id=1, source_target_pairs={{0,1},{1,0},{2,3},{3,2},{4,5},{5,4},{6,7},{7,6},{8,9},{9,8},{10,11... | collective-permute-start | bytes 393224 | tf_op jit(solution)/shard_map/ppermute | solution.py:473
  43.8 1.3 %collective-permute-start.12 = (bf16[8,8,512]{2,1,0:T(8,128)(2,1)S(1)}, bf16[8,8,512]{2,1,0:T(8,128)(2,1)S(1)}, u32[]{:S(2)}, u32[]{:S(2)}) collective-permute-start(bf16[8,8,512]{2,1,0:T(8,128)(2,1)S(1)} %get-tuple-element.74), channel_id=1, source_target_pairs={{0,1},{1,0},{2,3},{3,2},{4,5},{5,4},{6,7},{7,6},{8,9},{9,8},{10,11... | collective-permute-start | bytes 196616 | tf_op jit(solution)/shard_map/ppermute | solution.py:473
  47.6 4.3 %collective-permute-start.17 = (bf16[4,8,512]{2,1,0:T(8,128)(2,1)S(1)}, bf16[4,8,512]{2,1,0:T(8,128)(2,1)S(1)}, u32[]{:S(2)}, u32[]{:S(2)}) collective-permute-start(bf16[4,8,512]{2,1,0:T(8,128)(2,1)S(1)} %bitcast.15), channel_id=1, source_target_pairs={{0,16},{16,0},{1,17},{17,1},{2,18},{18,2},{3,19},{19,3},{4,20},{20... | collective-permute-start | bytes 98312 | tf_op jit(solution)/shard_map/ppermute | solution.py:470
  50.0 4.0 %collective-permute-start.16 = (bf16[4,8,512]{2,1,0:T(8,128)(2,1)S(1)}, bf16[4,8,512]{2,1,0:T(8,128)(2,1)S(1)}, u32[]{:S(2)}, u32[]{:S(2)}) collective-permute-start(bf16[4,8,512]{2,1,0:T(8,128)(2,1)S(1)} %bitcast.16), channel_id=1, source_target_pairs={{0,16},{16,0},{1,17},{17,1},{2,18},{18,2},{3,19},{19,3},{4,20},{20... | collective-permute-start | bytes 98312 | tf_op jit(solution)/shard_map/ppermute | solution.py:470
